TPU v7x, 32 devices: a whole 2x2x4 slice. The times are simulated.
32 devices in a mesh: dp: 8 (over y, x, core), tensor: 4 (over z).
Axes of the slice: x: 2, y: 2, z: 4, core: 2. Of those that a mesh axis runs over, the one named last changes fastest.
Arguments:
- tokens: bfloat16 [12288, 2048], P(('dp', 'tensor')), may hold values from -6 to 6
- norm_attn: bfloat16 [2048], P('dp'), may hold values from 0.099609375 to 1.8984375
- w_query: bfloat16 [2048, 2048], P('dp', 'tensor'), may hold values from -0.125 to 0.125
- w_key: bfloat16 [2048, 128], P('dp'), may hold values from -0.125 to 0.125
- w_value: bfloat16 [2048, 128], P('dp'), may hold values from -0.125 to 0.125
- w_out: bfloat16 [2048, 2048], P('tensor', 'dp'), may hold values from -0.75 to 0.75
- norm_ffn: bfloat16 [2048], P('dp'), may hold values from 0.099609375 to 1.8984375
- w_gate: bfloat16 [2048, 5632], P('dp', 'tensor'), may hold values from -0.125 to 0.125
- w_up: bfloat16 [2048, 5632], P('dp', 'tensor'), may hold values from -0.125 to 0.125
- w_down: bfloat16 [5632, 2048], P('tensor', 'dp'), may hold values from -0.078125 to 0.078125
- segment_ids: int32 [12288], P('dp'), may hold values from 0 to 103, as said below
- parents: int32 [104], replicated, may hold values from 0 to 95, as said below
- positions: int32 [12288], P('dp'), may hold values from 0 to 927, as said below
- d_out: bfloat16 [12288, 2048], P(('dp', 'tensor')), may hold values from -6 to 6
- d_keys: bfloat16 [12288, 128], P(('dp', 'tensor')), may hold values from -6 to 6
- d_values: bfloat16 [12288, 128], P(('dp', 'tensor')), may hold values from -6 to 6
Outputs:
- out: bfloat16 [12288, 2048], P(('dp', 'tensor'))
- keys: bfloat16 [12288, 128], P('dp')
- values: bfloat16 [12288, 128], P('dp')
- d_x: float32 [12288, 2048], P(('dp', 'tensor'))
- g_norm_attn: float32 [2048], P('dp')
- g_query: float32 [2048, 2048], P('dp', 'tensor')
- g_key: float32 [2048, 128], P('dp')
- g_value: float32 [2048, 128], P('dp')
- g_out: float32 [2048, 2048], P('tensor', 'dp')
- g_norm_ffn: float32 [2048], P('dp')
- g_gate: float32 [2048, 5632], P('dp', 'tensor')
- g_up: float32 [2048, 5632], P('dp', 'tensor')
- g_down: float32 [5632, 2048], P('tensor', 'dp')
Inputs may be any that keep to these rules, and one draw needn't show every extreme that they name: `segment_ids`: tree t holds tokens t * 1536 to (t + 1) * 1536 - 1 and segments 13 t to 13 t + 12 in this order: a trunk of 768 tokens, four branches of 64 tokens, eight leaves whose two of each branch have lengths summing to 128, each leaf 64 // 2 tokens or more; ids never fall. `parents`: A trunk is its own parent, a branch's parent is its tree's trunk, a leaf's parent is a branch of its tree, and each branch is the parent of exactly two leaves. `positions`: counts up by one within a segment from 0 at a trunk's first token, from 768 at a branch's first token and from 832 at a leaf's first token.
All inputs are finite; a program needn't handle non-finite values.
Results may differ from a plain program's by a relative error of at most 0.022.
Values may be sent and summed in bfloat16 or wider, within the bound.
No kernel may reach another device: no remote copies, remote signals or barrier semaphores. Data moves between devices by JAX's collectives and lax.ppermute only.
A program may use at most 256 MiB of HBM per device.

v0:
```python
import jax
import jax.numpy as jnp
from jax import lax
from jax.sharding import PartitionSpec as P

HD = 128
QBLOCK = 512


norm_eps = 1e-05


def lookup(ids, table):
    hits = ids[:, None] == jnp.arange(table.shape[0], dtype=jnp.int32)[None, :]
    return jnp.sum(jnp.where(hits, table[None, :], 0), axis=1)


def path_mask(segment_block, first_block, second_block, place_block, segment, place):
    linked = (
        (segment[None, :] == segment_block[:, None])
        | (segment[None, :] == first_block[:, None])
        | (segment[None, :] == second_block[:, None])
    )
    return linked & (place[None, :] <= place_block[:, None])


def norm_back(value, scale, gain, grad):
    weighted = grad * gain
    return scale * weighted - value * (scale * scale * scale) * jnp.mean(
        weighted * value, axis=-1, keepdims=True
    )


def contract_rows(left, right):
    return lax.dot_general(
        left, right, (((0,), (0,)), ((), ())), preferred_element_type=jnp.float32
    )


def contract_cols(left, right):
    return lax.dot_general(
        left, right, (((1,), (1,)), ((), ())), preferred_element_type=jnp.float32
    )


def on_device(
    tokens,
    norm_attn,
    w_query,
    w_key,
    w_value,
    w_out,
    norm_ffn,
    w_gate,
    w_up,
    w_down,
    segment_ids,
    parents,
    positions,
    d_out,
    d_keys,
    d_values,
):
    score_scale = HD ** (-0.5)
    attn_gain, query_w, key_w, value_w, out_w = (
        lax.all_gather(norm_attn, "dp", axis=0, tiled=True),
        lax.all_gather(w_query, "dp", axis=0, tiled=True),
        lax.all_gather(w_key, "dp", axis=0, tiled=True),
        lax.all_gather(w_value, "dp", axis=0, tiled=True),
        lax.all_gather(w_out, "dp", axis=1, tiled=True),
    )
    ffn_gain, gate_w, up_w, down_w = (
        lax.all_gather(norm_ffn, "dp", axis=0, tiled=True),
        lax.all_gather(w_gate, "dp", axis=0, tiled=True),
        lax.all_gather(w_up, "dp", axis=0, tiled=True),
        lax.all_gather(w_down, "dp", axis=1, tiled=True),
    )
    attn_gain = attn_gain.astype(jnp.float32)
    ffn_gain = ffn_gain.astype(jnp.float32)
    residual = tokens.astype(jnp.float32)
    attn_scale = lax.rsqrt(jnp.mean(residual * residual, axis=-1, keepdims=True) + norm_eps)
    normed_own = (residual * attn_scale * attn_gain).astype(jnp.bfloat16)
    normed = lax.all_gather(normed_own, "tensor", axis=0, tiled=True)
    query = jnp.dot(normed, query_w, preferred_element_type=jnp.float32).astype(jnp.bfloat16)
    keys = jnp.dot(normed, key_w, preferred_element_type=jnp.float32).astype(jnp.bfloat16)
    values = jnp.dot(normed, value_w, preferred_element_type=jnp.float32).astype(jnp.bfloat16)
    total = normed.shape[0]
    blocks = total // QBLOCK
    heads = query.shape[1] // HD
    first_up = lookup(segment_ids, parents)
    second_up = lookup(first_up, parents)
    query_blocks = query.reshape(blocks, QBLOCK, heads, HD)
    id_blocks = (
        segment_ids.reshape(blocks, QBLOCK),
        first_up.reshape(blocks, QBLOCK),
        second_up.reshape(blocks, QBLOCK),
        positions.reshape(blocks, QBLOCK),
    )

    def attend(operand):
        query_block, segment_block, first_block, second_block, place_block = operand
        mask = path_mask(
            segment_block, first_block, second_block, place_block, segment_ids, positions
        )
        scores = (
            jnp.einsum("qhd,kd->hqk", query_block, keys, preferred_element_type=jnp.float32)
            * score_scale
        )
        scores = jnp.where(mask[None], scores, -1e30)
        peak = jnp.max(scores, axis=-1, keepdims=True)
        raised = jnp.exp(scores - peak)
        sums = jnp.sum(raised, axis=-1, keepdims=True)
        shares = (raised / sums).astype(jnp.bfloat16)
        mixed_block = jnp.einsum(
            "hqk,kd->qhd", shares, values, preferred_element_type=jnp.float32
        ).astype(jnp.bfloat16)
        return (mixed_block.reshape(QBLOCK, heads * HD), (peak + jnp.log(sums))[..., 0])

    mixed, log_totals = lax.map(attend, (query_blocks,) + id_blocks)
    mixed = mixed.reshape(total, heads * HD)
    attn_part = lax.psum_scatter(
        jnp.dot(mixed, out_w, preferred_element_type=jnp.float32),
        "tensor",
        scatter_dimension=0,
        tiled=True,
    )
    after_attn = residual + attn_part
    ffn_scale = lax.rsqrt(jnp.mean(after_attn * after_attn, axis=-1, keepdims=True) + norm_eps)
    ffn_own = (after_attn * ffn_scale * ffn_gain).astype(jnp.bfloat16)
    ffn_normed = lax.all_gather(ffn_own, "tensor", axis=0, tiled=True)
    gate = jnp.dot(ffn_normed, gate_w, preferred_element_type=jnp.float32)
    upward = jnp.dot(ffn_normed, up_w, preferred_element_type=jnp.float32)
    sigma = jax.nn.sigmoid(gate)
    hidden = (gate * sigma * upward).astype(jnp.bfloat16)
    ffn_part = lax.psum_scatter(
        jnp.dot(hidden, down_w, preferred_element_type=jnp.float32).astype(jnp.bfloat16),
        "tensor",
        scatter_dimension=0,
        tiled=True,
    ).astype(jnp.float32)
    output = (after_attn + ffn_part).astype(jnp.bfloat16)
    grad_full = lax.all_gather(d_out, "tensor", axis=0, tiled=True)
    down_grad = contract_rows(hidden, grad_full)
    hidden_grad = contract_cols(grad_full, down_w)
    gate_grad = (hidden_grad * upward * sigma * (1.0 + gate * (1.0 - sigma))).astype(jnp.bfloat16)
    up_grad = (hidden_grad * gate * sigma).astype(jnp.bfloat16)
    gate_w_grad = contract_rows(ffn_normed, gate_grad)
    up_w_grad = contract_rows(ffn_normed, up_grad)
    ffn_normed_grad = lax.psum_scatter(
        contract_cols(gate_grad, gate_w) + contract_cols(up_grad, up_w),
        "tensor",
        scatter_dimension=0,
        tiled=True,
    )
    after_grad = d_out.astype(jnp.float32) + norm_back(
        after_attn, ffn_scale, ffn_gain, ffn_normed_grad
    )
    ffn_gain_term = jnp.sum(ffn_normed_grad * after_attn * ffn_scale, axis=0)
    branch_full = lax.all_gather(after_grad.astype(jnp.bfloat16), "tensor", axis=0, tiled=True)
    out_w_grad = contract_rows(mixed, branch_full)
    mixed_grad = contract_cols(branch_full, out_w).astype(jnp.bfloat16)
    mixed_grad_blocks = mixed_grad.reshape(blocks, QBLOCK, heads, HD)

    def attend_back(carry, operand):
        key_acc, value_acc = carry
        (
            query_block,
            grad_block,
            log_block,
            segment_block,
            first_block,
            second_block,
            place_block,
        ) = operand
        mask = path_mask(
            segment_block, first_block, second_block, place_block, segment_ids, positions
        )
        scores = (
            jnp.einsum("qhd,kd->hqk", query_block, keys, preferred_element_type=jnp.float32)
            * score_scale
        )
        scores = jnp.where(mask[None], scores, -1e30)
        shares = jnp.exp(scores - log_block[:, :, None])
        low_shares = shares.astype(jnp.bfloat16)
        share_grad = jnp.einsum(
            "qhd,kd->hqk", grad_block, values, preferred_element_type=jnp.float32
        )
        value_acc = value_acc + jnp.einsum(
            "hqk,qhd->kd", low_shares, grad_block, preferred_element_type=jnp.float32
        )
        inner = jnp.sum(shares * share_grad, axis=-1, keepdims=True)
        score_grad = (shares * (share_grad - inner)).astype(jnp.bfloat16)
        query_grad_block = (
            score_scale
            * jnp.einsum("hqk,kd->qhd", score_grad, keys, preferred_element_type=jnp.float32)
        ).astype(jnp.bfloat16)
        key_acc = key_acc + score_scale * jnp.einsum(
            "hqk,qhd->kd", score_grad, query_block, preferred_element_type=jnp.float32
        )
        return ((key_acc, value_acc), query_grad_block.reshape(QBLOCK, heads * HD))

    empty = jnp.zeros((total, HD), jnp.float32)
    (key_acc, value_acc), query_grad = lax.scan(
        attend_back, (empty, empty), (query_blocks, mixed_grad_blocks, log_totals) + id_blocks
    )
    query_grad = query_grad.reshape(total, heads * HD)
    query_w_grad = contract_rows(normed, query_grad)
    normed_part = contract_cols(query_grad, query_w)
    normed_sum, key_sum, value_sum = (
        lax.psum_scatter(
            normed_part.astype(jnp.bfloat16), "tensor", scatter_dimension=0, tiled=True
        ).astype(jnp.float32),
        lax.psum_scatter(
            key_acc.astype(jnp.bfloat16), "tensor", scatter_dimension=0, tiled=True
        ).astype(jnp.float32),
        lax.psum_scatter(
            value_acc.astype(jnp.bfloat16), "tensor", scatter_dimension=0, tiled=True
        ).astype(jnp.float32),
    )
    key_grad = (key_sum + d_keys.astype(jnp.float32)).astype(jnp.bfloat16)
    value_grad = (value_sum + d_values.astype(jnp.float32)).astype(jnp.bfloat16)
    normed_grad = normed_sum + contract_cols(key_grad, key_w) + contract_cols(value_grad, value_w)
    key_w_term = contract_rows(normed_own, key_grad)
    value_w_term = contract_rows(normed_own, value_grad)
    input_grad = after_grad + norm_back(residual, attn_scale, attn_gain, normed_grad)
    attn_gain_term = jnp.sum(normed_grad * residual * attn_scale, axis=0)
    key_w_grad, value_w_grad, attn_gain_grad, ffn_gain_grad = (
        lax.psum(key_w_term.astype(jnp.bfloat16), "tensor").astype(jnp.float32),
        lax.psum(value_w_term.astype(jnp.bfloat16), "tensor").astype(jnp.float32),
        lax.psum(attn_gain_term.astype(jnp.bfloat16), "tensor").astype(jnp.float32),
        lax.psum(ffn_gain_term.astype(jnp.bfloat16), "tensor").astype(jnp.float32),
    )
    (
        attn_gain_part,
        query_part,
        key_part,
        value_part,
        out_part,
        ffn_gain_part,
        gate_part,
        up_part,
        down_part,
    ) = (
        lax.psum_scatter(
            attn_gain_grad.astype(jnp.bfloat16), "dp", scatter_dimension=0, tiled=True
        ).astype(jnp.float32),
        lax.psum_scatter(
            query_w_grad.astype(jnp.bfloat16), "dp", scatter_dimension=0, tiled=True
        ).astype(jnp.float32),
        lax.psum_scatter(
            key_w_grad.astype(jnp.bfloat16), "dp", scatter_dimension=0, tiled=True
        ).astype(jnp.float32),
        lax.psum_scatter(
            value_w_grad.astype(jnp.bfloat16), "dp", scatter_dimension=0, tiled=True
        ).astype(jnp.float32),
        lax.psum_scatter(
            out_w_grad.astype(jnp.bfloat16), "dp", scatter_dimension=1, tiled=True
        ).astype(jnp.float32),
        lax.psum_scatter(
            ffn_gain_grad.astype(jnp.bfloat16), "dp", scatter_dimension=0, tiled=True
        ).astype(jnp.float32),
        lax.psum_scatter(
            gate_w_grad.astype(jnp.bfloat16), "dp", scatter_dimension=0, tiled=True
        ).astype(jnp.float32),
        lax.psum_scatter(
            up_w_grad.astype(jnp.bfloat16), "dp", scatter_dimension=0, tiled=True
        ).astype(jnp.float32),
        lax.psum_scatter(
            down_grad.astype(jnp.bfloat16), "dp", scatter_dimension=1, tiled=True
        ).astype(jnp.float32),
    )
    return (
        output,
        keys,
        values,
        input_grad,
        attn_gain_part,
        query_part,
        key_part,
        value_part,
        out_part,
        ffn_gain_part,
        gate_part,
        up_part,
        down_part,
    )


def solution(mesh):
    in_specs = (
        P(("dp", "tensor"), None),
        P("dp"),
        P("dp", "tensor"),
        P("dp", None),
        P("dp", None),
        P("tensor", "dp"),
        P("dp"),
        P("dp", "tensor"),
        P("dp", "tensor"),
        P("tensor", "dp"),
        P("dp"),
        P(),
        P("dp"),
        P(("dp", "tensor"), None),
        P(("dp", "tensor"), None),
        P(("dp", "tensor"), None),
    )
    out_specs = (
        P(("dp", "tensor"), None),
        P("dp", None),
        P("dp", None),
        P(("dp", "tensor"), None),
        P("dp"),
        P("dp", "tensor"),
        P("dp", None),
        P("dp", None),
        P("tensor", "dp"),
        P("dp"),
        P("dp", "tensor"),
        P("dp", "tensor"),
        P("tensor", "dp"),
    )
    return jax.shard_map(
        on_device, mesh=mesh, in_specs=in_specs, out_specs=out_specs, check_vma=False
    )
```

profile of v0, /device:TPU:0, one launch (start us, length us, event | category | flops | bytes accessed | tf_op | source)
XLA Modules:
  0.0 1988.3 jit_solution(13247573112457298185)
XLA Ops:
  10.4 10.3 all-gather
  26.3 9.8 all_gather.42
  36.1 8.9 all_gather.43
  45.0 95.1 %all-gather.12.cloned.1.call-done = bf16[1536,2048]{1,0:T(8,128)(2,1)} async-done(((bf16[384,2048]{1,0:T(8,128)(2,1)}), bf16[1536,2048]{1,0:T(8,128)(2,1)}) %all-gather.12.cloned.1.call-update) | async-done | bytes 6291472 | tf_op jit(solution)/shard_map/all_gather | solution.py:83
  144.9 23.2 %all-gather.14.cloned.1.call-done = bf16[2048,512]{1,0:T(8,128)(2,1)} async-done(((bf16[256,512]{1,0:T(8,128)(2,1)}), bf16[2048,512]{1,0:T(8,128)(2,1)}) %all-gather.14.cloned.1.call-update) | async-done | bytes 2097168 | tf_op jit(solution)/shard_map/all_gather | solution.py:67
  168.2 8.0 convolution_convert_fusion.8
  185.0 40.4 %while.27 = (s32[]{:T(128)}, bf16[3,512,512]{2,1,0:T(8,128)(2,1)S(1)}, f32[3,4,512]{2,1,0:T(4,128)S(1)}, s32[1536]{0:T(1024)S(1)}, s32[3,512]{1,0:T(4,128)S(1)},...) while((s32[]{:T(128)}, ...), condition=%wide.region_6.7_spmd, body=%wide.region_3.6_spmd.sunk | while | flops 1654126592 | bytes 44929176 | solution.py:119
  225.4 8.6 fusion.48
  234.7 8.8 all-gather.1
  243.6 202.5 %reduce-scatter.14.cloned.1.call-done = f32[384,2048]{1,0:T(8,128)} async-done(((f32[1536,2048]{1,0:T(8,128)}), f32[384,2048]{1,0:T(8,128)}) %reduce-scatter.14.cloned.1.call-update) | async-done | bytes 3145744 | tf_op jit(solution)/shard_map/reduce_scatter | solution.py:121
  452.7 39.5 %all-gather.22.cloned.1.call-done = bf16[2048,1408]{1,0:T(8,128)(2,1)} async-done(((bf16[256,1408]{1,0:T(8,128)(2,1)}), bf16[2048,1408]{1,0:T(8,128)(2,1)}) %all-gather.22.cloned.1.call-update) | async-done | bytes 5767184 | tf_op jit(solution)/shard_map/all_gather | solution.py:75
  492.2 117.4 %all-gather.18.cloned.1.call-done = bf16[1536,2048]{1,0:T(8,128)(2,1)} async-done(((bf16[384,2048]{1,0:T(8,128)(2,1)}), bf16[1536,2048]{1,0:T(8,128)(2,1)}) %all-gather.18.cloned.1.call-update) | async-done | bytes 6291472 | tf_op jit(solution)/shard_map/all_gather | solution.py:130
  609.6 15.5 fusion.50
  625.0 28.0 %all-gather.20.cloned.1.call-done = bf16[2048,1408]{1,0:T(8,128)(2,1)} async-done(((bf16[256,1408]{1,0:T(8,128)(2,1)}), bf16[2048,1408]{1,0:T(8,128)(2,1)}) %all-gather.20.cloned.1.call-update) | async-done | bytes 5767184 | tf_op jit(solution)/shard_map/all_gather | solution.py:74
  653.0 15.1 fusion.49
  668.2 101.8 %all-gather.26.cloned.1.call-done = bf16[1536,2048]{1,0:T(8,128)(2,1)} async-done(((bf16[384,2048]{1,0:T(8,128)(2,1)}), bf16[1536,2048]{1,0:T(8,128)(2,1)}) %all-gather.26.cloned.1.call-update) | async-done | bytes 6291472 | tf_op jit(solution)/shard_map/all_gather | solution.py:142
  770.0 44.5 %all-gather.24.cloned.1.call-done = bf16[1408,2048]{1,0:T(8,128)(2,1)} async-done(((bf16[1408,256]{1,0:T(8,128)(2,1)}), bf16[1408,2048]{1,0:T(8,128)(2,1)}) %all-gather.24.cloned.1.call-update) | async-done | bytes 5767184 | tf_op jit(solution)/shard_map/all_gather | solution.py:76
  814.5 22.9 %multiply_convert_fusion = (bf16[1536,1408]{1,0:T(8,128)(2,1)}, bf16[1536,1408]{1,0:T(8,128)(2,1)}, bf16[1536,1408]{1,0:T(8,128)(2,1)}) fusion(f32[1536,1408]{1,0:T(8,128)} %fusion.49, f32[1536,1408]{1,0:T(8,128)} %fusion.50, bf16[1536,2048]{1,0:T(8,128)(2,1)} %all-gather.26.cloned.1.call-done, bf16[1408,2048]{1,0:T(8,128)(2,1)} %all-gather.24.cloned.1.call-done), kind=kOutput, calls=%fused_computation.58 | convolution fusion | flops 8892973056 | bytes 42336256 | tf_op jit(solution)/shard_map/dot_general | solution.py:41
  837.4 16.4 fusion.51
  853.8 16.4 convolution_add_fusion
  870.3 15.0 convolution_convert_fusion.4
  885.4 196.9 %reduce-scatter.18.cloned.1.call-done = f32[384,2048]{1,0:T(8,128)} async-done(((f32[1536,2048]{1,0:T(8,128)}), f32[384,2048]{1,0:T(8,128)}) %reduce-scatter.18.cloned.1.call-update) | async-done | bytes 3145744 | tf_op jit(solution)/shard_map/reduce_scatter | solution.py:149
  1085.5 110.9 %reduce-scatter.16.cloned.1.call-done = bf16[384,2048]{1,0:T(8,128)(2,1)} async-done(((bf16[1536,2048]{1,0:T(8,128)(2,1)}), bf16[384,2048]{1,0:T(8,128)(2,1)}) %reduce-scatter.16.cloned.1.call-update) | async-done | bytes 1572880 | tf_op jit(solution)/shard_map/reduce_scatter | solution.py:135
  1196.4 6.7 fusion.47
  1205.1 114.0 %all-gather.28.cloned.1.call-done = bf16[1536,2048]{1,0:T(8,128)(2,1)} async-done(((bf16[384,2048]{1,0:T(8,128)(2,1)}), bf16[1536,2048]{1,0:T(8,128)(2,1)}) %all-gather.28.cloned.1.call-update) | async-done | bytes 6291472 | tf_op jit(solution)/shard_map/all_gather | solution.py:159
  1319.1 6.9 convolution_convert_fusion.7
  1329.5 71.5 %while.28 = (s32[]{:T(128)}, f32[1536,128]{1,0:T(8,128)}, f32[1536,128]{1,0:T(8,128)S(1)}, bf16[3,512,512]{2,1,0:T(8,128)(2,1)}, s32[1536]{0:T(1024)S(1)}, /*ind...) while((s32[]{:T(128)}, f32[1536,128]{1,0:T(8,128)}, ...), condition=%wide.region_14.15_spmd.clone, body=%wide.region_12.14_spmd.clone.sunk | while | flops 4061853696 | bytes 139145552 | solution.py:203
  1334.9 5.6 fusion.117
  1358.7 5.6 fusion.117
  1382.6 5.6 fusion.117
  1404.2 17.9 reduce-scatter.22.cloned.1.call-done
  1425.0 18.7 reduce-scatter.24.cloned.1.call-done
  1446.2 14.3 convolution_convert_fusion
  1460.5 15.0 convolution_convert_fusion.1
  1475.8 15.0 convolution_convert_fusion.2
  1490.9 26.8 %reduce-scatter.38.cloned.1.call-done = bf16[256,128]{1,0:T(8,128)(2,1)} async-done(((bf16[2048,128]{1,0:T(8,128)(2,1)}), bf16[256,128]{1,0:T(8,128)(2,1)}) %reduce-scatter.38.cloned.1.call-update) | async-done | bytes 65552 | tf_op jit(solution)/shard_map/reduce_scatter | solution.py:253
  1517.8 7.8 convolution_convert_fusion.6
  1525.6 7.9 convolution_convert_fusion.5
  1533.9 7.2 convolution_convert_fusion.3
  1542.9 37.1 %reduce-scatter.34.cloned.1.call-done = bf16[1408,256]{1,0:T(8,128)(2,1)} async-done(((bf16[1408,2048]{1,0:T(8,128)(2,1)}), bf16[1408,256]{1,0:T(8,128)(2,1)}) %reduce-scatter.34.cloned.1.call-update) | async-done | bytes 720912 | tf_op jit(solution)/shard_map/reduce_scatter | solution.py:268
  1582.4 60.4 %reduce-scatter.32.cloned.1.call-done = bf16[256,1408]{1,0:T(8,128)(2,1)} async-done(((bf16[2048,1408]{1,0:T(8,128)(2,1)}), bf16[256,1408]{1,0:T(8,128)(2,1)}) %reduce-scatter.32.cloned.1.call-update) | async-done | bytes 720912 | tf_op jit(solution)/shard_map/reduce_scatter | solution.py:265
  1645.1 60.2 %reduce-scatter.30.cloned.1.call-done = bf16[256,1408]{1,0:T(8,128)(2,1)} async-done(((bf16[2048,1408]{1,0:T(8,128)(2,1)}), bf16[256,1408]{1,0:T(8,128)(2,1)}) %reduce-scatter.30.cloned.1.call-update) | async-done | bytes 720912 | tf_op jit(solution)/shard_map/reduce_scatter | solution.py:262
  1709.9 32.3 %all-reduce.7.cloned.1.call-done = (bf16[256,128]{1,0:T(8,128)(2,1)}, bf16[256,128]{1,0:T(8,128)(2,1)}) async-done(((bf16[256,128]{1,0:T(8,128)(2,1)}, bf16[256,128]{1,0:T(8,128)(2,1)}), (bf16[256,128]{1,0:T(8,128)(2,1)}, bf16[256,128]{1,0:T(8,128)(2,1)})) %all-reduce.7.cloned.1.call-update) | async-done | bytes 131088 | tf_op jit(solution)/shard_map/psum | solution.py:228
  1745.3 41.2 %reduce-scatter.26.cloned.1.call-done = bf16[256,512]{1,0:T(8,128)(2,1)} async-done(((bf16[2048,512]{1,0:T(8,128)(2,1)}), bf16[256,512]{1,0:T(8,128)(2,1)}) %reduce-scatter.26.cloned.1.call-update) | async-done | bytes 262160 | tf_op jit(solution)/shard_map/reduce_scatter | solution.py:247
  1788.3 43.1 %reduce-scatter.28.cloned.1.call-done = bf16[512,256]{1,0:T(8,128)(2,1)} async-done(((bf16[512,2048]{1,0:T(8,128)(2,1)}), bf16[512,256]{1,0:T(8,128)(2,1)}) %reduce-scatter.28.cloned.1.call-update) | async-done | bytes 262160 | tf_op jit(solution)/shard_map/reduce_scatter | solution.py:256
  1833.2 111.3 %reduce-scatter.20.cloned.1.call-done = bf16[384,2048]{1,0:T(8,128)(2,1)} async-done(((bf16[1536,2048]{1,0:T(8,128)(2,1)}), bf16[384,2048]{1,0:T(8,128)(2,1)}) %reduce-scatter.20.cloned.1.call-update) | async-done | bytes 1572880 | tf_op jit(solution)/shard_map/reduce_scatter | solution.py:210
  1949.8 14.0 all-reduce.2
  1964.0 11.1 all-reduce.3
  (243 shorter events, 171.2 us)
Async XLA Ops:
  7.2 18.7 copy-start.15
  7.2 18.7 copy-start.29
  7.2 19.1 copy-start.16
  7.2 19.1 copy-start.23
  7.2 28.9 %copy-start.24 = (bf16[256,128]{1,0:T(8,128)(2,1)S(1)}, bf16[256,128]{1,0:T(8,128)(2,1)}, u32[]{:S(2)}) copy-start(bf16[256,128]{1,0:T(8,128)(2,1)} %param.24) | copy-start | bytes 196612
  7.2 132.9 %all-gather.12.cloned.1.call-start = ((), (), s32[]{:S(2)}) async-start(), calls=%async_computation.13 | async-start | bytes 7864320 | tf_op jit(solution)/shard_map/all_gather | solution.py:83
  10.4 134.4 %copy-start.25 = (f32[384]{0:T(512)}, f32[384]{0:T(512)S(1)}, u32[]{:S(2)}) copy-start(f32[384]{0:T(512)S(1)} %get-tuple-element.401) | copy-start | bytes 4612
  24.3 143.9 %all-gather.14.cloned.1.call-start = ((), (), s32[]{:S(2)}) async-start(), calls=%async_computation.14 | async-start | bytes 2359296 | tf_op jit(solution)/shard_map/all_gather | solution.py:67
  25.1 200.4 %all-gather.16.cloned.1.call-start = ((), (), s32[]{:S(2)}) async-start(), calls=%async_computation.15 | async-start | bytes 2359296 | tf_op jit(solution)/shard_map/all_gather | solution.py:70
  25.8 420.3 %reduce-scatter.14.cloned.1.call-start = ((), (), s32[]{:S(2)}) async-start(), calls=%async_computation.16 | async-start | bytes 15728640 | tf_op jit(solution)/shard_map/reduce_scatter | solution.py:121
  36.1 144.1 %copy-start.10 = (bf16[2048,128]{1,0:T(8,128)(2,1)}, bf16[2048,128]{1,0:T(8,128)(2,1)S(1)}, u32[]{:S(2)}) copy-start(bf16[2048,128]{1,0:T(8,128)(2,1)S(1)} %all_gather.42) | copy-start | bytes 1572868
  45.0 123.2 %copy-start.8 = (bf16[2048,128]{1,0:T(8,128)(2,1)}, bf16[2048,128]{1,0:T(8,128)(2,1)S(1)}, u32[]{:S(2)}) copy-start(bf16[2048,128]{1,0:T(8,128)(2,1)S(1)} %all_gather.43) | copy-start | bytes 1572868
  144.7 31.4 %copy-start.5 = (bf16[1536,128]{1,0:T(8,128)(2,1)}, bf16[1536,128]{1,0:T(8,128)(2,1)S(1)}, u32[]{:S(2)}) copy-start(bf16[1536,128]{1,0:T(8,128)(2,1)S(1)} %convolution_convert_fusion.11) | copy-start | bytes 1179652
  225.4 8.6 copy-start.6
  225.4 8.6 copy-start.13
  234.1 258.1 %all-gather.22.cloned.1.call-start = ((), (), s32[]{:S(2)}) async-start(), calls=%async_computation.19 | async-start | bytes 6488064 | tf_op jit(solution)/shard_map/all_gather | solution.py:75
  234.7 374.9 %all-gather.18.cloned.1.call-start = ((), (), s32[]{:S(2)}) async-start(), calls=%async_computation.17 | async-start | bytes 7864320 | tf_op jit(solution)/shard_map/all_gather | solution.py:130
  450.4 202.6 %all-gather.20.cloned.1.call-start = ((), (), s32[]{:S(2)}) async-start(), calls=%async_computation.18 | async-start | bytes 6488064 | tf_op jit(solution)/shard_map/all_gather | solution.py:74
  451.2 318.8 %all-gather.26.cloned.1.call-start = ((), (), s32[]{:S(2)}) async-start(), calls=%async_computation.22 | async-start | bytes 7864320 | tf_op jit(solution)/shard_map/all_gather | solution.py:142
  451.9 362.6 %all-gather.24.cloned.1.call-start = ((), (), s32[]{:S(2)}) async-start(), calls=%async_computation.20 | async-start | bytes 6488064 | tf_op jit(solution)/shard_map/all_gather | solution.py:76
  452.6 629.6 %reduce-scatter.18.cloned.1.call-start = ((), (), s32[]{:S(2)}) async-start(), calls=%async_computation.23 | async-start | bytes 15728640 | tf_op jit(solution)/shard_map/reduce_scatter | solution.py:149
  837.4 16.4 copy-start.32
  870.2 326.1 %reduce-scatter.16.cloned.1.call-start = ((), (), s32[]{:S(2)}) async-start(), calls=%async_computation.21 | async-start | bytes 7864320 | tf_op jit(solution)/shard_map/reduce_scatter | solution.py:135
  885.3 433.8 %all-gather.28.cloned.1.call-start = ((), (), s32[]{:S(2)}) async-start(), calls=%async_computation.24 | async-start | bytes 7864320 | tf_op jit(solution)/shard_map/all_gather | solution.py:159
  1203.1 219.0 %reduce-scatter.22.cloned.1.call-start = ((), (), s32[]{:S(2)}) async-start(), calls=%async_computation.26 | async-start | bytes 491520 | tf_op jit(solution)/shard_map/reduce_scatter | solution.py:213
  1401.1 42.7 %copy-start.4 = (bf16[384,2048]{1,0:T(8,128)(2,1)S(1)}, bf16[384,2048]{1,0:T(8,128)(2,1)}, u32[]{:S(2)}) copy-start(bf16[384,2048]{1,0:T(8,128)(2,1)} %fusion.39) | copy-start | bytes 4718596
  1401.1 42.7 %copy-start.17 = (bf16[384,128]{1,0:T(8,128)(2,1)S(1)}, bf16[384,128]{1,0:T(8,128)(2,1)}, u32[]{:S(2)}) copy-start(bf16[384,128]{1,0:T(8,128)(2,1)} %param.35) | copy-start | bytes 294916
  1403.1 40.6 %reduce-scatter.24.cloned.1.call-start = ((), (), s32[]{:S(2)}) async-start(), calls=%async_computation.27 | async-start | bytes 491520 | tf_op jit(solution)/shard_map/reduce_scatter | solution.py:216
  1404.0 86.9 %reduce-scatter.36.cloned.1.call-start = ((), (), s32[]{:S(2)}) async-start(), calls=%async_computation.33 | async-start | bytes 589824 | tf_op jit(solution)/shard_map/reduce_scatter | solution.py:250
  1425.0 92.7 %reduce-scatter.38.cloned.1.call-start = ((), (), s32[]{:S(2)}) async-start(), calls=%async_computation.34 | async-start | bytes 589824 | tf_op jit(solution)/shard_map/reduce_scatter | solution.py:253
  1446.1 133.9 %reduce-scatter.34.cloned.1.call-start = ((), (), s32[]{:S(2)}) async-start(), calls=%async_computation.32 | async-start | bytes 6488064 | tf_op jit(solution)/shard_map/reduce_scatter | solution.py:268
  1460.5 182.4 %reduce-scatter.32.cloned.1.call-start = ((), (), s32[]{:S(2)}) async-start(), calls=%async_computation.31 | async-start | bytes 6488064 | tf_op jit(solution)/shard_map/reduce_scatter | solution.py:265
  1475.5 229.8 %reduce-scatter.30.cloned.1.call-start = ((), (), s32[]{:S(2)}) async-start(), calls=%async_computation.30 | async-start | bytes 6488064 | tf_op jit(solution)/shard_map/reduce_scatter | solution.py:262
  1490.8 27.0 %copy-start.12 = (bf16[3,512,512]{2,1,0:T(8,128)(2,1)S(1)}, bf16[3,512,512]{2,1,0:T(8,128)(2,1)}, u32[]{:S(2)}) copy-start(bf16[3,512,512]{2,1,0:T(8,128)(2,1)} %get-tuple-element.157) | copy-start | bytes 4718596
  1490.8 251.4 %all-reduce.7.cloned.1.call-start = ((), (), s32[]{:S(2)}) async-start(), calls=%async_computation.35 | async-start | bytes 262144 | tf_op jit(solution)/shard_map/psum | solution.py:228
  1517.7 268.8 %reduce-scatter.26.cloned.1.call-start = ((), (), s32[]{:S(2)}) async-start(), calls=%async_computation.28 | async-start | bytes 2359296 | tf_op jit(solution)/shard_map/reduce_scatter | solution.py:247
  1525.6 305.8 %reduce-scatter.28.cloned.1.call-start = ((), (), s32[]{:S(2)}) async-start(), calls=%async_computation.29 | async-start | bytes 2359296 | tf_op jit(solution)/shard_map/reduce_scatter | solution.py:256
  1533.6 410.9 %reduce-scatter.20.cloned.1.call-start = ((), (), s32[]{:S(2)}) async-start(), calls=%async_computation.25 | async-start | bytes 7864320 | tf_op jit(solution)/shard_map/reduce_scatter | solution.py:210
  1541.1 166.6 %copy-start.11 = (bf16[2048,128]{1,0:T(8,128)(2,1)S(1)}, bf16[2048,128]{1,0:T(8,128)(2,1)}, u32[]{:S(2)}) copy-start(bf16[2048,128]{1,0:T(8,128)(2,1)} %copy-done.10) | copy-start | bytes 1572868
  1541.1 166.6 %copy-start.19 = (bf16[384,128]{1,0:T(8,128)(2,1)S(1)}, bf16[384,128]{1,0:T(8,128)(2,1)}, u32[]{:S(2)}) copy-start(bf16[384,128]{1,0:T(8,128)(2,1)} %param.34) | copy-start | bytes 294916
  1541.1 166.6 %copy-start.20 = (bf16[384,128]{1,0:T(8,128)(2,1)S(1)}, bf16[384,128]{1,0:T(8,128)(2,1)}, u32[]{:S(2)}) copy-start(bf16[384,128]{1,0:T(8,128)(2,1)} %reduce-scatter.22.cloned.1.call-done) | copy-start | bytes 294916
  1645.1 299.4 %copy-start.1 = (bf16[384,2048]{1,0:T(8,128)(2,1)S(1)}, bf16[384,2048]{1,0:T(8,128)(2,1)}, u32[]{:S(2)}) copy-start(bf16[384,2048]{1,0:T(8,128)(2,1)} %param.20) | copy-start | bytes 4718596
  1645.1 299.4 %copy-start.9 = (bf16[2048,128]{1,0:T(8,128)(2,1)S(1)}, bf16[2048,128]{1,0:T(8,128)(2,1)}, u32[]{:S(2)}) copy-start(bf16[2048,128]{1,0:T(8,128)(2,1)} %copy-done.8) | copy-start | bytes 1572868
  1645.1 299.4 %copy-start.18 = (bf16[384,128]{1,0:T(8,128)(2,1)S(1)}, bf16[384,128]{1,0:T(8,128)(2,1)}, u32[]{:S(2)}) copy-start(bf16[384,128]{1,0:T(8,128)(2,1)} %reduce-scatter.24.cloned.1.call-done) | copy-start | bytes 294916
  1645.1 299.4 %copy-start.22 = (f32[8,1,256]{2,1,0:T(1,128)S(1)}, f32[8,1,256]{2,1,0:T(1,128)}, u32[]{:S(2)}) copy-start(f32[8,1,256]{2,1,0:T(1,128)} %copy-done.21) | copy-start | bytes 24580
  1645.1 299.4 %copy-start.26 = (f32[384]{0:T(512)S(1)}, f32[384]{0:T(512)}, u32[]{:S(2)}) copy-start(f32[384]{0:T(512)} %copy-done.25) | copy-start | bytes 4612
  1833.2 116.6 %copy-start.27 = (bf16[2048]{0:T(1024)(128)(2,1)S(1)}, bf16[2048]{0:T(1024)(128)(2,1)}, u32[]{:S(2)}) copy-start(bf16[2048]{0:T(1024)(128)(2,1)} %get-tuple-element.316) | copy-start | bytes 12292
  1833.2 143.0 %copy-start.28 = (f32[384]{0:T(512)S(1)}, f32[384]{0:T(512)}, u32[]{:S(2)}) copy-start(f32[384]{0:T(512)} %get-tuple-element.400) | copy-start | bytes 4612
  (16 other events, 36.2 us)
Sparse Core Ops, SparseCore 0:
  24.4 115.6 all-gather.11
  142.0 26.1 all-gather.13
  170.1 28.1 all-gather.15
  234.2 211.8 reduce-scatter.13
  447.8 44.3 all-gather.21
  494.2 115.3 all-gather.17
  611.4 41.5 all-gather.19
  654.6 115.3 all-gather.25
  771.9 42.5 all-gather.23
  870.4 211.8 reduce-scatter.17
  1084.6 111.7 reduce-scatter.15
  1203.2 115.8 all-gather.27
  1403.3 18.7 reduce-scatter.21
  1424.9 18.8 reduce-scatter.23
  1447.3 32.3 reduce-scatter.35
  1483.5 34.1 reduce-scatter.37
  1521.0 59.0 reduce-scatter.33
  1583.8 59.0 reduce-scatter.31
  1646.3 59.0 reduce-scatter.29
  1707.7 34.5 all-reduce.6
  1745.5 40.9 reduce-scatter.25
  1790.1 41.2 reduce-scatter.27
  1833.7 110.7 reduce-scatter.19
where the time goes:
time: 2000 us; the launch traced here: 1990 us
  waiting for transfers between devices  1530 us (76%)
  matrix products  286 us (14%)
  other arithmetic  72.1 us (4%)
  blocking collectives  62.9 us (3%)
  local copies, waits for them, and re-layouts  22.5 us (1%)
    reduce_scatter x1, waiting for transfers between devices, on_device(): lax.psum_scatter(jnp.dot(mixed, out_w, preferred_element_type=jnp.float32...  203 us
    reduce_scatter x1, waiting for transfers between devices, on_device(): lax.psum_scatter(contract_cols(gate_grad, gate_w) + contract_cols(up_grad...  197 us
    all_gather x1, waiting for transfers between devices, on_device(): ffn_normed = lax.all_gather(ffn_own, 'tensor', axis=0, tiled=True)  117 us
    all_gather x1, waiting for transfers between devices, on_device(): lax.all_gather(after_grad.astype(jnp.bfloat16), 'tensor', axis=0, tiled=T...  114 us
    reduce_scatter x1, waiting for transfers between devices, on_device(): lax.psum_scatter(normed_part.astype(jnp.bfloat16), 'tensor', scatter_dime...  111 us
    reduce_scatter x1, waiting for transfers between devices, on_device(): lax.psum_scatter(jnp.dot(hidden, down_w, preferred_element_type=jnp.float...  111 us
    all_gather x1, waiting for transfers between devices, on_device(): grad_full = lax.all_gather(d_out, 'tensor', axis=0, tiled=True)  102 us
    all_gather x1, waiting for transfers between devices, on_device(): normed = lax.all_gather(normed_own, 'tensor', axis=0, tiled=True)  95.1 us
  transfers between devices with their start and end apart: 23, of which 21 were waited for; matrix products, arithmetic and copies ran while one was open for 10% of the time, Pallas kernels for 0%

commit v1 on v0

v1 whole, which is shorter than its diff:
```python
import functools

import jax
import jax.numpy as jnp
from jax import lax
from jax.sharding import PartitionSpec as P

HD = 128
norm_eps = 1e-05
F32 = jnp.float32
BF16 = jnp.bfloat16


def dot(left, right, dims):
    return lax.dot_general(left, right, ((dims[0], dims[1]), ((), ())), preferred_element_type=F32)


def nn(left, right):
    return dot(left, right, ((1,), (0,)))


def nt(left, right):
    return dot(left, right, ((1,), (1,)))


def tn(left, right):
    return dot(left, right, ((0,), (0,)))


def lookup(ids, table):
    hits = ids[:, None] == jnp.arange(table.shape[0], dtype=jnp.int32)[None, :]
    return jnp.sum(jnp.where(hits, table[None, :], 0), axis=1)


def norm_back(value, scale, gain, grad):
    weighted = grad * gain
    return scale * weighted - value * (scale * scale * scale) * jnp.mean(
        weighted * value, axis=-1, keepdims=True
    )


def bit_orders(ndp):
    bits = []
    bit = 2
    while bit < ndp:
        bits.append(bit)
        bit *= 2
    return bits, bits[::-1]


def plane_swap(array, ndp, step):
    orders = bit_orders(ndp)
    return lax.ppermute(array, "dp", [(d, d ^ orders[d & 1][step]) for d in range(ndp)])


def core_swap(array, ndp):
    return lax.ppermute(array, "dp", [(d, d ^ 1) for d in range(ndp)])


def slice_table(me, ndp):
    orders = bit_orders(ndp)
    count = len(orders[0])
    table = []
    for place in range(ndp):
        base = me ^ (place // (ndp // 2))
        even = base % 2 == 0
        owner = base
        for step in range(count):
            if (place >> step) & 1:
                owner = owner ^ jnp.where(even, orders[0][step], orders[1][step])
        table.append(owner)
    return table


def gather_plane(shard, ndp):
    steps = len(bit_orders(ndp)[0])
    pieces = [jnp.concatenate([shard, plane_swap(shard, ndp, 0)], axis=0)]
    for step in range(1, steps):
        pieces = pieces + [plane_swap(piece, ndp, step) for piece in pieces]
    return pieces + [core_swap(piece, ndp) for piece in pieces]


def add_low(left, right):
    return (left.astype(F32) + right.astype(F32)).astype(BF16)


def scatter_plane(pieces, ndp):
    steps = len(bit_orders(ndp)[0])
    half = len(pieces) // 2
    moved = [core_swap(piece, ndp) for piece in pieces[half:]]
    pieces = [add_low(keep, come) for keep, come in zip(pieces[:half], moved)]
    for step in range(steps - 1, 0, -1):
        half = len(pieces) // 2
        moved = [plane_swap(piece, ndp, step) for piece in pieces[half:]]
        pieces = [add_low(keep, come) for keep, come in zip(pieces[:half], moved)]
    piece = pieces[0]
    rows = piece.shape[0] // 2
    return add_low(piece[:rows], plane_swap(piece[rows:], ndp, 0))


def ring_next(array, nt_):
    return lax.ppermute(array, "tensor", [(i, (i + 1) % nt_) for i in range(nt_)])


def shift(array, nt_, by):
    return lax.ppermute(array, "tensor", [(i, (i + by) % nt_) for i in range(nt_)])


def ring_gather(array, nt_):
    blocks = [array]
    for _ in range(nt_ - 1):
        blocks.append(ring_next(blocks[-1], nt_))
    return blocks


def ring_scatter(parts, nt_):
    moving = parts[1]
    for place in range(2, nt_):
        moving = add_low(ring_next(moving, nt_), parts[place])
    return ring_next(moving, nt_).astype(F32) + parts[0].astype(F32)


def stack_rows(pieces):
    return jnp.concatenate(pieces, axis=0)


def take_columns(array, table, width):
    return jnp.concatenate(
        [lax.dynamic_slice_in_dim(array, owner * width, width, axis=1) for owner in table], axis=1
    )


def put_columns(array, table, width):
    out = jnp.zeros_like(array)
    for place, owner in enumerate(table):
        out = lax.dynamic_update_slice_in_dim(
            out, array[:, place * width : (place + 1) * width], owner * width, axis=1
        )
    return out


def attend(query, keys, values, bias):
    tokens = query.shape[0]
    heads = query.shape[1] // HD
    scale = HD ** (-0.5)
    mixed, totals = [], []
    for head in range(heads):
        scores = nt(keys, query[:, head * HD : (head + 1) * HD]) * scale + bias
        peak = jnp.max(scores, axis=0, keepdims=True)
        raised = jnp.exp(scores - peak)
        sums = jnp.sum(raised, axis=0, keepdims=True)
        shares = (raised / sums).astype(BF16)
        mixed.append(tn(shares, values).astype(BF16))
        totals.append(peak + jnp.log(sums))
    return jnp.concatenate(mixed, axis=1), jnp.concatenate(totals, axis=0)


def attend_back(query, keys, values, bias, totals, mixed_grad):
    heads = query.shape[1] // HD
    scale = HD ** (-0.5)
    key_acc, value_acc, query_grad = 0.0, 0.0, []
    for head in range(heads):
        cols = slice(head * HD, (head + 1) * HD)
        scores = nt(keys, query[:, cols]) * scale + bias
        shares = jnp.exp(scores - totals[head : head + 1])
        low_shares = shares.astype(BF16)
        share_grad = nt(values, mixed_grad[:, cols])
        value_acc = value_acc + nn(low_shares, mixed_grad[:, cols])
        inner = jnp.sum(shares * share_grad, axis=0, keepdims=True)
        score_grad = (shares * (share_grad - inner)).astype(BF16)
        query_grad.append((scale * tn(score_grad, keys)).astype(BF16))
        key_acc = key_acc + scale * nn(score_grad, query[:, cols])
    return jnp.concatenate(query_grad, axis=1), key_acc, value_acc


def ffn_block(normed, grad, pieces):
    whole = stack_rows(pieces)
    hidden_units = whole.shape[1] // 3
    gate_w = whole[:, :hidden_units]
    up_w = whole[:, hidden_units : 2 * hidden_units]
    down_w = whole[:, 2 * hidden_units :]
    gate = nn(normed, gate_w)
    upward = nn(normed, up_w)
    sigma = jax.nn.sigmoid(gate)
    hidden = (gate * sigma * upward).astype(BF16)
    part = nt(hidden, down_w).astype(BF16)
    hidden_grad = nn(grad, down_w)
    gate_grad = (hidden_grad * upward * sigma * (1.0 + gate * (1.0 - sigma))).astype(BF16)
    up_grad = (hidden_grad * gate * sigma).astype(BF16)
    back = (nt(gate_grad, gate_w) + nt(up_grad, up_w)).astype(BF16)
    return hidden, gate_grad, up_grad, part, back


def on_device(
    ndp,
    nz,
    tokens,
    norm_attn,
    w_query,
    w_key,
    w_value,
    w_out,
    norm_ffn,
    w_gate,
    w_up,
    w_down,
    segment_ids,
    parents,
    positions,
    d_out,
    d_keys,
    d_values,
):
    me = lax.axis_index("dp")
    place_z = lax.axis_index("tensor")
    table = slice_table(me, ndp)
    own, width = tokens.shape[0], tokens.shape[1]
    rows = width // ndp
    heads_w = w_query.shape[1]
    hidden_units = w_gate.shape[1]

    gains = jnp.concatenate(
        [norm_attn[:, None], norm_ffn[:, None], jnp.zeros((rows, HD - 2), BF16)], axis=1
    )
    small = gather_plane(jnp.concatenate([w_key, w_value, gains], axis=1), ndp)
    attn_ring = ring_gather(jnp.concatenate([w_query, w_out.T], axis=1), nz)
    attn_w = [gather_plane(block, ndp) for block in attn_ring]
    ffn_w = gather_plane(jnp.concatenate([w_gate, w_up, w_down.T], axis=1), ndp)

    small_w = stack_rows(small)
    gain_rows = small_w[:, 2 * HD : 2 * HD + 2].astype(F32).T
    attn_gain, ffn_gain = gain_rows[0:1], gain_rows[1:2]
    kv_w = small_w[:, : 2 * HD]

    residual = take_columns(tokens, table, rows).astype(F32)
    grad_low = take_columns(d_out, table, rows)
    grad_ring = ring_gather(grad_low, nz)

    attn_scale = lax.rsqrt(jnp.mean(residual * residual, axis=-1, keepdims=True) + norm_eps)
    normed = (residual * attn_scale * attn_gain).astype(BF16)
    kv_own = nn(normed, kv_w).astype(BF16)
    kv_ring = [kv_own] + [shift(kv_own, nz, by) for by in range(1, nz)]
    kv = stack_rows(kv_ring)
    keys, values = kv[:, :HD], kv[:, HD:]

    first_up = lookup(segment_ids, parents)
    second_up = lookup(first_up, parents)

    def own_rows(vector):
        return lax.dynamic_slice_in_dim(vector, place_z * own, own, axis=0)

    def ring_rows(vector):
        return jnp.concatenate(
            [
                lax.dynamic_slice_in_dim(vector, ((place_z - r) % nz) * own, own, axis=0)
                for r in range(nz)
            ],
            axis=0,
        )

    key_segment, key_place = ring_rows(segment_ids)[:, None], ring_rows(positions)[:, None]
    linked = (
        (key_segment == own_rows(segment_ids)[None])
        | (key_segment == own_rows(first_up)[None])
        | (key_segment == own_rows(second_up)[None])
    )
    bias = jnp.where(linked & (key_place <= own_rows(positions)[None]), 0.0, -1e30).astype(F32)

    queries, mixes, totals = [], [], []
    attn_sum = 0.0
    for block in range(nz):
        whole = stack_rows(attn_w[block])
        query = nn(normed, whole[:, :heads_w]).astype(BF16)
        mixed, total = attend(query, keys, values, bias)
        attn_sum = attn_sum + nt(mixed, whole[:, heads_w:])
        queries.append(query)
        mixes.append(mixed)
        totals.append(total)
    after_attn = residual + attn_sum
    ffn_scale = lax.rsqrt(jnp.mean(after_attn * after_attn, axis=-1, keepdims=True) + norm_eps)
    ffn_own = (after_attn * ffn_scale * ffn_gain).astype(BF16)

    ffn_ring = ring_gather(ffn_own, nz)
    hiddens, gate_grads, up_grads, parts, backs = [], [], [], [], []
    for block in range(nz):
        hidden, gate_grad, up_grad, part, back = ffn_block(
            ffn_ring[block], grad_ring[block], ffn_w
        )
        hiddens.append(hidden)
        gate_grads.append(gate_grad)
        up_grads.append(up_grad)
        parts.append(part)
        backs.append(back)
    ffn_normed_grad = ring_scatter(backs, nz)
    output = (after_attn + ring_scatter(parts, nz)).astype(BF16)

    ffn_all, grad_all = stack_rows(ffn_ring), stack_rows(grad_ring)
    hidden_all = stack_rows(hiddens)
    gate_up_grad = jnp.concatenate([stack_rows(gate_grads), stack_rows(up_grads)], axis=1)
    pieces = []
    step = width // len(ffn_w)
    for piece in range(len(ffn_w)):
        cols = slice(piece * step, (piece + 1) * step)
        pieces.append(
            jnp.concatenate(
                [tn(ffn_all[:, cols], gate_up_grad), tn(grad_all[:, cols], hidden_all)], axis=1
            ).astype(BF16)
        )
    ffn_w_grad = scatter_plane(pieces, ndp).astype(F32)

    after_grad = grad_low.astype(F32) + norm_back(after_attn, ffn_scale, ffn_gain, ffn_normed_grad)
    ffn_gain_term = jnp.sum(ffn_normed_grad * after_attn * ffn_scale, axis=0)
    branch = after_grad.astype(BF16)

    key_acc, value_acc = 0.0, 0.0
    normed_grad = 0.0
    attn_grads = []
    for block in range(nz):
        whole = stack_rows(attn_w[block])
        mixed_grad = nn(branch, whole[:, heads_w:]).astype(BF16)
        query_grad, key_part, value_part = attend_back(
            queries[block], keys, values, bias, totals[block], mixed_grad
        )
        key_acc, value_acc = key_acc + key_part, value_acc + value_part
        normed_grad = normed_grad + nt(query_grad, whole[:, :heads_w])
        pieces = []
        for piece in range(len(ffn_w)):
            cols = slice(piece * step, (piece + 1) * step)
            pieces.append(
                jnp.concatenate(
                    [tn(normed[:, cols], query_grad), tn(branch[:, cols], mixes[block])], axis=1
                ).astype(BF16)
            )
        attn_grads.append(scatter_plane(pieces, ndp))
    attn_w_grad = ring_scatter(attn_grads, nz)

    kv_acc = jnp.concatenate([key_acc, value_acc], axis=1).astype(BF16)
    kv_sum = kv_acc[:own].astype(F32)
    for by in range(1, nz):
        kv_sum = kv_sum + shift(kv_acc[by * own : (by + 1) * own], nz, -by).astype(F32)
    kv_given = jnp.concatenate([d_keys, d_values], axis=1).astype(F32)
    kv_grad = (kv_sum + kv_given).astype(BF16)
    normed_grad = normed_grad + nt(kv_grad, kv_w)
    input_grad = after_grad + norm_back(residual, attn_scale, attn_gain, normed_grad)
    attn_gain_term = jnp.sum(normed_grad * residual * attn_scale, axis=0)

    small_grad = jnp.concatenate(
        [
            tn(normed, kv_grad),
            attn_gain_term[:, None],
            ffn_gain_term[:, None],
            jnp.zeros((width, HD - 2), F32),
        ],
        axis=1,
    ).astype(BF16)
    small_sum = scatter_plane(
        [small_grad[p * step : (p + 1) * step] for p in range(len(ffn_w))], ndp
    )
    total = small_sum.astype(F32)
    for by in range(1, nz):
        total = total + shift(small_sum, nz, by).astype(F32)

    kv_out = jnp.zeros((nz * own, 2 * HD), BF16)
    for r in range(nz):
        kv_out = lax.dynamic_update_slice_in_dim(
            kv_out, kv_ring[r], ((place_z - r) % nz) * own, axis=0
        )
    return (
        put_columns(output, table, rows),
        kv_out[:, :HD],
        kv_out[:, HD:],
        put_columns(input_grad, table, rows),
        total[:, 2 * HD],
        attn_w_grad[:, :heads_w],
        total[:, :HD],
        total[:, HD : 2 * HD],
        attn_w_grad[:, heads_w:].T,
        total[:, 2 * HD + 1],
        ffn_w_grad[:, :hidden_units],
        ffn_w_grad[:, hidden_units : 2 * hidden_units],
        ffn_w_grad[:, 2 * hidden_units :].T,
    )


def solution(mesh):
    in_specs = (
        P(("dp", "tensor"), None),
        P("dp"),
        P("dp", "tensor"),
        P("dp", None),
        P("dp", None),
        P("tensor", "dp"),
        P("dp"),
        P("dp", "tensor"),
        P("dp", "tensor"),
        P("tensor", "dp"),
        P("dp"),
        P(),
        P("dp"),
        P(("dp", "tensor"), None),
        P(("dp", "tensor"), None),
        P(("dp", "tensor"), None),
    )
    out_specs = (
        P(("dp", "tensor"), None),
        P("dp", None),
        P("dp", None),
        P(("dp", "tensor"), None),
        P("dp"),
        P("dp", "tensor"),
        P("dp", None),
        P("dp", None),
        P("tensor", "dp"),
        P("dp"),
        P("dp", "tensor"),
        P("dp", "tensor"),
        P("tensor", "dp"),
    )
    body = functools.partial(on_device, mesh.shape["dp"], mesh.shape["tensor"])
    return jax.shard_map(
        body, mesh=mesh, in_specs=in_specs, out_specs=out_specs, check_vma=False
    )
```

time: 2000 us -> 1050 us (0.53)
  waiting for transfers between devices: 1530 us -> 382 us
  local copies, waits for them, and re-layouts: 22.5 us -> 104 us
  starting transfers between devices: 1.57 us -> 82.2 us
  other arithmetic: 72.1 us -> 144 us
  blocking collectives: 62.9 us -> 0 us
  matrix products: 286 us -> 327 us
    reduce_scatter x13 -> x0, waiting for transfers between devices: 927 us -> none  [the longest x1 203 us: on_device(): lax.psum_scatter(jnp.dot(mixed, out_w, preferred_element_type=jnp.float32...]
    all_gather x9 -> x0, waiting for transfers between devices: 564 us -> none  [the longest x1 117 us: on_device(): ffn_normed = lax.all_gather(ffn_own, 'tensor', axis=0, tiled=True)]
    ppermute x0 -> x75, waiting for transfers between devices: none -> 382 us  [the longest x18 277 us: ring_next(): lax.ppermute(array, 'tensor', [(i, (i + 1) % nt_) for i in range(nt_)])]
    concatenate x0 -> x21, other arithmetic: none -> 92.5 us  [the longest x1 65 us: on_device(): jnp.concatenate([stack_rows(gate_grads), stack_rows(up_grads)], axis=1)]
    ppermute x0 -> x75, starting transfers between devices: none -> 82.2 us  [the longest x24 33.3 us: plane_swap(): lax.ppermute(array, 'dp', [(d, d ^ orders[d & 1][step]) for d in range(nd...]
    unnamed x64 -> x595, local copies, waits for them, and re-layouts: 4.64 us -> 72.2 us
    dot_general x42 -> x179, matrix products: 286 us -> 327 us  [dot(): lax.dot_general(left, right, ((dims[0], dims[1]), ((), ())), preferred_el...]
    all_gather x4 -> x0, blocking collectives: 37.9 us -> none  [the longest x1 10.3 us: on_device(): lax.all_gather(norm_attn, 'dp', axis=0, tiled=True)]
  transfers between devices with their start and end apart: 23 -> 75, of which waited for: 21 -> 29; matrix products, arithmetic and copies ran while one was open for 10% -> 32% of each run, Pallas kernels for 0% -> 0%
where the time goes in v1:
time: 1050 us
  waiting for transfers between devices  382 us (36%)
  matrix products  327 us (31%)
  other arithmetic  144 us (14%)
  local copies, waits for them, and re-layouts  104 us (10%)
  starting transfers between devices  82.2 us (8%)
    dot_general x179, matrix products, dot(): lax.dot_general(left, right, ((dims[0], dims[1]), ((), ())), preferred_el...  327 us
    ppermute x18, waiting for transfers between devices, ring_next(): lax.ppermute(array, 'tensor', [(i, (i + 1) % nt_) for i in range(nt_)])  277 us
    unnamed x595, local copies, waits for them, and re-layouts  72.2 us
    ppermute x24, waiting for transfers between devices, plane_swap(): lax.ppermute(array, 'dp', [(d, d ^ orders[d & 1][step]) for d in range(nd...  70.7 us
    concatenate x1, other arithmetic, on_device(): jnp.concatenate([stack_rows(gate_grads), stack_rows(up_grads)], axis=1)  65 us
    ppermute x24, starting transfers between devices, plane_swap(): lax.ppermute(array, 'dp', [(d, d ^ orders[d & 1][step]) for d in range(nd...  33.3 us
    ppermute x18, starting transfers between devices, ring_next(): lax.ppermute(array, 'tensor', [(i, (i + 1) % nt_) for i in range(nt_)])  31.8 us
    ppermute x9, waiting for transfers between devices, shift(): lax.ppermute(array, 'tensor', [(i, (i + by) % nt_) for i in range(nt_)])  30.9 us
  transfers between devices with their start and end apart: 75, of which 29 were waited for; matrix products, arithmetic and copies ran while one was open for 32% of the time, Pallas kernels for 0%

profile of v1, /device:TPU:0, one launch (start us, length us, event | category | flops | bytes accessed | tf_op | source)
XLA Modules:
  0.0 1046.1 jit_solution(2502076009558806018)
XLA Ops:
  61.4 7.6 collective-permute-done.16
  78.1 13.9 %collective-permute-done.5 = bf16[384,256]{1,0:T(8,128)(2,1)S(1)} collective-permute-done((bf16[384,256]{1,0:T(8,128)(2,1)S(1)}, bf16[384,256]{1,0:T(8,128)(2,1)S(1)}, u32[]{:S(2)}, u32[]{:S(2)}) %collective-permute-start.5) | collective-permute-done | bytes 196640 | tf_op jit(solution)/shard_map/ppermute | solution.py:106
  92.8 7.2 collective-permute-done.6
  105.7 20.6 %collective-permute-done.13 = bf16[512,1024]{0,1:T(8,128)(2,1)S(1)} collective-permute-done((bf16[512,1024]{0,1:T(8,128)(2,1)S(1)}, bf16[512,1024]{0,1:T(8,128)(2,1)S(1)}, u32[]{:S(2)}, u32[]{:S(2)}) %collective-permute-start.13) | collective-permute-done | bytes 1048608 | tf_op jit(solution)/shard_map/ppermute | solution.py:53
  127.4 10.5 %collective-permute-done.36 = bf16[384,2048]{1,0:T(8,128)(2,1)} collective-permute-done((bf16[384,2048]{1,0:T(8,128)(2,1)S(1)}, bf16[384,2048]{1,0:T(8,128)(2,1)}, u32[]{:S(2)}, u32[]{:S(2)}) %collective-permute-start.36) | collective-permute-done | bytes 1572896 | tf_op jit(solution)/shard_map/ppermute | solution.py:102
  147.2 12.2 %pad_maximum_fusion.2 = bf16[512,4224]{0,1:T(8,128)(2,1)S(1)} fusion(bf16[256,4224]{0,1:T(8,128)(2,1)S(1)} %collective-permute-done.27, bf16[256,1408]{0,1:T(8,128)(2,1)S(1)} %bitcast.83, bf16[256,1408]{0,1:T(8,128)(2,1)S(1)} %copy-done.46, bf16[256,1408]{0,1:T(8,128)(2,1)S(1)} %copy-done.47), kind=kLoop, calls=%fused_computation.32 | loop fusion | flops 17301504 | bytes 8650752 | tf_op jit(solution)/shard_map/concatenate | solution.py:77
  214.0 34.2 %collective-permute-done.26 = bf16[384,2048]{1,0:T(8,128)(2,1)S(1)} collective-permute-done((bf16[384,2048]{1,0:T(8,128)(2,1)S(1)}, bf16[384,2048]{1,0:T(8,128)(2,1)S(1)}, u32[]{:S(2)}, u32[]{:S(2)}) %collective-permute-start.26) | collective-permute-done | bytes 1572896 | tf_op jit(solution)/shard_map/ppermute | solution.py:102
  253.1 62.1 %collective-permute-done.32 = bf16[384,2048]{1,0:T(8,128)(2,1)S(1)} collective-permute-done((bf16[384,2048]{1,0:T(8,128)(2,1)S(1)}, bf16[384,2048]{1,0:T(8,128)(2,1)S(1)}, u32[]{:S(2)}, u32[]{:S(2)}) %collective-permute-start.32) | collective-permute-done | bytes 1572896 | tf_op jit(solution)/shard_map/ppermute | solution.py:102
  327.3 25.5 %collective-permute-done.34 = bf16[384,2048]{1,0:T(8,128)(2,1)S(1)} collective-permute-done((bf16[384,2048]{1,0:T(8,128)(2,1)S(1)}, bf16[384,2048]{1,0:T(8,128)(2,1)S(1)}, u32[]{:S(2)}, u32[]{:S(2)}) %collective-permute-start.34) | collective-permute-done | bytes 1572896 | tf_op jit(solution)/shard_map/ppermute | solution.py:102
  359.1 5.3 fusion.202
  364.3 5.3 fusion.222
  369.6 5.7 fusion.208
  375.4 6.6 fusion.228
  382.0 8.0 multiply_convert_fusion.24
  390.0 7.5 convolution_convert_fusion.11
  397.5 7.0 multiply_convert_fusion.18
  404.5 7.9 fusion.206
  412.4 6.6 fusion.226
  419.1 5.4 fusion.204
  424.5 5.6 fusion.224
  430.1 8.4 multiply_convert_fusion.22
  438.5 7.5 multiply_convert_fusion.20
  452.6 5.0 fusion.220
  457.6 65.0 %maximum_maximum_fusion = bf16[1536,2816]{1,0:T(8,128)(2,1)S(1)} fusion(bf16[384,1408]{1,0:T(8,128)(2,1)S(1)} %copy-done.125, bf16[384,1408]{1,0:T(8,128)(2,1)S(1)} %copy-done.130, bf16[384,1408]{1,0:T(8,128)(2,1)} %copy-done.132, bf16[384,1408]{1,0:T(8,128)(2,1)S(1)} %get-tuple-element.74, bf16[384,1408]{1,0:T(8,128)(2,1)S(1)} %copy-done.123, ...), kind=kLoop, calls=%fused_computation.16 | loop fusion | flops 69206016 | bytes 17301504 | tf_op jit(solution)/shard_map/concatenate | solution.py:299
  522.7 6.5 convolution_convert_fusion
  529.2 6.1 convolution_convert_fusion.1
  539.1 4.9 convolution_convert_fusion.2
  544.1 5.3 convolution_convert_fusion.7
  549.4 6.2 convolution_convert_fusion.3
  555.6 5.5 add_convert_fusion.9
  562.4 4.7 fusion.218
  569.6 56.7 %collective-permute-done.37 = bf16[384,2048]{1,0:T(8,128)(2,1)S(1)} collective-permute-done((bf16[384,2048]{1,0:T(8,128)(2,1)S(1)}, bf16[384,2048]{1,0:T(8,128)(2,1)S(1)}, u32[]{:S(2)}, u32[]{:S(2)}) %collective-permute-start.37) | collective-permute-done | bytes 1572896 | tf_op jit(solution)/shard_map/ppermute | solution.py:102
  626.3 5.2 add_convert_fusion.7
  631.6 5.4 add_convert_fusion.12
  637.1 4.8 fusion.216
  646.7 24.0 %collective-permute-done.39 = bf16[384,2048]{1,0:T(8,128)(2,1)S(1)} collective-permute-done((bf16[384,2048]{1,0:T(8,128)(2,1)S(1)}, bf16[384,2048]{1,0:T(8,128)(2,1)S(1)}, u32[]{:S(2)}, u32[]{:S(2)}) %collective-permute-start.39) | collective-permute-done | bytes 1572896 | tf_op jit(solution)/shard_map/ppermute | solution.py:102
  670.7 5.4 add_convert_fusion.5
  676.2 28.2 %collective-permute-done.33 = bf16[384,2048]{1,0:T(8,128)(2,1)S(1)} collective-permute-done((bf16[384,2048]{1,0:T(8,128)(2,1)S(1)}, bf16[384,2048]{1,0:T(8,128)(2,1)S(1)}, u32[]{:S(2)}, u32[]{:S(2)}) %collective-permute-start.33) | collective-permute-done | bytes 1572896 | tf_op jit(solution)/shard_map/ppermute | solution.py:102
  704.4 6.4 add_convert_fusion.11
  716.6 21.6 %collective-permute-done.41 = bf16[384,2048]{1,0:T(8,128)(2,1)S(1)} collective-permute-done((bf16[384,2048]{1,0:T(8,128)(2,1)S(1)}, bf16[384,2048]{1,0:T(8,128)(2,1)S(1)}, u32[]{:S(2)}, u32[]{:S(2)}) %collective-permute-start.41) | collective-permute-done | bytes 1572896 | tf_op jit(solution)/shard_map/ppermute | solution.py:102
  738.1 6.0 multiply_reduce_fusion
  864.2 7.2 add_convert_fusion.10
  931.9 10.7 %collective-permute-done.54 = bf16[512,1024]{0,1:T(8,128)(2,1)S(1)} collective-permute-done((bf16[512,1024]{0,1:T(8,128)(2,1)S(1)}, bf16[512,1024]{0,1:T(8,128)(2,1)S(1)}, u32[]{:S(2)}, u32[]{:S(2)}) %collective-permute-start.54) | collective-permute-done | bytes 1048608 | tf_op jit(solution)/shard_map/ppermute | solution.py:53
  945.6 8.2 collective-permute-done.59
  955.6 15.1 %collective-permute-done.64 = bf16[512,1024]{0,1:T(8,128)(2,1)S(1)} collective-permute-done((bf16[512,1024]{0,1:T(8,128)(2,1)S(1)}, bf16[512,1024]{0,1:T(8,128)(2,1)S(1)}, u32[]{:S(2)}, u32[]{:S(2)}) %collective-permute-start.64) | collective-permute-done | bytes 1048608 | tf_op jit(solution)/shard_map/ppermute | solution.py:53
  982.8 6.5 collective-permute-done.60
  1001.5 6.9 collective-permute-done.61
  1010.9 18.4 %collective-permute-start.66 = (bf16[256,1024]{0,1:T(8,128)(2,1)}, bf16[256,1024]{0,1:T(8,128)(2,1)}, u32[]{:S(2)}, u32[]{:S(2)}) collective-permute-start(bf16[256,1024]{0,1:T(8,128)(2,1)} %add_convert_fusion.26), channel_id=1, source_target_pairs={{0,1},{1,2},{2,3},{3,0},{4,5},{5,6},{6,7},{7,4},{8,9},{9,10},{10,1... | collective-permute-start | bytes 1572872 | tf_op jit(solution)/shard_map/ppermute | solution.py:102
  (1036 shorter events, 414.0 us)
Async XLA Ops:
  3.8 48.3 %collective-permute-start.11 = (bf16[256,1024]{0,1:T(8,128)(2,1)}, bf16[256,1024]{0,1:T(8,128)(2,1)}, u32[]{:S(2)}, u32[]{:S(2)}) collective-permute-start(bf16[256,1024]{0,1:T(8,128)(2,1)} %get-tuple-element.95), channel_id=1, source_target_pairs={{0,1},{1,2},{2,3},{3,0},{4,5},{5,6},{6,7},{7,4},{8,9},{9,10},{10,1... | collective-permute-start | bytes 1572872 | tf_op jit(solution)/shard_map/ppermute | solution.py:102
  6.8 42.5 %collective-permute-start.7 = (bf16[256,1024]{0,1:T(8,128)(2,1)}, bf16[256,1024]{0,1:T(8,128)(2,1)}, u32[]{:S(2)}, u32[]{:S(2)}) collective-permute-start(bf16[256,1024]{0,1:T(8,128)(2,1)} %get-tuple-element.95), channel_id=1, source_target_pairs={{0,8},{4,20},{8,0},{12,28},{16,24},{20,4},{24,16},{28,12},{1,9},{5... | collective-permute-start | bytes 1572872 | tf_op jit(solution)/shard_map/ppermute | solution.py:53
  11.5 27.9 %collective-permute-start = (bf16[256,384]{1,0:T(8,128)(2,1)}, bf16[256,384]{1,0:T(8,128)(2,1)}, u32[]{:S(2)}, u32[]{:S(2)}) collective-permute-start(bf16[256,384]{1,0:T(8,128)(2,1)} %concatenate.214), channel_id=1, source_target_pairs={{0,8},{4,20},{8,0},{12,28},{16,24},{20,4},{24,16},{28,12},{1,9},{5... | collective-permute-start | bytes 589832 | tf_op jit(solution)/shard_map/ppermute | solution.py:53
  50.5 50.4 %collective-permute-start.8 = (bf16[512,1024]{0,1:T(8,128)(2,1)S(1)}, bf16[512,1024]{0,1:T(8,128)(2,1)S(1)}, u32[]{:S(2)}, u32[]{:S(2)}) collective-permute-start(bf16[512,1024]{0,1:T(8,128)(2,1)S(1)} %pad_maximum_fusion.7), channel_id=1, source_target_pairs={{0,16},{4,12},{8,24},{12,4},{16,0},{20,28},{24,8},{28,20},{1,17},{... | collective-permute-start | bytes 3145736 | tf_op jit(solution)/shard_map/ppermute | solution.py:53
  53.7 21.9 %collective-permute-start.12 = (bf16[256,1024]{0,1:T(8,128)(2,1)}, bf16[256,1024]{0,1:T(8,128)(2,1)S(1)}, u32[]{:S(2)}, u32[]{:S(2)}) collective-permute-start(bf16[256,1024]{0,1:T(8,128)(2,1)} %collective-permute-done.11), channel_id=1, source_target_pairs={{0,8},{4,20},{8,0},{12,28},{16,24},{20,4},{24,16},{28,12},{1,9},{5... | collective-permute-start | bytes 1572872 | tf_op jit(solution)/shard_map/ppermute | solution.py:53
  60.1 31.9 %collective-permute-start.5 = (bf16[384,256]{1,0:T(8,128)(2,1)S(1)}, bf16[384,256]{1,0:T(8,128)(2,1)S(1)}, u32[]{:S(2)}, u32[]{:S(2)}) collective-permute-start(bf16[384,256]{1,0:T(8,128)(2,1)S(1)} %get-tuple-element.153), channel_id=1, source_target_pairs={{0,2},{1,3},{2,0},{3,1},{4,6},{5,7},{6,4},{7,5},{8,10},{9,11},{10,... | collective-permute-start | bytes 589832 | tf_op jit(solution)/shard_map/ppermute | solution.py:106
  69.0 31.0 %collective-permute-start.21 = (bf16[256,1024]{0,1:T(8,128)(2,1)S(1)}, bf16[256,1024]{0,1:T(8,128)(2,1)S(1)}, u32[]{:S(2)}, u32[]{:S(2)}) collective-permute-start(bf16[256,1024]{0,1:T(8,128)(2,1)S(1)} %collective-permute-done.16), channel_id=1, source_target_pairs={{0,1},{1,2},{2,3},{3,0},{4,5},{5,6},{6,7},{7,4},{8,9},{9,10},{10,1... | collective-permute-start | bytes 1572872 | tf_op jit(solution)/shard_map/ppermute | solution.py:102
  72.8 19.9 %collective-permute-start.4 = (bf16[384,256]{1,0:T(8,128)(2,1)S(1)}, bf16[384,256]{1,0:T(8,128)(2,1)S(1)}, u32[]{:S(2)}, u32[]{:S(2)}) collective-permute-start(bf16[384,256]{1,0:T(8,128)(2,1)S(1)} %get-tuple-element.153), channel_id=1, source_target_pairs={{0,1},{1,2},{2,3},{3,0},{4,5},{5,6},{6,7},{7,4},{8,9},{9,10},{10,1... | collective-permute-start | bytes 589832 | tf_op jit(solution)/shard_map/ppermute | solution.py:106
  75.6 24.5 %collective-permute-start.17 = (bf16[256,1024]{0,1:T(8,128)(2,1)S(1)}, bf16[256,1024]{0,1:T(8,128)(2,1)S(1)}, u32[]{:S(2)}, u32[]{:S(2)}) collective-permute-start(bf16[256,1024]{0,1:T(8,128)(2,1)S(1)} %collective-permute-done.16), channel_id=1, source_target_pairs={{0,8},{4,20},{8,0},{12,28},{16,24},{20,4},{24,16},{28,12},{1,9},{5... | collective-permute-start | bytes 1572872 | tf_op jit(solution)/shard_map/ppermute | solution.py:53
  92.0 51.7 %collective-permute-start.27 = (bf16[256,4224]{0,1:T(8,128)(2,1)S(1)}, bf16[256,4224]{0,1:T(8,128)(2,1)S(1)}, u32[]{:S(2)}, u32[]{:S(2)}) collective-permute-start(bf16[256,4224]{0,1:T(8,128)(2,1)S(1)} %copy-done.98), channel_id=1, source_target_pairs={{0,8},{4,20},{8,0},{12,28},{16,24},{20,4},{24,16},{28,12},{1,9},{5... | collective-permute-start | bytes 6488072 | tf_op jit(solution)/shard_map/ppermute | solution.py:53
  100.0 37.9 %collective-permute-start.36 = (bf16[384,2048]{1,0:T(8,128)(2,1)S(1)}, bf16[384,2048]{1,0:T(8,128)(2,1)}, u32[]{:S(2)}, u32[]{:S(2)}) collective-permute-start(bf16[384,2048]{1,0:T(8,128)(2,1)S(1)} %dynamic-slice_dynamic-update-slice_fusion), channel_id=1, source_target_pairs={{0,1},{1,2},{2,3},{3,0},{4,5},{5,6},{6,7},{7,4},{8,9},{9,10},{10,1... | collective-permute-start | bytes 4718600 | tf_op jit(solution)/shard_map/ppermute | solution.py:102
  100.1 26.2 %collective-permute-start.13 = (bf16[512,1024]{0,1:T(8,128)(2,1)S(1)}, bf16[512,1024]{0,1:T(8,128)(2,1)S(1)}, u32[]{:S(2)}, u32[]{:S(2)}) collective-permute-start(bf16[512,1024]{0,1:T(8,128)(2,1)S(1)} %get-tuple-element.90), channel_id=1, source_target_pairs={{0,16},{4,12},{8,24},{12,4},{16,0},{20,28},{24,8},{28,20},{1,17},{... | collective-permute-start | bytes 3145736 | tf_op jit(solution)/shard_map/ppermute | solution.py:53
  100.9 26.2 %collective-permute-start.14 = (bf16[512,1024]{0,1:T(8,128)(2,1)S(1)}, bf16[512,1024]{0,1:T(8,128)(2,1)S(1)}, u32[]{:S(2)}, u32[]{:S(2)}) collective-permute-start(bf16[512,1024]{0,1:T(8,128)(2,1)S(1)} %get-tuple-element.90), channel_id=1, source_target_pairs={{0,4},{4,0},{8,12},{12,8},{16,20},{20,16},{24,28},{28,24},{1,5},{5... | collective-permute-start | bytes 3145736 | tf_op jit(solution)/shard_map/ppermute | solution.py:57
  103.3 39.1 %collective-permute-start.22 = (bf16[256,1024]{0,1:T(8,128)(2,1)S(1)}, bf16[256,1024]{0,1:T(8,128)(2,1)S(1)}, u32[]{:S(2)}, u32[]{:S(2)}) collective-permute-start(bf16[256,1024]{0,1:T(8,128)(2,1)S(1)} %collective-permute-done.21), channel_id=1, source_target_pairs={{0,8},{4,20},{8,0},{12,28},{16,24},{20,4},{24,16},{28,12},{1,9},{5... | collective-permute-start | bytes 1572872 | tf_op jit(solution)/shard_map/ppermute | solution.py:53
  126.3 41.5 %collective-permute-start.18 = (bf16[512,1024]{0,1:T(8,128)(2,1)}, bf16[512,1024]{0,1:T(8,128)(2,1)S(1)}, u32[]{:S(2)}, u32[]{:S(2)}) collective-permute-start(bf16[512,1024]{0,1:T(8,128)(2,1)} %get-tuple-element.96), channel_id=1, source_target_pairs={{0,16},{4,12},{8,24},{12,4},{16,0},{20,28},{24,8},{28,20},{1,17},{... | collective-permute-start | bytes 3145736 | tf_op jit(solution)/shard_map/ppermute | solution.py:53
  127.2 42.5 %collective-permute-start.19 = (bf16[512,1024]{0,1:T(8,128)(2,1)}, bf16[512,1024]{0,1:T(8,128)(2,1)S(1)}, u32[]{:S(2)}, u32[]{:S(2)}) collective-permute-start(bf16[512,1024]{0,1:T(8,128)(2,1)} %get-tuple-element.96), channel_id=1, source_target_pairs={{0,4},{4,0},{8,12},{12,8},{16,20},{20,16},{24,28},{28,24},{1,5},{5... | collective-permute-start | bytes 3145736 | tf_op jit(solution)/shard_map/ppermute | solution.py:57
  137.9 21.4 %collective-permute-start.10 = (bf16[512,1024]{0,1:T(8,128)(2,1)S(1)}, bf16[512,1024]{0,1:T(8,128)(2,1)}, u32[]{:S(2)}, u32[]{:S(2)}) collective-permute-start(bf16[512,1024]{0,1:T(8,128)(2,1)S(1)} %collective-permute-done.8), channel_id=1, source_target_pairs={{0,4},{4,0},{8,12},{12,8},{16,20},{20,16},{24,28},{28,24},{1,5},{5... | collective-permute-start | bytes 3145736 | tf_op jit(solution)/shard_map/ppermute | solution.py:57
  142.4 71.6 %collective-permute-start.38 = (bf16[384,2048]{1,0:T(8,128)(2,1)}, bf16[384,2048]{1,0:T(8,128)(2,1)}, u32[]{:S(2)}, u32[]{:S(2)}) collective-permute-start(bf16[384,2048]{1,0:T(8,128)(2,1)} %collective-permute-done.36), channel_id=1, source_target_pairs={{0,1},{1,2},{2,3},{3,0},{4,5},{5,6},{6,7},{7,4},{8,9},{9,10},{10,1... | collective-permute-start | bytes 4718600 | tf_op jit(solution)/shard_map/ppermute | solution.py:102
  143.8 36.3 %collective-permute-start.23 = (bf16[512,1024]{0,1:T(8,128)(2,1)}, bf16[512,1024]{0,1:T(8,128)(2,1)S(1)}, u32[]{:S(2)}, u32[]{:S(2)}) collective-permute-start(bf16[512,1024]{0,1:T(8,128)(2,1)} %get-tuple-element.86), channel_id=1, source_target_pairs={{0,16},{4,12},{8,24},{12,4},{16,0},{20,28},{24,8},{28,20},{1,17},{... | collective-permute-start | bytes 3145736 | tf_op jit(solution)/shard_map/ppermute | solution.py:53
  159.4 22.3 %collective-permute-start.24 = (bf16[512,1024]{0,1:T(8,128)(2,1)}, bf16[512,1024]{0,1:T(8,128)(2,1)S(1)}, u32[]{:S(2)}, u32[]{:S(2)}) collective-permute-start(bf16[512,1024]{0,1:T(8,128)(2,1)} %get-tuple-element.86), channel_id=1, source_target_pairs={{0,4},{4,0},{8,12},{12,8},{16,20},{20,16},{24,28},{28,24},{1,5},{5... | collective-permute-start | bytes 3145736 | tf_op jit(solution)/shard_map/ppermute | solution.py:57
  169.7 79.2 %collective-permute-start.28 = (bf16[512,4224]{0,1:T(8,128)(2,1)S(1)}, bf16[512,4224]{0,1:T(8,128)(2,1)}, u32[]{:S(2)}, u32[]{:S(2)}) collective-permute-start(bf16[512,4224]{0,1:T(8,128)(2,1)S(1)} %pad_maximum_fusion.2), channel_id=1, source_target_pairs={{0,16},{4,12},{8,24},{12,4},{16,0},{20,28},{24,8},{28,20},{1,17},{... | collective-permute-start | bytes 12976136 | tf_op jit(solution)/shard_map/ppermute | solution.py:53
  172.4 150.4 %collective-permute-start.29 = (bf16[512,4224]{0,1:T(8,128)(2,1)S(1)}, bf16[512,4224]{0,1:T(8,128)(2,1)}, u32[]{:S(2)}, u32[]{:S(2)}) collective-permute-start(bf16[512,4224]{0,1:T(8,128)(2,1)S(1)} %pad_maximum_fusion.2), channel_id=1, source_target_pairs={{0,4},{4,0},{8,12},{12,8},{16,20},{20,16},{24,28},{28,24},{1,5},{5... | collective-permute-start | bytes 12976136 | tf_op jit(solution)/shard_map/ppermute | solution.py:57
  209.2 39.1 %collective-permute-start.26 = (bf16[384,2048]{1,0:T(8,128)(2,1)S(1)}, bf16[384,2048]{1,0:T(8,128)(2,1)S(1)}, u32[]{:S(2)}, u32[]{:S(2)}) collective-permute-start(bf16[384,2048]{1,0:T(8,128)(2,1)S(1)} %multiply_convert_fusion), channel_id=1, source_target_pairs={{0,1},{1,2},{2,3},{3,0},{4,5},{5,6},{6,7},{7,4},{8,9},{9,10},{10,1... | collective-permute-start | bytes 4718600 | tf_op jit(solution)/shard_map/ppermute | solution.py:102
  214.0 101.1 %collective-permute-start.40 = (bf16[384,2048]{1,0:T(8,128)(2,1)}, bf16[384,2048]{1,0:T(8,128)(2,1)S(1)}, u32[]{:S(2)}, u32[]{:S(2)}) collective-permute-start(bf16[384,2048]{1,0:T(8,128)(2,1)} %collective-permute-done.38), channel_id=1, source_target_pairs={{0,1},{1,2},{2,3},{3,0},{4,5},{5,6},{6,7},{7,4},{8,9},{9,10},{10,1... | collective-permute-start | bytes 4718600 | tf_op jit(solution)/shard_map/ppermute | solution.py:102
  248.3 66.9 %collective-permute-start.32 = (bf16[384,2048]{1,0:T(8,128)(2,1)S(1)}, bf16[384,2048]{1,0:T(8,128)(2,1)S(1)}, u32[]{:S(2)}, u32[]{:S(2)}) collective-permute-start(bf16[384,2048]{1,0:T(8,128)(2,1)S(1)} %collective-permute-done.26), channel_id=1, source_target_pairs={{0,1},{1,2},{2,3},{3,0},{4,5},{5,6},{6,7},{7,4},{8,9},{9,10},{10,1... | collective-permute-start | bytes 4718600 | tf_op jit(solution)/shard_map/ppermute | solution.py:102
  248.9 105.6 %collective-permute-start.30 = (bf16[512,4224]{0,1:T(8,128)(2,1)}, bf16[512,4224]{0,1:T(8,128)(2,1)}, u32[]{:S(2)}, u32[]{:S(2)}) collective-permute-start(bf16[512,4224]{0,1:T(8,128)(2,1)} %collective-permute-done.28), channel_id=1, source_target_pairs={{0,4},{4,0},{8,12},{12,8},{16,20},{20,16},{24,28},{28,24},{1,5},{5... | collective-permute-start | bytes 12976136 | tf_op jit(solution)/shard_map/ppermute | solution.py:57
  315.1 37.7 %collective-permute-start.34 = (bf16[384,2048]{1,0:T(8,128)(2,1)S(1)}, bf16[384,2048]{1,0:T(8,128)(2,1)S(1)}, u32[]{:S(2)}, u32[]{:S(2)}) collective-permute-start(bf16[384,2048]{1,0:T(8,128)(2,1)S(1)} %collective-permute-done.32), channel_id=1, source_target_pairs={{0,1},{1,2},{2,3},{3,0},{4,5},{5,6},{6,7},{7,4},{8,9},{9,10},{10,1... | collective-permute-start | bytes 4718600 | tf_op jit(solution)/shard_map/ppermute | solution.py:102
  555.6 76.0 %collective-permute-start.31 = (bf16[384,2048]{1,0:T(8,128)(2,1)}, bf16[384,2048]{1,0:T(8,128)(2,1)S(1)}, u32[]{:S(2)}, u32[]{:S(2)}) collective-permute-start(bf16[384,2048]{1,0:T(8,128)(2,1)} %convolution_convert_fusion.11), channel_id=1, source_target_pairs={{0,1},{1,2},{2,3},{3,0},{4,5},{5,6},{6,7},{7,4},{8,9},{9,10},{10,1... | collective-permute-start | bytes 4718600 | tf_op jit(solution)/shard_map/ppermute | solution.py:102
  561.2 65.1 %collective-permute-start.37 = (bf16[384,2048]{1,0:T(8,128)(2,1)S(1)}, bf16[384,2048]{1,0:T(8,128)(2,1)S(1)}, u32[]{:S(2)}, u32[]{:S(2)}) collective-permute-start(bf16[384,2048]{1,0:T(8,128)(2,1)S(1)} %add_convert_fusion.9), channel_id=1, source_target_pairs={{0,1},{1,2},{2,3},{3,0},{4,5},{5,6},{6,7},{7,4},{8,9},{9,10},{10,1... | collective-permute-start | bytes 4718600 | tf_op jit(solution)/shard_map/ppermute | solution.py:102
  567.1 143.7 %collective-permute-start.72 = (bf16[512,4224]{1,0:T(8,128)(2,1)S(1)}, bf16[512,4224]{1,0:T(8,128)(2,1)S(1)}, u32[]{:S(2)}, u32[]{:S(2)}) collective-permute-start(bf16[512,4224]{1,0:T(8,128)(2,1)S(1)} %pad_maximum_fusion.5), channel_id=1, source_target_pairs={{0,4},{4,0},{8,12},{12,8},{16,20},{20,16},{24,28},{28,24},{1,5},{5... | collective-permute-start | bytes 12976136 | tf_op jit(solution)/shard_map/ppermute | solution.py:57
  631.5 39.2 %collective-permute-start.39 = (bf16[384,2048]{1,0:T(8,128)(2,1)S(1)}, bf16[384,2048]{1,0:T(8,128)(2,1)S(1)}, u32[]{:S(2)}, u32[]{:S(2)}) collective-permute-start(bf16[384,2048]{1,0:T(8,128)(2,1)S(1)} %add_convert_fusion.7), channel_id=1, source_target_pairs={{0,1},{1,2},{2,3},{3,0},{4,5},{5,6},{6,7},{7,4},{8,9},{9,10},{10,1... | collective-permute-start | bytes 4718600 | tf_op jit(solution)/shard_map/ppermute | solution.py:102
  637.0 67.4 %collective-permute-start.33 = (bf16[384,2048]{1,0:T(8,128)(2,1)S(1)}, bf16[384,2048]{1,0:T(8,128)(2,1)S(1)}, u32[]{:S(2)}, u32[]{:S(2)}) collective-permute-start(bf16[384,2048]{1,0:T(8,128)(2,1)S(1)} %add_convert_fusion.12), channel_id=1, source_target_pairs={{0,1},{1,2},{2,3},{3,0},{4,5},{5,6},{6,7},{7,4},{8,9},{9,10},{10,1... | collective-permute-start | bytes 4718600 | tf_op jit(solution)/shard_map/ppermute | solution.py:102
  641.9 332.5 %collective-permute-start.71 = (bf16[512,4224]{1,0:T(8,128)(2,1)}, bf16[512,4224]{1,0:T(8,128)(2,1)}, u32[]{:S(2)}, u32[]{:S(2)}) collective-permute-start(bf16[512,4224]{1,0:T(8,128)(2,1)} %pad_maximum_fusion.4), channel_id=1, source_target_pairs={{0,4},{4,0},{8,12},{12,8},{16,20},{20,16},{24,28},{28,24},{1,5},{5... | collective-permute-start | bytes 12976136 | tf_op jit(solution)/shard_map/ppermute | solution.py:57
  676.2 62.0 %collective-permute-start.41 = (bf16[384,2048]{1,0:T(8,128)(2,1)S(1)}, bf16[384,2048]{1,0:T(8,128)(2,1)S(1)}, u32[]{:S(2)}, u32[]{:S(2)}) collective-permute-start(bf16[384,2048]{1,0:T(8,128)(2,1)S(1)} %add_convert_fusion.5), channel_id=1, source_target_pairs={{0,1},{1,2},{2,3},{3,0},{4,5},{5,6},{6,7},{7,4},{8,9},{9,10},{10,1... | collective-permute-start | bytes 4718600 | tf_op jit(solution)/shard_map/ppermute | solution.py:102
  710.8 153.3 %collective-permute-start.35 = (bf16[384,2048]{1,0:T(8,128)(2,1)}, bf16[384,2048]{1,0:T(8,128)(2,1)}, u32[]{:S(2)}, u32[]{:S(2)}) collective-permute-start(bf16[384,2048]{1,0:T(8,128)(2,1)} %add_convert_fusion.11), channel_id=1, source_target_pairs={{0,1},{1,2},{2,3},{3,0},{4,5},{5,6},{6,7},{7,4},{8,9},{9,10},{10,1... | collective-permute-start | bytes 4718600 | tf_op jit(solution)/shard_map/ppermute | solution.py:102
  714.1 261.4 %collective-permute-start.73 = (bf16[512,4224]{1,0:T(8,128)(2,1)}, bf16[512,4224]{1,0:T(8,128)(2,1)}, u32[]{:S(2)}, u32[]{:S(2)}) collective-permute-start(bf16[512,4224]{1,0:T(8,128)(2,1)} %add_convert_fusion.1), channel_id=1, source_target_pairs={{0,16},{4,12},{8,24},{12,4},{16,0},{20,28},{24,8},{28,20},{1,17},{... | collective-permute-start | bytes 12976136 | tf_op jit(solution)/shard_map/ppermute | solution.py:53
  930.3 23.5 %collective-permute-start.59 = (bf16[512,1024]{0,1:T(8,128)(2,1)S(1)}, bf16[512,1024]{0,1:T(8,128)(2,1)S(1)}, u32[]{:S(2)}, u32[]{:S(2)}) collective-permute-start(bf16[512,1024]{0,1:T(8,128)(2,1)S(1)} %add_convert_fusion.20), channel_id=1, source_target_pairs={{0,16},{4,12},{8,24},{12,4},{16,0},{20,28},{24,8},{28,20},{1,17},{... | collective-permute-start | bytes 3145736 | tf_op jit(solution)/shard_map/ppermute | solution.py:53
  931.8 23.7 %collective-permute-start.62 = (bf16[512,1024]{0,1:T(8,128)(2,1)S(1)}, bf16[512,1024]{0,1:T(8,128)(2,1)S(1)}, u32[]{:S(2)}, u32[]{:S(2)}) collective-permute-start(bf16[512,1024]{0,1:T(8,128)(2,1)S(1)} %pad_maximum_fusion.12), channel_id=1, source_target_pairs={{0,4},{4,0},{8,12},{12,8},{16,20},{20,16},{24,28},{28,24},{1,5},{5... | collective-permute-start | bytes 3145736 | tf_op jit(solution)/shard_map/ppermute | solution.py:57
  942.6 28.1 %collective-permute-start.64 = (bf16[512,1024]{0,1:T(8,128)(2,1)S(1)}, bf16[512,1024]{0,1:T(8,128)(2,1)S(1)}, u32[]{:S(2)}, u32[]{:S(2)}) collective-permute-start(bf16[512,1024]{0,1:T(8,128)(2,1)S(1)} %add_convert_fusion.17), channel_id=1, source_target_pairs={{0,16},{4,12},{8,24},{12,4},{16,0},{20,28},{24,8},{28,20},{1,17},{... | collective-permute-start | bytes 3145736 | tf_op jit(solution)/shard_map/ppermute | solution.py:53
  953.8 18.5 %collective-permute-start.55 = (bf16[256,1024]{0,1:T(8,128)(2,1)S(1)}, bf16[256,1024]{0,1:T(8,128)(2,1)S(1)}, u32[]{:S(2)}, u32[]{:S(2)}) collective-permute-start(bf16[256,1024]{0,1:T(8,128)(2,1)S(1)} %slice.626), channel_id=1, source_target_pairs={{0,8},{4,20},{8,0},{12,28},{16,24},{20,4},{24,16},{28,12},{1,9},{5... | collective-permute-start | bytes 1572872 | tf_op jit(solution)/shard_map/ppermute | solution.py:53
  955.5 38.9 %collective-permute-start.67 = (bf16[512,1024]{0,1:T(8,128)(2,1)S(1)}, bf16[512,1024]{0,1:T(8,128)(2,1)S(1)}, u32[]{:S(2)}, u32[]{:S(2)}) collective-permute-start(bf16[512,1024]{0,1:T(8,128)(2,1)S(1)} %pad_maximum_fusion.14), channel_id=1, source_target_pairs={{0,4},{4,0},{8,12},{12,8},{16,20},{20,16},{24,28},{28,24},{1,5},{5... | collective-permute-start | bytes 3145736 | tf_op jit(solution)/shard_map/ppermute | solution.py:57
  970.7 20.9 %collective-permute-start.48 = (bf16[256,384]{0,1:T(8,128)(2,1)S(1)}, bf16[256,384]{0,1:T(8,128)(2,1)S(1)}, u32[]{:S(2)}, u32[]{:S(2)}) collective-permute-start(bf16[256,384]{0,1:T(8,128)(2,1)S(1)} %slice.615), channel_id=1, source_target_pairs={{0,8},{4,20},{8,0},{12,28},{16,24},{20,4},{24,16},{28,12},{1,9},{5... | collective-permute-start | bytes 589832 | tf_op jit(solution)/shard_map/ppermute | solution.py:53
  972.3 23.3 %collective-permute-start.69 = (bf16[512,1024]{0,1:T(8,128)(2,1)S(1)}, bf16[512,1024]{0,1:T(8,128)(2,1)S(1)}, u32[]{:S(2)}, u32[]{:S(2)}) collective-permute-start(bf16[512,1024]{0,1:T(8,128)(2,1)S(1)} %add_convert_fusion.14), channel_id=1, source_target_pairs={{0,16},{4,12},{8,24},{12,4},{16,0},{20,28},{24,8},{28,20},{1,17},{... | collective-permute-start | bytes 3145736 | tf_op jit(solution)/shard_map/ppermute | solution.py:53
  990.5 49.3 %collective-permute-start.74 = (bf16[256,4224]{1,0:T(8,128)(2,1)S(1)}, bf16[256,4224]{1,0:T(8,128)(2,1)}, u32[]{:S(2)}, u32[]{:S(2)}) collective-permute-start(bf16[256,4224]{1,0:T(8,128)(2,1)S(1)} %slice.647), channel_id=1, source_target_pairs={{0,8},{4,20},{8,0},{12,28},{16,24},{20,4},{24,16},{28,12},{1,9},{5... | collective-permute-start | bytes 6488072 | tf_op jit(solution)/shard_map/ppermute | solution.py:53
  995.6 37.2 %collective-permute-start.50 = (bf16[256,384]{0,1:T(8,128)(2,1)S(1)}, bf16[256,384]{0,1:T(8,128)(2,1)S(1)}, u32[]{:S(2)}, u32[]{:S(2)}) collective-permute-start(bf16[256,384]{0,1:T(8,128)(2,1)S(1)} %add_convert_fusion.34), channel_id=1, source_target_pairs={{0,2},{1,3},{2,0},{3,1},{4,6},{5,7},{6,4},{7,5},{8,10},{9,11},{10,... | collective-permute-start | bytes 589832 | tf_op jit(solution)/shard_map/ppermute | solution.py:106
  998.8 34.0 %collective-permute-start.49 = (bf16[256,384]{0,1:T(8,128)(2,1)S(1)}, bf16[256,384]{0,1:T(8,128)(2,1)S(1)}, u32[]{:S(2)}, u32[]{:S(2)}) collective-permute-start(bf16[256,384]{0,1:T(8,128)(2,1)S(1)} %add_convert_fusion.34), channel_id=1, source_target_pairs={{0,1},{1,2},{2,3},{3,0},{4,5},{5,6},{6,7},{7,4},{8,9},{9,10},{10,1... | collective-permute-start | bytes 589832 | tf_op jit(solution)/shard_map/ppermute | solution.py:106
  1008.3 28.2 %collective-permute-start.70 = (bf16[256,1024]{0,1:T(8,128)(2,1)}, bf16[256,1024]{0,1:T(8,128)(2,1)}, u32[]{:S(2)}, u32[]{:S(2)}) collective-permute-start(bf16[256,1024]{0,1:T(8,128)(2,1)} %slice.632), channel_id=1, source_target_pairs={{0,8},{4,20},{8,0},{12,28},{16,24},{20,4},{24,16},{28,12},{1,9},{5... | collective-permute-start | bytes 1572872 | tf_op jit(solution)/shard_map/ppermute | solution.py:53
  1010.9 25.6 %collective-permute-start.66 = (bf16[256,1024]{0,1:T(8,128)(2,1)}, bf16[256,1024]{0,1:T(8,128)(2,1)}, u32[]{:S(2)}, u32[]{:S(2)}) collective-permute-start(bf16[256,1024]{0,1:T(8,128)(2,1)} %add_convert_fusion.26), channel_id=1, source_target_pairs={{0,1},{1,2},{2,3},{3,0},{4,5},{5,6},{6,7},{7,4},{8,9},{9,10},{10,1... | collective-permute-start | bytes 1572872 | tf_op jit(solution)/shard_map/ppermute | solution.py:102
  (304 other events, 3025.8 us)

commit v2 on v1

v2 whole, which is shorter than its diff:
```python
import functools

import jax
import jax.numpy as jnp
from jax import lax
from jax.experimental import pallas as pl
from jax.experimental.pallas import tpu as pltpu
from jax.sharding import PartitionSpec as P

HD = 128
norm_eps = 1e-05
F32 = jnp.float32
BF16 = jnp.bfloat16


def dot(left, right, dims):
    return lax.dot_general(left, right, ((dims[0], dims[1]), ((), ())), preferred_element_type=F32)


def nn(left, right):
    return dot(left, right, ((1,), (0,)))


def nt(left, right):
    return dot(left, right, ((1,), (1,)))


def tn(left, right):
    return dot(left, right, ((0,), (0,)))


def lookup(ids, table):
    hits = ids[:, None] == jnp.arange(table.shape[0], dtype=jnp.int32)[None, :]
    return jnp.sum(jnp.where(hits, table[None, :], 0), axis=1)


def norm_back(value, scale, gain, grad):
    weighted = grad * gain
    return scale * weighted - value * (scale * scale * scale) * jnp.mean(
        weighted * value, axis=-1, keepdims=True
    )


def bit_orders(ndp):
    bits = []
    bit = 2
    while bit < ndp:
        bits.append(bit)
        bit *= 2
    return bits, bits[::-1]


def plane_swap(array, ndp, step):
    orders = bit_orders(ndp)
    return lax.ppermute(array, "dp", [(d, d ^ orders[d & 1][step]) for d in range(ndp)])


def core_swap(array, ndp):
    return lax.ppermute(array, "dp", [(d, d ^ 1) for d in range(ndp)])


def slice_table(me, ndp):
    orders = bit_orders(ndp)
    count = len(orders[0])
    table = []
    for place in range(ndp):
        base = me ^ (place // (ndp // 2))
        even = base % 2 == 0
        owner = base
        for step in range(count):
            if (place >> step) & 1:
                owner = owner ^ jnp.where(even, orders[0][step], orders[1][step])
        table.append(owner)
    return table


def gather_steps(shard, ndp):
    moved = yield [plane_swap(shard, ndp, 0)]
    pieces = [jnp.concatenate([shard, moved[0]], axis=0)]
    for step in range(1, len(bit_orders(ndp)[0])):
        pieces = pieces + (yield [plane_swap(piece, ndp, step) for piece in pieces])
    pieces = pieces + (yield [core_swap(piece, ndp) for piece in pieces])
    yield tuple(pieces)


def ring_gather_steps(block, nt_):
    blocks = [block]
    for _ in range(nt_ - 1):
        blocks += yield [ring_next(blocks[-1], nt_)]
    yield tuple(blocks)


def add_low(left, right):
    return (left.astype(F32) + right.astype(F32)).astype(BF16)


def scatter_steps(keep, send, ndp):
    (come,) = yield [core_swap(send, ndp)]
    rows = keep.shape[0] // 2
    low, high = add_low(keep[:rows], come[:rows]), add_low(keep[rows:], come[rows:])
    yield from chip_steps(low, high, ndp)


def chip_steps(low, high, ndp):
    for step in range(len(bit_orders(ndp)[0]) - 1, 0, -1):
        (come,) = yield [plane_swap(high, ndp, step)]
        rows = low.shape[0] // 2
        low, high = add_low(low[:rows], come[:rows]), add_low(low[rows:], come[rows:])
    (come,) = yield [plane_swap(high, ndp, 0)]
    yield (low, come)


def ring_steps(parts, nt_):
    moving = yield [ring_next(parts[1], nt_)]
    for place in range(2, nt_):
        moving = yield [ring_next(add_low(moving[0], parts[place]), nt_)]
    yield (moving[0], parts[0])


class Flow:
    def __init__(self, name, steps):
        self.name, self.steps = name, steps
        with jax.named_scope(name):
            self.held = next(steps)

    def moving(self):
        return isinstance(self.held, list)

    def go(self, times=1):
        for _ in range(times):
            if self.moving():
                with jax.named_scope(self.name):
                    self.held = self.steps.send(self.held)

    def finish(self):
        while self.moving():
            self.go()
        return self.held


def meet(values, flows, others=()):
    going = [flow for flow in flows if flow.moving()]
    flows = going + [flow for flow in others if flow.moving()]
    held = [item for flow in flows for item in flow.held]
    count = len(values)
    tied = list(tie(*values, *held))
    values, held = tied[:count], tied[count:]
    for flow in flows:
        flow.held, held = held[: len(flow.held)], held[len(flow.held) :]
    for flow in going:
        flow.go()
    return values


def ring_next(array, nt_):
    return lax.ppermute(array, "tensor", [(i, (i + 1) % nt_) for i in range(nt_)])


def shift(array, nt_, by):
    return lax.ppermute(array, "tensor", [(i, (i + by) % nt_) for i in range(nt_)])


def stack_rows(pieces):
    return jnp.concatenate(pieces, axis=0)


def scoped(name, function, *items):
    with jax.named_scope(name):
        return function(*items)


def tie(*values):
    return lax.optimization_barrier(values)


LOG2E = 1.4426950408889634
TILE = 512


def params(count=1):
    return pltpu.CompilerParams(
        dimension_semantics=("arbitrary",) * count, vmem_limit_bytes=58 * 1024 * 1024
    )


def whole(array):
    zeros = (0,) * array.ndim
    return pl.BlockSpec(array.shape, lambda *_: zeros, pipeline_mode=pl.Buffered(1))


def move_kernel(table_ref, in_ref, out_ref):
    out_ref[...] = in_ref[...]


def move_columns(array, table, width, back=False):
    tokens = array.shape[0]

    def far(k, table_ref):
        return (0, table_ref[k])

    def near(k, table_ref):
        return (0, k)

    return pl.pallas_call(
        move_kernel,
        out_shape=jax.ShapeDtypeStruct(array.shape, array.dtype),
        grid_spec=pltpu.PrefetchScalarGridSpec(
            num_scalar_prefetch=1,
            grid=(array.shape[1] // width,),
            in_specs=[pl.BlockSpec((tokens, width), near if back else far)],
            out_specs=pl.BlockSpec((tokens, width), far if back else near),
        ),
        cost_estimate=pl.CostEstimate(flops=0, transcendentals=0, bytes_accessed=2 * array.nbytes),
        compiler_params=params(),
        name="put_columns" if back else "take_columns",
    )(jnp.stack(table).astype(jnp.int32), array)


def pack_attn_kernel(query_ref, out_ref, key_ref, value_ref, gains_ref, near_ref, ring_ref):
    heads_w = query_ref.shape[1]
    turned = out_ref[...].T
    for ref in (near_ref, ring_ref):
        ref[:, :heads_w] = query_ref[...]
        ref[:, heads_w : 2 * heads_w] = turned
    for k, ref in enumerate((key_ref, value_ref, gains_ref)):
        near_ref[:, 2 * heads_w + k * HD : 2 * heads_w + (k + 1) * HD] = ref[...]


def pack_attn(w_query, w_out, w_key, w_value, gains):
    rows, heads_w = w_query.shape
    return pl.pallas_call(
        pack_attn_kernel,
        out_shape=(
            jax.ShapeDtypeStruct((rows, 2 * heads_w + 3 * HD), BF16),
            jax.ShapeDtypeStruct((rows, 2 * heads_w), BF16),
        ),
        cost_estimate=pl.CostEstimate(flops=0, transcendentals=0, bytes_accessed=2_000_000),
        compiler_params=params(0),
        name="pack_attn",
    )(w_query, w_out, w_key, w_value, gains)


def plain_pack_attn(w_query, w_out, w_key, w_value, gains):
    ring = jnp.concatenate([w_query, w_out.T], axis=1)
    return jnp.concatenate([ring, w_key, w_value, gains], axis=1), ring


def pack_ffn_kernel(gate_ref, up_ref, down_ref, out_ref):
    units = gate_ref.shape[1]
    for at in range(0, units, TILE):
        size = min(TILE, units - at)
        out_ref[:, 3 * at : 3 * at + size] = gate_ref[:, at : at + size]
        out_ref[:, 3 * at + size : 3 * at + 2 * size] = up_ref[:, at : at + size]
        out_ref[:, 3 * at + 2 * size : 3 * at + 3 * size] = down_ref[at : at + size, :].T


def pack_ffn(w_gate, w_up, w_down):
    rows, units = w_gate.shape
    return pl.pallas_call(
        pack_ffn_kernel,
        out_shape=jax.ShapeDtypeStruct((rows, 3 * units), BF16),
        cost_estimate=pl.CostEstimate(flops=0, transcendentals=0, bytes_accessed=12 * rows * units),
        compiler_params=params(0),
        name="pack_ffn",
    )(w_gate, w_up, w_down)


def plain_pack_ffn(w_gate, w_up, w_down):
    return jnp.concatenate([w_gate, w_up, w_down.T], axis=1)


def enter_kernel(count, tail, table_ref, tokens_ref, *refs):
    key_refs, value_refs, gain_refs = refs[:count], refs[count : 2 * count], refs[2 * count : tail]
    low_ref, normed_ref, turned_ref, kv_ref, gains_ref = refs[tail:]
    rows = key_refs[0].shape[0]
    slices = table_ref.shape[0]
    size = low_ref.shape[1] // slices
    squares = 0.0
    for k in range(slices):
        start = pl.multiple_of(table_ref[k] * size, size)
        block = tokens_ref[:, pl.ds(start, size)]
        low_ref[:, k * size : (k + 1) * size] = block
        block = block.astype(F32)
        squares = squares + jnp.sum(block * block, axis=-1, keepdims=True)
    scale = lax.rsqrt(squares / low_ref.shape[1] + norm_eps)
    kv = 0.0
    for i in range(count):
        part = slice(i * rows, (i + 1) * rows)
        gains = gain_refs[i][...].astype(F32).T
        gains_ref[:, part] = gains[:8]
        normed = (low_ref[:, part].astype(F32) * scale * gains[0:1]).astype(BF16)
        normed_ref[:, part] = normed
        turned_ref[part, :] = normed.T
        weights = jnp.concatenate([key_refs[i][...], value_refs[i][...]], axis=1)
        kv = kv + nn(normed, weights)
    kv_ref[...] = kv.astype(BF16)


def enter(tokens, table, near, at):
    own, width = tokens.shape
    count, rows = len(near), near[0].shape[0]

    def columns(place):
        return [pl.BlockSpec((rows, HD), lambda i, table_ref: (0, at // HD + place))] * count

    def full(shape):
        return pl.BlockSpec(shape, lambda i, table_ref: (0, 0))

    return pl.pallas_call(
        functools.partial(enter_kernel, count, 3 * count),
        out_shape=(
            jax.ShapeDtypeStruct((own, width), BF16),
            jax.ShapeDtypeStruct((own, width), BF16),
            jax.ShapeDtypeStruct((width, own), BF16),
            jax.ShapeDtypeStruct((own, 2 * HD), BF16),
            jax.ShapeDtypeStruct((8, width), F32),
        ),
        grid_spec=pltpu.PrefetchScalarGridSpec(
            num_scalar_prefetch=1,
            grid=(1,),
            in_specs=[full(tokens.shape)] + columns(0) + columns(1) + columns(2),
            out_specs=[full((own, width))] * 2
            + [full((width, own)), full((own, 2 * HD)), full((8, width))],
        ),
        cost_estimate=pl.CostEstimate(
            flops=4 * own * width * HD, transcendentals=0, bytes_accessed=6_000_000
        ),
        compiler_params=params(),
        name="enter",
    )(jnp.stack(table).astype(jnp.int32), tokens, *near, *near, *near)


def plain_enter(tokens, table, near, at):
    rows = tokens.shape[1] // len(table)
    low = move_columns(tokens, table, rows)
    weights = stack_rows([piece[:, at:] for piece in near])
    gains = weights[:, 2 * HD : 2 * HD + 8].astype(F32).T
    value = low.astype(F32)
    scale = lax.rsqrt(jnp.mean(value * value, axis=-1, keepdims=True) + norm_eps)
    normed = (value * scale * gains[0:1]).astype(BF16)
    return low, normed, normed.T, nn(normed, weights[:, : 2 * HD]).astype(BF16), gains


def pair_up(block):
    return jnp.concatenate([block[:, :HD], block[:, HD:]], axis=0)


def pair_off(block):
    tokens = block.shape[0] // 2
    return jnp.concatenate([block[:tokens], block[tokens:]], axis=1)


def attend_kernel(count, blocks, refs):
    normed_ref, bias_ref, acc_ref = refs[:3]
    kv_refs = refs[3 : 3 + blocks]
    wq_refs = refs[3 + blocks : 3 + blocks + count]
    wo_refs = refs[3 + blocks + count : 3 + blocks + 2 * count]
    query_ref, mixed_ref, total_ref, sum_ref, score_ref = refs[3 + blocks + 2 * count :]
    rows = wq_refs[0].shape[0]
    tokens = normed_ref.shape[0]

    query = sum(
        nn(normed_ref[:, i * rows : (i + 1) * rows], wq_refs[i][...]) for i in range(count)
    ).astype(BF16)
    query_ref[...] = query
    query = pair_up(query)
    peak = None
    for b in range(blocks):
        bias = bias_ref[b * tokens : (b + 1) * tokens, :]
        scores = nt(kv_refs[b][:, :HD], query) * (HD ** (-0.5) * LOG2E)
        scores = scores + jnp.concatenate([bias, bias], axis=1)
        score_ref[b] = scores
        top = jnp.max(scores, axis=0, keepdims=True)
        peak = top if peak is None else jnp.maximum(peak, top)
    sums, mixed = 0.0, 0.0
    for b in range(blocks):
        raised = jnp.exp2(score_ref[b] - peak)
        sums = sums + jnp.sum(raised, axis=0, keepdims=True)
        mixed = mixed + tn(kv_refs[b][:, HD:], raised.astype(BF16))
    total_ref[0] = peak + jnp.log2(sums)
    mixed = pair_off((mixed / sums).T.astype(BF16))
    mixed_ref[...] = mixed

    @pl.when(pl.program_id(0) == 0)
    def _():
        sum_ref[...] = acc_ref[...].astype(F32)

    for i in range(count):
        sum_ref[:, i * rows : (i + 1) * rows] += nt(mixed, wo_refs[i][...])


def attend_block(normed, bias, acc, kv_ring, pieces, many):
    tokens, width = normed.shape
    count, blocks = len(pieces), len(kv_ring)
    rows = pieces[0].shape[0]
    pairs = width // blocks // (2 * HD)
    heads_w = many * width // blocks

    def query_at(j):
        return (0, j // pairs * (2 * pairs) + j % pairs)

    def out_at(j):
        return (0, j // pairs * (2 * pairs) + pairs + j % pairs)

    total = blocks * tokens
    flops = 2 * tokens * heads_w * (2 * width + 2 * total)
    return pl.pallas_call(
        lambda *refs: attend_kernel(count, blocks, refs),
        out_shape=(
            jax.ShapeDtypeStruct((tokens, heads_w), BF16),
            jax.ShapeDtypeStruct((tokens, heads_w), BF16),
            jax.ShapeDtypeStruct((many * pairs, 1, 2 * tokens), F32),
            jax.ShapeDtypeStruct((tokens, width), F32),
        ),
        grid=(many * pairs,),
        in_specs=[whole(normed), whole(bias), whole(acc)]
        + [whole(kv) for kv in kv_ring]
        + [pl.BlockSpec((rows, 2 * HD), query_at)] * count
        + [pl.BlockSpec((rows, 2 * HD), out_at)] * count,
        out_specs=(
            pl.BlockSpec((tokens, 2 * HD), lambda j: (0, j)),
            pl.BlockSpec((tokens, 2 * HD), lambda j: (0, j)),
            pl.BlockSpec((1, 1, 2 * tokens), lambda j: (j, 0, 0)),
            pl.BlockSpec((tokens, width), lambda j: (0, 0)),
        ),
        scratch_shapes=[pltpu.VMEM((blocks, tokens, 2 * tokens), F32)],
        cost_estimate=pl.CostEstimate(
            flops=flops, transcendentals=tokens * total * heads_w // HD, bytes_accessed=14_000_000
        ),
        compiler_params=params(),
        name="attend",
    )(normed, bias, acc, *kv_ring, *pieces, *pieces)


def attend_back_kernel(count, blocks, first, refs):
    branch_ref, bias_ref = refs[:2]
    refs = refs[2:]
    if not first:
        kv_in_ref, normed_in_ref = refs[:2]
        refs = refs[2:]
    query_ref, mixed_ref, total_ref = refs[:3]
    refs = refs[3:]
    kv_refs, refs = refs[:blocks], refs[blocks:]
    wq_refs, refs = refs[:count], refs[count:]
    wo_refs, refs = refs[:count], refs[count:]
    query_grad_ref, kv_grad_ref, normed_grad_ref = refs
    rows = wq_refs[0].shape[0]
    tokens = branch_ref.shape[0]
    scale = HD ** (-0.5)

    @pl.when(pl.program_id(0) == 0)
    def _():
        if first:
            kv_grad_ref[...] = jnp.zeros_like(kv_grad_ref)
            normed_grad_ref[...] = jnp.zeros_like(normed_grad_ref)
        else:
            kv_grad_ref[...] = kv_in_ref[...]
            normed_grad_ref[...] = normed_in_ref[...]

    grad = sum(
        nn(branch_ref[:, i * rows : (i + 1) * rows], wo_refs[i][...]) for i in range(count)
    ).astype(BF16)
    product = pair_up(grad.astype(F32) * mixed_ref[...].astype(F32))
    inner = jnp.sum(product.T, axis=0, keepdims=True)
    grad = pair_up(grad)
    query = pair_up(query_ref[...])
    totals = total_ref[0]
    query_grad = 0.0
    for b in range(blocks):
        keys, values = kv_refs[b][:, :HD], kv_refs[b][:, HD:]
        bias = bias_ref[b * tokens : (b + 1) * tokens, :]
        scores = nt(keys, query) * (scale * LOG2E) + jnp.concatenate([bias, bias], axis=1)
        shares = jnp.exp2(scores - totals)
        score_grad = (shares * (nt(values, grad) - inner)).astype(BF16)
        query_grad = query_grad + tn(keys, score_grad)
        at = slice(b * tokens, (b + 1) * tokens)
        kv_grad_ref[at, :HD] += scale * nn(score_grad, query)
        kv_grad_ref[at, HD:] += nn(shares.astype(BF16), grad)
    query_grad = pair_off((scale * query_grad).T.astype(BF16))
    query_grad_ref[...] = query_grad
    for i in range(count):
        normed_grad_ref[:, i * rows : (i + 1) * rows] += nt(query_grad, wq_refs[i][...])


def attend_back_block(branch, bias, sums, query, mixed, total, kv_ring, pieces, at):
    tokens, width = branch.shape
    first = sums is None
    count, blocks = len(pieces), len(kv_ring)
    rows = pieces[0].shape[0]
    heads_w = width // blocks
    pairs = heads_w // (2 * HD)
    base = 2 * pairs * at
    two = pl.BlockSpec((tokens, 2 * HD), lambda j: (0, j))
    kept = pl.BlockSpec((tokens, 2 * HD), lambda j: (0, pairs * at + j))
    sums = [] if first else list(sums)
    keys = blocks * tokens
    return pl.pallas_call(
        lambda *refs: attend_back_kernel(count, blocks, first, refs),
        out_shape=(
            jax.ShapeDtypeStruct((tokens, heads_w), BF16),
            jax.ShapeDtypeStruct((keys, 2 * HD), F32),
            jax.ShapeDtypeStruct((tokens, width), F32),
        ),
        grid=(pairs,),
        in_specs=[whole(branch), whole(bias)]
        + [whole(item) for item in sums]
        + [kept, kept, pl.BlockSpec((1, 1, 2 * tokens), lambda j: (pairs * at + j, 0, 0))]
        + [whole(kv) for kv in kv_ring]
        + [pl.BlockSpec((rows, 2 * HD), lambda j: (0, base + j))] * count
        + [pl.BlockSpec((rows, 2 * HD), lambda j: (0, base + pairs + j))] * count,
        out_specs=(
            two,
            pl.BlockSpec((keys, 2 * HD), lambda j: (0, 0)),
            pl.BlockSpec((tokens, width), lambda j: (0, 0)),
        ),
        cost_estimate=pl.CostEstimate(
            flops=2 * tokens * heads_w * (2 * width + 5 * keys),
            transcendentals=tokens * keys * heads_w // HD,
            bytes_accessed=16_000_000,
        ),
        compiler_params=params(),
        name="attend_back",
    )(branch, bias, *sums, query, mixed, total, *kv_ring, *pieces, *pieces)


def attend_weights_kernel(sends, keeps, refs):
    outs = refs[len(refs) - sends - keeps :]

    def work(normed_ref, branch_ref, query_grad_ref, mixed_ref, out_ref, come_ref):
        half = query_grad_ref.shape[1]
        left = nn(normed_ref[...], query_grad_ref[...])
        right = nn(branch_ref[...], mixed_ref[...])
        if come_ref is not None:
            come = come_ref[...].astype(F32)
            left, right = left + come[:, :half], right + come[:, half:]
        out_ref[:, :half] = left.astype(BF16)
        out_ref[:, half:] = right.astype(BF16)

    if sends:
        work(*refs[:4], outs[0], None)
    if keeps:
        refs = refs[4 * sends :]
        work(*refs[:4], outs[-1], refs[4])


def attend_weights(normed, branch, send=None, keep=None):
    width, tokens = normed.shape
    steps = 4
    rows = width // 2 // steps
    specs, arrays, out_shape = [], [], []
    for item, first in ((send, steps), (keep, 0)):
        if item is None:
            continue
        query_grad, mixed, at, *come = item
        heads_w = query_grad.shape[1]
        left = pl.BlockSpec((rows, tokens), lambda i, first=first: (first + i, 0))
        right = pl.BlockSpec(
            (tokens, heads_w), lambda i, at=at: (0, at), pipeline_mode=pl.Buffered(1)
        )
        out = pl.BlockSpec((rows, 2 * heads_w), lambda i: (i, 0))
        specs += [left, left, whole(query_grad), right] + [out] * len(come)
        arrays += [normed, branch, query_grad, mixed, *come]
        out_shape.append(jax.ShapeDtypeStruct((width // 2, 2 * heads_w), BF16))
    return pl.pallas_call(
        lambda *refs: attend_weights_kernel(int(send is not None), int(keep is not None), refs),
        out_shape=out_shape,
        grid=(steps,),
        in_specs=specs,
        out_specs=[out] * len(out_shape),
        cost_estimate=pl.CostEstimate(
            flops=2 * tokens * width * heads_w * len(out_shape),
            transcendentals=0,
            bytes_accessed=6_000_000,
        ),
        compiler_params=params(),
        name="attend_weights",
    )(*arrays)


def ffn_kernel(count, steps, last, refs):
    normed_ref, grad_ref = refs[:2]
    w_refs = refs[2 : 2 + count]
    act_ref, part_ref, back_ref, part_acc, back_acc = refs[2 + count :]
    rows = w_refs[0].shape[0]
    step = pl.program_id(0)

    @pl.when(step == 0)
    def _():
        part_acc[...] = jnp.zeros_like(part_acc)
        back_acc[...] = jnp.zeros_like(back_acc)

    def work(tile):
        parts = [slice(i * rows, (i + 1) * rows) for i in range(count)]
        gate = sum(nn(normed_ref[:, p], w[:, :tile]) for p, w in zip(parts, w_refs))
        upward = sum(nn(normed_ref[:, p], w[:, tile : 2 * tile]) for p, w in zip(parts, w_refs))
        hidden_grad = sum(
            nn(grad_ref[:, p], w[:, 2 * tile : 3 * tile]) for p, w in zip(parts, w_refs)
        )
        sigma = jax.nn.sigmoid(gate)
        silu = gate * sigma
        hidden = (silu * upward).astype(BF16)
        up_grad = (hidden_grad * silu).astype(BF16)
        gate_grad = (hidden_grad * upward * sigma * (1.0 + gate * (1.0 - sigma))).astype(BF16)
        act_ref[:, :tile] = gate_grad
        act_ref[:, tile : 2 * tile] = up_grad
        act_ref[:, 2 * tile : 3 * tile] = hidden
        both = jnp.concatenate([gate_grad, up_grad], axis=1)
        for p, w in zip(parts, w_refs):
            part_acc[:, p] += nt(hidden, w[:, 2 * tile : 3 * tile])
            back_acc[:, p] += nt(both, w[:, : 2 * tile])

    if steps > 1:
        pl.when(step < steps - 1)(lambda: work(TILE))
    pl.when(step == steps - 1)(lambda: work(last))

    @pl.when(step == steps - 1)
    def _():
        part_ref[...] = part_acc[...].astype(BF16)
        back_ref[...] = back_acc[...].astype(BF16)


def ffn_block(normed, grad, pieces):
    tokens, width = normed.shape
    count, rows = len(pieces), pieces[0].shape[0]
    units = pieces[0].shape[1] // 3
    steps = -(-units // TILE)
    last = units - (steps - 1) * TILE
    full = pl.BlockSpec((tokens, width), lambda j: (0, 0))
    out = jax.ShapeDtypeStruct((tokens, width), BF16)
    return pl.pallas_call(
        lambda *refs: ffn_kernel(count, steps, last, refs),
        out_shape=(jax.ShapeDtypeStruct((tokens, 3 * units), BF16), out, out),
        grid=(steps,),
        in_specs=[whole(normed), whole(grad)]
        + [pl.BlockSpec((rows, 3 * TILE), lambda j: (0, j))] * count,
        out_specs=(pl.BlockSpec((tokens, 3 * TILE), lambda j: (0, j)), full, full),
        scratch_shapes=[pltpu.VMEM((tokens, width), F32)] * 2,
        cost_estimate=pl.CostEstimate(
            flops=12 * tokens * width * units,
            transcendentals=tokens * units,
            bytes_accessed=6 * width * units + 12 * tokens * width,
        ),
        compiler_params=params(),
        name="ffn_block",
    )(normed, grad, *pieces)


def ffn_weights_kernel(blocks, count, steps, last, adds, refs):
    normed_refs, refs = refs[:blocks], refs[blocks:]
    grad_refs, refs = refs[:blocks], refs[blocks:]
    act_refs, refs = refs[:blocks], refs[blocks:]
    added_refs, out_refs = refs[: adds * count], refs[adds * count :]

    def work(piece, tile):
        both = sum(tn(normed_refs[b][...], act_refs[b][:, : 2 * tile]) for b in range(blocks))
        down = sum(
            tn(grad_refs[b][...], act_refs[b][:, 2 * tile : 3 * tile]) for b in range(blocks)
        )
        for k in range(adds):
            added = added_refs[k * count + piece]
            both = both + added[:, : 2 * tile].astype(F32)
            down = down + added[:, 2 * tile : 3 * tile].astype(F32)
        out_refs[piece][:, : 2 * tile] = both.astype(BF16)
        out_refs[piece][:, 2 * tile : 3 * tile] = down.astype(BF16)

    turn, step = pl.program_id(0), pl.program_id(1)
    for at in range(count):
        if steps > 1:
            pl.when((turn == at) & (step < steps - 1))(functools.partial(work, at, TILE))
        pl.when((turn == at) & (step == steps - 1))(functools.partial(work, at, last))


def ffn_weights(normed_ring, grad_ring, acts, first, count, rows, added=()):
    tokens = normed_ring[0].shape[0]
    units = acts[0].shape[1] // 3
    blocks = len(acts)
    steps = -(-units // TILE)
    last = units - (steps - 1) * TILE
    left = pl.BlockSpec((tokens, rows), lambda i, j: (0, first + i))

    def piece_spec(piece, block):
        def place(i, j):
            return (block, jnp.where(i < piece, 0, jnp.where(i > piece, steps - 1, j)))

        return pl.BlockSpec((rows, 3 * TILE), place)

    wide = [piece_spec(piece, 0) for piece in range(count)]
    specs, arrays = [], []
    for item in added:
        if isinstance(item, (list, tuple)):
            specs, arrays = specs + wide, arrays + list(item)
        else:
            specs = specs + [piece_spec(piece, piece) for piece in range(count)]
            arrays = arrays + [item] * count
    return pl.pallas_call(
        lambda *refs: ffn_weights_kernel(blocks, count, steps, last, len(added), refs),
        out_shape=[jax.ShapeDtypeStruct((rows, 3 * units), BF16)] * count,
        grid=(count, steps),
        in_specs=[left] * (2 * blocks)
        + [pl.BlockSpec((tokens, 3 * TILE), lambda i, j: (0, j))] * blocks
        + specs,
        out_specs=wide,
        cost_estimate=pl.CostEstimate(
            flops=6 * tokens * blocks * count * rows * units,
            transcendentals=0,
            bytes_accessed=6 * tokens * blocks * units * count + 6 * count * rows * units,
        ),
        compiler_params=params(2),
        name="ffn_weights",
    )(*normed_ring, *grad_ring, *acts, *arrays)


def turn_kernel(come_ref, part_ref, given_ref, value_ref, gain_ref, *refs):
    after_ref, low_ref, turned_ref, term_ref = refs
    value = value_ref[...]
    grad = come_ref[...].astype(F32) + part_ref[...].astype(F32)
    scale = lax.rsqrt(jnp.mean(value * value, axis=-1, keepdims=True) + norm_eps)
    term_ref[...] = jnp.sum(grad * value * scale, axis=0, keepdims=True)
    after = given_ref[...].astype(F32) + norm_back(value, scale, gain_ref[1:2, :], grad)
    after_ref[...] = after
    low = after.astype(BF16)
    low_ref[...] = low
    turned_ref[...] = low.T


def turn(come, part, given, value, gains):
    own, width = value.shape
    return pl.pallas_call(
        turn_kernel,
        out_shape=(
            jax.ShapeDtypeStruct((own, width), F32),
            jax.ShapeDtypeStruct((own, width), BF16),
            jax.ShapeDtypeStruct((width, own), BF16),
            jax.ShapeDtypeStruct((1, width), F32),
        ),
        cost_estimate=pl.CostEstimate(
            flops=0, transcendentals=0, bytes_accessed=20 * own * width
        ),
        compiler_params=params(0),
        name="turn",
    )(come, part, given, value, gains)


def plain_turn(come, part, given, value, gains):
    grad = come.astype(F32) + part.astype(F32)
    scale = lax.rsqrt(jnp.mean(value * value, axis=-1, keepdims=True) + norm_eps)
    term = jnp.sum(grad * value * scale, axis=0, keepdims=True)
    after = given.astype(F32) + norm_back(value, scale, gains[1:2], grad)
    low = after.astype(BF16)
    return after, low, low.T, term


def leave_kernel(come_count, count, slices, table_ref, *refs):
    kv_ref, refs = refs[0], refs[1:]
    come_refs, refs = refs[:come_count], refs[come_count:]
    d_key_ref, d_value_ref, grad_ref, normed_ref, low_ref, after_ref, gain_ref, ffn_ref = refs[:8]
    refs = refs[8:]
    key_refs, value_refs, refs = refs[:count], refs[count : 2 * count], refs[2 * count :]
    out_ref, keep_ref, send_ref, total_ref = refs
    rows = key_refs[0].shape[0]
    width = low_ref.shape[1]
    size = width // slices
    kv_grad = kv_ref[...]
    for ref in come_refs:
        kv_grad = kv_grad + ref[...].astype(F32)
    given = jnp.concatenate([d_key_ref[...], d_value_ref[...]], axis=1)
    kv_grad = (kv_grad + given.astype(F32)).astype(BF16)
    squares, inner = 0.0, 0.0
    for i in range(count):
        part = slice(i * rows, (i + 1) * rows)
        weights = jnp.concatenate([key_refs[i][...], value_refs[i][...]], axis=1)
        total = grad_ref[:, part] + nt(kv_grad, weights)
        total_ref[:, part] = total
        value = low_ref[:, part].astype(F32)
        squares = squares + jnp.sum(value * value, axis=-1, keepdims=True)
        inner = inner + jnp.sum(total * gain_ref[0:1, part] * value, axis=-1, keepdims=True)
    scale = lax.rsqrt(squares / width + norm_eps)
    shrink = scale * scale * scale * (inner / width)
    for i in range(count):
        part = slice(i * rows, (i + 1) * rows)
        total, value = total_ref[:, part], low_ref[:, part].astype(F32)
        gain_term = jnp.sum(total * value * scale, axis=0, keepdims=True)
        terms = jnp.concatenate(
            [gain_term, ffn_ref[:, part], jnp.zeros((HD - 2, rows), F32)], axis=0
        )
        block = jnp.concatenate([tn(normed_ref[:, part], kv_grad), terms.T], axis=1).astype(BF16)
        half = count // 2
        ref = keep_ref if i < half else send_ref
        ref[(i % half) * rows : (i % half + 1) * rows, :] = block
    for k in range(slices):
        part = slice(k * size, (k + 1) * size)
        value = low_ref[:, part].astype(F32)
        grad = scale * (total_ref[:, part] * gain_ref[0:1, part]) - value * shrink
        start = pl.multiple_of(table_ref[k] * size, size)
        out_ref[:, pl.ds(start, size)] = after_ref[:, part] + grad


def leave(table, kv_acc, kv_come, d_keys, d_values, normed_grad, normed, low, after_grad, gains,
          ffn_term, near, at):
    own, width = normed.shape
    count, rows = len(near), near[0].shape[0]

    def columns(place):
        return [pl.BlockSpec((rows, HD), lambda i, table_ref: (0, at // HD + place))] * count

    def full(shape):
        return pl.BlockSpec(shape, lambda i, table_ref: (0, 0))

    given = [*kv_come, d_keys, d_values, normed_grad, normed, low, after_grad, gains, ffn_term]
    half = jax.ShapeDtypeStruct((width // 2, 3 * HD), BF16)
    return pl.pallas_call(
        functools.partial(leave_kernel, len(kv_come), count, len(table)),
        out_shape=(jax.ShapeDtypeStruct((own, width), F32), half, half),
        grid_spec=pltpu.PrefetchScalarGridSpec(
            num_scalar_prefetch=1,
            grid=(1,),
            in_specs=[full((own, 2 * HD))]
            + [full(item.shape) for item in given]
            + columns(0)
            + columns(1),
            out_specs=[full((own, width)), full(half.shape), full(half.shape)],
            scratch_shapes=[pltpu.VMEM((own, width), F32)],
        ),
        cost_estimate=pl.CostEstimate(
            flops=8 * own * width * HD, transcendentals=0, bytes_accessed=16_000_000
        ),
        compiler_params=params(),
        name="leave",
    )(jnp.stack(table).astype(jnp.int32), kv_acc, *given, *near, *near)


def leave_out_kernel(slices, table_ref, after_ref, come_ref, part_ref, out_ref):
    size = after_ref.shape[1] // slices
    for k in range(slices):
        part = slice(k * size, (k + 1) * size)
        total = come_ref[:, part].astype(F32) + part_ref[:, part].astype(F32)
        start = pl.multiple_of(table_ref[k] * size, size)
        out_ref[:, pl.ds(start, size)] = (after_ref[:, part] + total).astype(BF16)


def leave_out(table, after_attn, come, part):
    def full(shape):
        return pl.BlockSpec(shape, lambda i, table_ref: (0, 0))

    return pl.pallas_call(
        functools.partial(leave_out_kernel, len(table)),
        out_shape=jax.ShapeDtypeStruct(after_attn.shape, BF16),
        grid_spec=pltpu.PrefetchScalarGridSpec(
            num_scalar_prefetch=1,
            grid=(1,),
            in_specs=[full(after_attn.shape)] * 3,
            out_specs=full(after_attn.shape),
        ),
        cost_estimate=pl.CostEstimate(flops=0, transcendentals=0, bytes_accessed=8_000_000),
        compiler_params=params(),
        name="leave_out",
    )(jnp.stack(table).astype(jnp.int32), after_attn, come, part)


def unpack_ffn_kernel(keep_ref, come_ref, gate_ref, up_ref, down_ref):
    units = gate_ref.shape[1]
    for at in range(0, units, TILE):
        size = min(TILE, units - at)

        def take(k):
            cols = slice(3 * at + k * size, 3 * at + (k + 1) * size)
            return keep_ref[:, cols].astype(F32) + come_ref[:, cols].astype(F32)

        gate_ref[:, at : at + size] = take(0)
        up_ref[:, at : at + size] = take(1)
        down_ref[at : at + size, :] = take(2).T


def unpack_ffn(keep, come):
    rows, units = keep.shape[0], keep.shape[1] // 3
    flat = jax.ShapeDtypeStruct((rows, units), F32)
    return pl.pallas_call(
        unpack_ffn_kernel,
        out_shape=(flat, flat, jax.ShapeDtypeStruct((units, rows), F32)),
        cost_estimate=pl.CostEstimate(flops=0, transcendentals=0, bytes_accessed=24 * rows * units),
        compiler_params=params(0),
        name="unpack_ffn",
    )(keep, come)


def unpack_attn_kernel(moving_ref, keep_ref, come_ref, query_ref, out_ref):
    heads_w = query_ref.shape[1]
    total = keep_ref[...].astype(F32) + come_ref[...].astype(F32) + moving_ref[...].astype(F32)
    query_ref[...] = total[:, :heads_w]
    out_ref[...] = total[:, heads_w:].T


def unpack_attn(moving, keep, come):
    rows, heads_w = keep.shape[0], keep.shape[1] // 2
    return pl.pallas_call(
        unpack_attn_kernel,
        out_shape=(
            jax.ShapeDtypeStruct((rows, heads_w), F32),
            jax.ShapeDtypeStruct((heads_w, rows), F32),
        ),
        cost_estimate=pl.CostEstimate(flops=0, transcendentals=0, bytes_accessed=4_000_000),
        compiler_params=params(0),
        name="unpack_attn",
    )(moving, keep, come)


def place_kv_kernel(count, place_ref, *refs):
    kv_refs, (key_ref, value_ref) = refs[:count], refs[count:]
    own = kv_refs[0].shape[0]
    for r in range(count):
        start = pl.multiple_of(place_ref[r] * own, own)
        key_ref[pl.ds(start, own), :] = kv_refs[r][:, :HD]
        value_ref[pl.ds(start, own), :] = kv_refs[r][:, HD:]


def place_kv(places, kv_ring):
    own, count = kv_ring[0].shape[0], len(kv_ring)
    out = jax.ShapeDtypeStruct((count * own, HD), BF16)
    return pl.pallas_call(
        functools.partial(place_kv_kernel, count),
        out_shape=(out, out),
        grid_spec=pltpu.PrefetchScalarGridSpec(
            num_scalar_prefetch=1,
            grid=(1,),
            in_specs=[pl.BlockSpec((own, 2 * HD), lambda i, place_ref: (0, 0))] * count,
            out_specs=[pl.BlockSpec(out.shape, lambda i, place_ref: (0, 0))] * 2,
        ),
        cost_estimate=pl.CostEstimate(flops=0, transcendentals=0, bytes_accessed=1_600_000),
        compiler_params=params(),
        name="place_kv",
    )(jnp.stack(places).astype(jnp.int32), *kv_ring)


def plain_attend_block(normed, bias, acc, kv_ring, pieces, many):
    step = normed.shape[1] // len(kv_ring)
    heads_w = many * step
    weights = stack_rows(pieces)
    blocks = [weights[:, at * step : (at + 1) * step] for at in range(2 * many)]
    weights = jnp.concatenate(blocks[::2] + blocks[1::2], axis=1)
    kv = stack_rows(kv_ring)
    query = nn(normed, weights[:, :heads_w]).astype(BF16)
    mixed, totals = [], []
    for head in range(heads_w // HD):
        scores = nt(kv[:, :HD], query[:, head * HD : (head + 1) * HD]) * (HD ** (-0.5)) + bias
        peak = jnp.max(scores, axis=0, keepdims=True)
        raised = jnp.exp(scores - peak)
        sums = jnp.sum(raised, axis=0, keepdims=True)
        mixed.append(tn((raised / sums).astype(BF16), kv[:, HD:]).astype(BF16))
        totals.append(peak + jnp.log(sums))
    mixed = jnp.concatenate(mixed, axis=1)
    return query, mixed, jnp.concatenate(totals, axis=0), acc + nt(mixed, weights[:, heads_w:])


def plain_attend_back_block(branch, bias, sums, query, mixed, total, kv_ring, pieces, at):
    heads_w = branch.shape[1] // len(kv_ring)
    weights = stack_rows(pieces)[:, 2 * at * heads_w : 2 * (at + 1) * heads_w]
    query = query[:, at * heads_w : (at + 1) * heads_w]
    total = total[at * heads_w // HD : (at + 1) * heads_w // HD]
    kv = stack_rows(kv_ring)
    keys, values = kv[:, :HD], kv[:, HD:]
    scale = HD ** (-0.5)
    grad = nn(branch, weights[:, heads_w:]).astype(BF16)
    key_acc, value_acc, query_grad = 0.0, 0.0, []
    for head in range(heads_w // HD):
        cols = slice(head * HD, (head + 1) * HD)
        scores = nt(keys, query[:, cols]) * scale + bias
        shares = jnp.exp(scores - total[head : head + 1])
        share_grad = nt(values, grad[:, cols])
        value_acc = value_acc + nn(shares.astype(BF16), grad[:, cols])
        inner = jnp.sum(shares * share_grad, axis=0, keepdims=True)
        score_grad = (shares * (share_grad - inner)).astype(BF16)
        query_grad.append((scale * tn(score_grad, keys)).astype(BF16))
        key_acc = key_acc + scale * nn(score_grad, query[:, cols])
    query_grad = jnp.concatenate(query_grad, axis=1)
    kv_grad = jnp.concatenate([key_acc, value_acc], axis=1)
    normed_grad = nt(query_grad, weights[:, :heads_w])
    if sums is not None:
        kv_grad, normed_grad = kv_grad + sums[0], normed_grad + sums[1]
    return query_grad, kv_grad, normed_grad


def plain_attend_weights(normed, branch, send=None, keep=None):
    half = normed.shape[0] // 2
    outs = []
    for item, first in ((send, half), (keep, 0)):
        if item is None:
            continue
        query_grad, mixed, at, *come = item
        heads_w = query_grad.shape[1]
        mixed = mixed[:, at * heads_w : (at + 1) * heads_w]
        part = slice(first, first + half)
        out = jnp.concatenate([nn(normed[part], query_grad), nn(branch[part], mixed)], axis=1)
        outs.append((out + come[0].astype(F32) if come else out).astype(BF16))
    return outs


def plain_ffn_block(normed, grad, pieces):
    weights = stack_rows(pieces)
    units = weights.shape[1] // 3
    gate_w, up_w, down_w = jnp.split(weights, 3, axis=1)
    gate = nn(normed, gate_w)
    upward = nn(normed, up_w)
    sigma = jax.nn.sigmoid(gate)
    hidden = (gate * sigma * upward).astype(BF16)
    part = nt(hidden, down_w).astype(BF16)
    hidden_grad = nn(grad, down_w)
    gate_grad = (hidden_grad * upward * sigma * (1.0 + gate * (1.0 - sigma))).astype(BF16)
    up_grad = (hidden_grad * gate * sigma).astype(BF16)
    back = (nt(gate_grad, gate_w) + nt(up_grad, up_w)).astype(BF16)
    return jnp.concatenate([gate_grad, up_grad, hidden], axis=1), part, back


def plain_ffn_weights(normed_ring, grad_ring, acts, first, count, rows, added=()):
    normed, grad, acts = stack_rows(normed_ring), stack_rows(grad_ring), stack_rows(acts)
    units = acts.shape[1] // 3
    pieces = []
    for piece in range(count):
        cols = slice((first + piece) * rows, (first + piece + 1) * rows)
        out = [tn(normed[:, cols], acts[:, : 2 * units]), tn(grad[:, cols], acts[:, 2 * units :])]
        out = jnp.concatenate(out, axis=1)
        for item in added:
            single = isinstance(item, (list, tuple))
            out = out + (item[piece] if single else item[piece * rows :][:rows]).astype(F32)
        pieces.append(out.astype(BF16))
    return pieces


def plain_leave(table, kv_acc, kv_come, d_keys, d_values, normed_grad, normed, low, after_grad,
                gains, ffn_term, near, at):
    own, width = normed.shape
    kv_grad = kv_acc[:own]
    for come in kv_come:
        kv_grad = kv_grad + come.astype(F32)
    kv_grad = kv_grad + jnp.concatenate([d_keys, d_values], axis=1).astype(F32)
    kv_grad = kv_grad.astype(BF16)
    kv_w = stack_rows([piece[:, at : at + 2 * HD] for piece in near])
    normed_grad = normed_grad + nt(kv_grad, kv_w)
    value = low.astype(F32)
    scale = lax.rsqrt(jnp.mean(value * value, axis=-1, keepdims=True) + norm_eps)
    grad = after_grad + norm_back(value, scale, gains[0:1], normed_grad)
    gain_term = jnp.sum(normed_grad * value * scale, axis=0)
    small = [tn(normed, kv_grad), gain_term[:, None], ffn_term.T, jnp.zeros((width, HD - 2), F32)]
    small = jnp.concatenate(small, axis=1).astype(BF16)
    grad = move_columns(grad, table, width // len(table), back=True)
    return grad, small[: width // 2], small[width // 2 :]


def plain_leave_out(table, after_attn, come, part):
    out = (after_attn + (come.astype(F32) + part.astype(F32))).astype(BF16)
    return move_columns(out, table, out.shape[1] // len(table), back=True)


def plain_unpack_ffn(keep, come):
    gate, up, down = jnp.split(keep.astype(F32) + come.astype(F32), 3, axis=1)
    return gate, up, down.T


def plain_unpack_attn(moving, keep, come):
    total = keep.astype(F32) + come.astype(F32) + moving.astype(F32)
    heads_w = total.shape[1] // 2
    return total[:, :heads_w], total[:, heads_w:].T


def plain_place_kv(places, kv_ring):
    own = kv_ring[0].shape[0]
    out = jnp.zeros((len(kv_ring) * own, 2 * HD), BF16)
    for start, block in zip(places, kv_ring):
        out = lax.dynamic_update_slice_in_dim(out, block, start * own, axis=0)
    return out[:, :HD], out[:, HD:]


KERNELS = (
    pack_attn,
    pack_ffn,
    enter,
    attend_block,
    attend_back_block,
    attend_weights,
    ffn_block,
    ffn_weights,
    turn,
    leave,
    leave_out,
    unpack_ffn,
    unpack_attn,
    place_kv,
)
PLAIN = (
    plain_pack_attn,
    plain_pack_ffn,
    plain_enter,
    plain_attend_block,
    plain_attend_back_block,
    plain_attend_weights,
    plain_ffn_block,
    plain_ffn_weights,
    plain_turn,
    plain_leave,
    plain_leave_out,
    plain_unpack_ffn,
    plain_unpack_attn,
    plain_place_kv,
)


def on_device(
    ndp,
    nz,
    tokens,
    norm_attn,
    w_query,
    w_key,
    w_value,
    w_out,
    norm_ffn,
    w_gate,
    w_up,
    w_down,
    segment_ids,
    parents,
    positions,
    d_out,
    d_keys,
    d_values,
):
    me = lax.axis_index("dp")
    place_z = lax.axis_index("tensor")
    table = slice_table(me, ndp)
    own, width = tokens.shape[0], tokens.shape[1]
    rows = width // ndp
    heads_w = w_query.shape[1]
    units = w_gate.shape[1]
    fits = own % HD == 0 and rows % HD == 0 and units % HD == 0 and heads_w % (2 * HD) == 0
    (
        do_pack_attn,
        do_pack_ffn,
        do_enter,
        do_attend,
        do_attend_back,
        do_attend_weights,
        do_ffn,
        do_ffn_weights,
        do_turn,
        do_leave,
        do_leave_out,
        do_unpack_ffn,
        do_unpack_attn,
        do_place_kv,
    ) = KERNELS if fits else PLAIN

    gains = jnp.concatenate(
        [norm_attn[:, None], norm_ffn[:, None], jnp.zeros((rows, HD - 2), BF16)], axis=1
    )
    first_up = lookup(segment_ids, parents)
    second_up = lookup(first_up, parents)

    def own_rows(vector):
        return lax.dynamic_slice_in_dim(vector, place_z * own, own, axis=0)

    def ring_rows(vector):
        return jnp.concatenate(
            [
                lax.dynamic_slice_in_dim(vector, ((place_z - r) % nz) * own, own, axis=0)
                for r in range(nz)
            ],
            axis=0,
        )

    key_segment, key_place = ring_rows(segment_ids)[:, None], ring_rows(positions)[:, None]
    linked = (
        (key_segment == own_rows(segment_ids)[None])
        | (key_segment == own_rows(first_up)[None])
        | (key_segment == own_rows(second_up)[None])
    )
    bias = jnp.where(linked & (key_place <= own_rows(positions)[None]), 0.0, -1e30).astype(F32)

    near_item, ring_item = do_pack_attn(w_query, w_out, w_key, w_value, gains)
    near_flow = Flow("attn_w_near", gather_steps(near_item, ndp))
    attn_flow = Flow("attn_w_ring", ring_gather_steps(ring_item, nz))
    grad_low = move_columns(d_out, table, rows)
    (ring_item,) = meet([ring_item], [near_flow, attn_flow])
    near_flow.go(len(bit_orders(ndp)[0]) - 2)
    ffn_pack = do_pack_ffn(w_gate, w_up, w_down)
    grad_low, bias, ffn_pack = meet([grad_low, bias, ffn_pack], [near_flow, attn_flow])
    ffn_flow = Flow("ffn_w", gather_steps(ffn_pack, ndp))
    near = list(near_flow.finish())
    near = meet(near, [attn_flow])
    tokens_low, normed, normed_turned, kv_own, gain_rows = do_enter(
        tokens, table, near, 2 * heads_w
    )
    ffn_gain = gain_rows[1:2]
    kv_ring = [kv_own] + [scoped("kv", shift, kv_own, nz, by) for by in range(1, nz)]
    *kv_ring, grad_low = meet(kv_ring + [grad_low], [attn_flow])
    attn_ring = attn_flow.finish()[1:]
    far_flow = Flow("attn_w_far", gather_steps(jnp.concatenate(attn_ring, axis=1), ndp))
    grad_flow = Flow("grad_ring", ring_gather_steps(grad_low, nz))

    normed, *kv_ring = meet([normed] + kv_ring, [far_flow], [ffn_flow])
    *kept_near, after_attn = do_attend(normed, bias, tokens_low, kv_ring, near, 1)
    grad_first = grad_flow.held[0]
    (after_attn,) = meet([after_attn], [grad_flow])
    (after_attn,) = meet([after_attn], [far_flow, ffn_flow])
    far = far_flow.finish()
    *kept_far, after_attn = do_attend(normed, bias, after_attn, kv_ring, far, nz - 1)
    (after_attn,) = meet([after_attn], [ffn_flow, grad_flow])
    ffn_w = ffn_flow.finish()
    grad_ring = [grad_low, grad_first]
    ffn_scale = lax.rsqrt(jnp.mean(after_attn * after_attn, axis=-1, keepdims=True) + norm_eps)
    ffn_own = (after_attn * ffn_scale * ffn_gain).astype(BF16)

    ring_flow = Flow("ffn_ring", ring_gather_steps(ffn_own, nz))
    ffn_ring, acts, parts, backs = [ffn_own], [], [], []
    early = nz // 2 + 1
    backs_flow = None
    for block in range(nz):
        if block > 0:
            come, acts[-1], *ring_flow.held = tie(ring_flow.held[0], acts[-1])
            ring_flow.held = [come]
            ring_flow.go()
            ffn_ring.append(come)
            if block == 2:
                (ffn_ring[-1],) = meet(ffn_ring[-1:], [], [grad_flow])
                grad_ring = grad_flow.finish()
        if block == early:
            first = (ffn_ring[:early], grad_ring[:early], acts[:early])
            (send,) = do_ffn_weights(*first, 1, 1, width // 2)
            kept = do_ffn_weights(*first, 0, 2, width // 4)
            (send,) = meet([send], [backs_flow] if block > 2 else [])
            ffn_ring[-1], send, *kept = tie(ffn_ring[-1], send, *kept)
        elif block > 2:
            (ffn_ring[-1],) = meet(ffn_ring[-1:], [backs_flow])
        act, part, back = do_ffn(ffn_ring[block], grad_ring[block], ffn_w)
        acts.append(act)
        parts.append(part)
        backs.append(back)
        if block == 1:
            backs_flow = Flow("backs", ring_steps(backs, nz))

    (acts[-1],) = meet([acts[-1]], [backs_flow])
    rest = (ffn_ring[early:], grad_ring[early:], acts[early:])
    (send,) = do_ffn_weights(*rest, 1, 1, width // 2, ([send],))
    come = scoped("ffn_g", core_swap, send, ndp)
    made = do_ffn_weights(*rest, 0, 2, width // 4, (kept, come))
    parts[1], *made = meet([parts[1], *made], [backs_flow])
    after_grad, branch, branch_turned, ffn_term = do_turn(
        *backs_flow.finish(), grad_low, after_attn, gain_rows
    )
    part_flow = Flow("parts", ring_steps(parts, nz))
    ffn_flow = Flow("ffn_g", chip_steps(*made, ndp))

    order = list(range(1, nz)) + [0]
    flows = [None] * nz
    sums = None
    for turn, block in enumerate(order):
        stored, pieces, at = (kept_far, far, block - 1) if block else (kept_near, near, 0)
        if turn > 0:
            branch, *made = meet([branch, *made], [part_flow] + [ffn_flow] * (turn == 1))
            sent = scoped(f"attn_g_{order[turn - 1]}", core_swap, made[0], ndp)
            if turn > 1:
                flow = Flow(f"attn_g_{order[turn - 2]}", chip_steps(*made[1:], ndp))
                flows[order[turn - 2]] = flow
        query_grad, kv_acc, normed_grad = do_attend_back(
            branch, bias, sums, *stored, kv_ring, pieces, at
        )
        sums = (kv_acc, normed_grad)
        due = [flow for flow in flows if flow is not None]
        if turn == 1:
            due.append(ffn_flow)
        if turn == nz - 1:
            due.remove(flow)
        this = (query_grad, stored[1], at)
        if turn == 0:
            made = do_attend_weights(normed_turned, branch_turned, this)
        else:
            query_grad, sent = meet([query_grad, sent], due)
            this = (query_grad, stored[1], at)
            made, both = do_attend_weights(normed_turned, branch_turned, this, (*back, sent))
            made = [made, both[: width // 4], both[width // 4 :]]
        back = this
    kv_low = kv_acc.astype(BF16)
    kv_come = [
        scoped("kv_g", shift, kv_low[by * own : (by + 1) * own], nz, -by) for by in range(1, nz)
    ]
    done = [None] * nz
    for place in range(1, nz - 2):
        done[place] = add_low(*flows[place].finish())
    ring_flow = Flow("attn_g_ring", ring_steps(done, nz))
    for _ in range(nz - 4):
        ring_flow.go()
    tied = meet([*made, *kv_come], [flows[nz - 2], part_flow], [ring_flow])
    (send, *made), kv_come = tied[:3], tied[3:]
    sent = scoped("attn_g_0", core_swap, send, ndp)
    flows[nz - 1] = Flow(f"attn_g_{nz - 1}", chip_steps(*made, ndp))
    input_grad, keep, send = do_leave(
        table,
        kv_acc,
        kv_come,
        d_keys,
        d_values,
        normed_grad,
        normed,
        tokens_low,
        after_grad,
        gain_rows,
        ffn_term,
        near,
        2 * heads_w,
    )
    keep, send, sent = meet([keep, send, sent], [flows[nz - 2], flows[nz - 1]])
    done[nz - 2] = add_low(*flows[nz - 2].finish())
    small_flow = Flow("small_g", scatter_steps(keep, send, ndp))
    (done[nz - 2],) = meet([done[nz - 2]], [ring_flow])
    (both,) = do_attend_weights(normed_turned, branch_turned, None, (*back, sent))
    flows[0] = Flow("attn_g_0", chip_steps(both[: width // 4], both[width // 4 :], ndp))

    meet([], [small_flow, flows[0], flows[nz - 1]])
    done[nz - 1] = add_low(*flows[nz - 1].finish())
    meet([], [ring_flow])
    meet([], [small_flow, flows[0]])
    done[0] = flows[0].finish()
    small_sum = add_low(*small_flow.finish())
    total = small_sum.astype(F32)
    for by in range(1, nz):
        total = total + scoped("small_g_ring", shift, small_sum, nz, by).astype(F32)
    moving, _ = ring_flow.finish()
    query_w_grad, out_w_grad = do_unpack_attn(moving, *done[0])
    gate_grad, up_grad, down_grad = do_unpack_ffn(*ffn_flow.finish())
    keys, values = do_place_kv([(place_z - r) % nz for r in range(nz)], kv_ring)
    return (
        do_leave_out(table, after_attn, *part_flow.finish()),
        keys,
        values,
        input_grad,
        total[:, 2 * HD],
        query_w_grad,
        total[:, :HD],
        total[:, HD : 2 * HD],
        out_w_grad,
        total[:, 2 * HD + 1],
        gate_grad,
        up_grad,
        down_grad,
    )


def solution(mesh):
    in_specs = (
        P(("dp", "tensor"), None),
        P("dp"),
        P("dp", "tensor"),
        P("dp", None),
        P("dp", None),
        P("tensor", "dp"),
        P("dp"),
        P("dp", "tensor"),
        P("dp", "tensor"),
        P("tensor", "dp"),
        P("dp"),
        P(),
        P("dp"),
        P(("dp", "tensor"), None),
        P(("dp", "tensor"), None),
        P(("dp", "tensor"), None),
    )
    out_specs = (
        P(("dp", "tensor"), None),
        P("dp", None),
        P("dp", None),
        P(("dp", "tensor"), None),
        P("dp"),
        P("dp", "tensor"),
        P("dp", None),
        P("dp", None),
        P("tensor", "dp"),
        P("dp"),
        P("dp", "tensor"),
        P("dp", "tensor"),
        P("tensor", "dp"),
    )
    body = functools.partial(on_device, mesh.shape["dp"], mesh.shape["tensor"])
    return jax.shard_map(
        body, mesh=mesh, in_specs=in_specs, out_specs=out_specs, check_vma=False
    )
```

time: 1050 us -> 757 us (0.72)
  Pallas kernels: 0 us -> 346 us
  matrix products: 327 us -> 0 us
  other arithmetic: 144 us -> 27.3 us
  waiting for transfers between devices: 382 us -> 300 us
  local copies, waits for them, and re-layouts: 104 us -> 35.6 us
  starting transfers between devices: 82.2 us -> 36.1 us
    pallas_call x0 -> x29, Pallas kernels: none -> 346 us  [the longest x4 86.5 us: ffn_block(): pl.pallas_call(lambda *refs: ffn_kernel(count, steps, last, refs), out_sh...]
    dot_general x179 -> x0, matrix products: 327 us -> none  [dot(): lax.dot_general(left, right, ((dims[0], dims[1]), ((), ())), preferred_el...]
    ppermute x18, waiting for transfers between devices: 277 us -> 183 us  [ring_next(): lax.ppermute(array, 'tensor', [(i, (i + 1) % nt_) for i in range(nt_)])]
    concatenate x20 -> x2, other arithmetic: 91.9 us -> 2.93 us  [the longest x1 2.2 us: gather_steps(): pieces = [jnp.concatenate([shard, moved[0]], axis=0)]]
    unnamed x595 -> x92, local copies, waits for them, and re-layouts: 72.2 us -> 16.1 us
    ppermute x18, starting transfers between devices: 31.8 us -> 2.84 us  [ring_next(): lax.ppermute(array, 'tensor', [(i, (i + 1) % nt_) for i in range(nt_)])]
    ppermute x24 -> x12, waiting for transfers between devices: 3.42 us -> 26.4 us  [core_swap(): return lax.ppermute(array, 'dp', [(d, d ^ 1) for d in range(ndp)])]
    ppermute x24 -> x18, starting transfers between devices: 33.3 us -> 18.5 us  [plane_swap(): lax.ppermute(array, 'dp', [(d, d ^ orders[d & 1][step]) for d in range(nd...]
  transfers between devices with their start and end apart: 75 -> 57, of which waited for: 29 -> 32; matrix products, arithmetic and copies ran while one was open for 32% -> 5% of each run, Pallas kernels for 0% -> 44%
where the time goes in v2:
time: 757 us; the launch traced here: 746 us
  Pallas kernels  346 us (46%)
  waiting for transfers between devices  300 us (40%)
  starting transfers between devices  36.1 us (5%)
  local copies, waits for them, and re-layouts  35.6 us (5%)
  other arithmetic  27.3 us (4%)
    ppermute x18, waiting for transfers between devices, ring_next(): lax.ppermute(array, 'tensor', [(i, (i + 1) % nt_) for i in range(nt_)])  183 us
    pallas_call x4, Pallas kernels, ffn_block(): pl.pallas_call(lambda *refs: ffn_kernel(count, steps, last, refs), out_sh...  86.5 us
    pallas_call x4, Pallas kernels, ffn_weights(): pl.pallas_call(lambda *refs: ffn_weights_kernel(blocks, count, steps, las...  67.7 us
    pallas_call x4, Pallas kernels, attend_back_block(): pl.pallas_call(lambda *refs: attend_back_kernel(count, blocks, first, ref...  64.5 us
    ppermute x18, waiting for transfers between devices, plane_swap(): lax.ppermute(array, 'dp', [(d, d ^ orders[d & 1][step]) for d in range(nd...  61.9 us
    pallas_call x2, Pallas kernels, attend_block(): pl.pallas_call(lambda *refs: attend_kernel(count, blocks, refs), out_shap...  44.3 us
    pallas_call x5, Pallas kernels, attend_weights(): pl.pallas_call(lambda *refs: attend_weights_kernel(int(send is not None),...  32 us
    ppermute x9, waiting for transfers between devices, shift(): lax.ppermute(array, 'tensor', [(i, (i + by) % nt_) for i in range(nt_)])  28.7 us
  transfers between devices with their start and end apart: 57, of which 32 were waited for; matrix products, arithmetic and copies ran while one was open for 5% of the time, Pallas kernels for 44%

profile of v2, /device:TPU:0, one launch (start us, length us, event | category | flops | bytes accessed | tf_op | source)
XLA Modules:
  0.0 746.4 jit_solution(14716417769700553231)
XLA Ops:
  10.9 12.7 %collective-permute-done.1 = bf16[256,1024]{1,0:T(8,128)(2,1)S(1)} collective-permute-done((bf16[256,1024]{1,0:T(8,128)(2,1)}, bf16[256,1024]{1,0:T(8,128)(2,1)S(1)}, u32[]{:S(2)}, u32[]{:S(2)}) %collective-permute-start.1) | collective-permute-done | bytes 524320 | tf_op jit(solution)/shard_map/attn_w_ring/ppermute | solution.py:156
  26.1 6.2 take_columns.1.refs_1_.refs_3_.given_ref
  38.5 13.5 %collective-permute-done.3 = bf16[256,1024]{1,0:T(8,128)(2,1)S(1)} collective-permute-done((bf16[256,1024]{1,0:T(8,128)(2,1)S(1)}, bf16[256,1024]{1,0:T(8,128)(2,1)S(1)}, u32[]{:S(2)}, u32[]{:S(2)}) %collective-permute-start.3) | collective-permute-done | bytes 524320 | tf_op jit(solution)/shard_map/attn_w_ring/ppermute | solution.py:156
  54.2 14.0 %collective-permute-done.6 = bf16[256,1024]{1,0:T(8,128)(2,1)S(1)} collective-permute-done((bf16[256,1024]{1,0:T(8,128)(2,1)S(1)}, bf16[256,1024]{1,0:T(8,128)(2,1)S(1)}, u32[]{:S(2)}, u32[]{:S(2)}) %collective-permute-start.6) | collective-permute-done | bytes 524320 | tf_op jit(solution)/shard_map/attn_w_ring/ppermute | solution.py:156
  69.6 5.5 enter.1
  78.9 6.1 collective-permute-done.7.refs_4_.refs_6_.refs_8_.refs_1_
  85.0 7.1 collective-permute-done.8.refs_5_.refs_7_.refs_9_.refs_2_
  102.6 13.6 %attend.2 = (bf16[384,512]{1,0:T(8,128)(2,1)}, bf16[384,512]{1,0:T(8,128)(2,1)}, f32[2,1,768]{2,1,0:T(1,128)}, f32[384,2048]{1,0:T(8,128)}) custom-call(bf16[384,2048]{1,0:T(8,128)(2,1)} %get-tuple-element.189.refs_0_.refs_7_, f32[1536,384]{1,0:T(8,128)} %and_select_fusion.refs_1_, bf16[384,2048]{1,0:T(8,128)(2,1)} %get-tuple-element.191.refs_2_.refs_8_, ...), custom_call_target="tpu_custom_call" | custom-call | flops 2818572288 | bytes 14000000 | tf_op jit(solution)/shard_map/attend/pallas_call | solution.py:407
  116.2 20.1 %collective-permute-done.12.refs_1_.refs_4_ = bf16[384,2048]{1,0:T(8,128)(2,1)} collective-permute-done((bf16[384,2048]{1,0:T(8,128)(2,1)S(1)}, bf16[384,2048]{1,0:T(8,128)(2,1)}, u32[]{:S(2)}, u32[]{:S(2)}) %collective-permute-start.12) | collective-permute-done | bytes 1572896 | tf_op jit(solution)/shard_map/grad_ring/ppermute | solution.py:156
  141.5 9.0 %collective-permute-done.14.refs_9_.refs_13_.refs_11_.refs_15_.refs_17_ = bf16[512,3072]{1,0:T(8,128)(2,1)S(1)} collective-permute-done((bf16[512,3072]{1,0:T(8,128)(2,1)S(1)}, bf16[512,3072]{1,0:T(8,128)(2,1)S(1)}, u32[]{:S(2)}, u32[]{:S(2)}) %collective-permute-start.14) | collective-permute-done | bytes 3145760 | tf_op jit(solution)/shard_map/attn_w_far/ppermute | solution.py:59
  152.1 30.7 %attend.3 = (bf16[384,1536]{1,0:T(8,128)(2,1)}, bf16[384,1536]{1,0:T(8,128)(2,1)}, f32[6,1,768]{2,1,0:T(1,128)}, f32[384,2048]{1,0:T(8,128)}) custom-call(bf16[384,2048]{1,0:T(8,128)(2,1)} %get-tuple-element.189.refs_0_.refs_7_, f32[1536,384]{1,0:T(8,128)} %and_select_fusion.refs_1_, f32[384,2048]{1,0:T(8,128)} %get-tuple-element.201.refs_2_, ...), custom_call_target="tpu_custom_call" | custom-call | flops 8455716864 | bytes 14000000 | tf_op jit(solution)/shard_map/attend/pallas_call | solution.py:407
  182.9 6.7 collective-permute-done.16.refs_3_
  197.2 21.5 %ffn_block.4 = (bf16[384,4224]{1,0:T(8,128)(2,1)}, bf16[384,2048]{1,0:T(8,128)(2,1)}, bf16[384,2048]{1,0:T(8,128)(2,1)}) custom-call(bf16[384,2048]{1,0:T(8,128)(2,1)} %copy-done.21, bf16[384,2048]{1,0:T(8,128)(2,1)} %take_columns.1.refs_1_.refs_3_.given_ref, bf16[512,4224]{1,0:T(8,128)(2,1)} %constant_dynamic-update-slice_fusion.5.refs_2_, ...), custom_call_target="tpu_custom_call" | custom-call | flops 13287555072 | bytes 26738688 | tf_op jit(solution)/shard_map/ffn_block/pallas_call | solution.py:630
  218.7 12.9 %collective-permute-done.18.refs_0_.refs_1_ = bf16[384,2048]{1,0:T(8,128)(2,1)S(1)} collective-permute-done((bf16[384,2048]{1,0:T(8,128)(2,1)S(1)}, bf16[384,2048]{1,0:T(8,128)(2,1)S(1)}, u32[]{:S(2)}, u32[]{:S(2)}) %collective-permute-start.18) | collective-permute-done | bytes 1572896 | tf_op jit(solution)/shard_map/ffn_ring/ppermute | solution.py:156
  232.7 21.3 %ffn_block.5 = (bf16[384,4224]{1,0:T(8,128)(2,1)}, bf16[384,2048]{1,0:T(8,128)(2,1)}, bf16[384,2048]{1,0:T(8,128)(2,1)}) custom-call(bf16[384,2048]{1,0:T(8,128)(2,1)} %copy-done.40, bf16[384,2048]{1,0:T(8,128)(2,1)} %collective-permute-done.12.refs_1_.refs_4_, bf16[512,4224]{1,0:T(8,128)(2,1)} %constant_dynamic-update-slice_fusion.5.refs_2_, ...), custom_call_target="tpu_custom_call" | custom-call | flops 13287555072 | bytes 26738688 | tf_op jit(solution)/shard_map/ffn_block/pallas_call | solution.py:630
  254.1 16.7 %collective-permute-done.21.refs_0_.refs_2_ = bf16[384,2048]{1,0:T(8,128)(2,1)} collective-permute-done((bf16[384,2048]{1,0:T(8,128)(2,1)S(1)}, bf16[384,2048]{1,0:T(8,128)(2,1)}, u32[]{:S(2)}, u32[]{:S(2)}) %collective-permute-start.21) | collective-permute-done | bytes 1572896 | tf_op jit(solution)/shard_map/ffn_ring/ppermute | solution.py:156
  271.0 33.4 %collective-permute-done.23.refs_1_ = bf16[384,2048]{1,0:T(8,128)(2,1)S(1)} collective-permute-done((bf16[384,2048]{1,0:T(8,128)(2,1)}, bf16[384,2048]{1,0:T(8,128)(2,1)S(1)}, u32[]{:S(2)}, u32[]{:S(2)}) %collective-permute-start.23) | collective-permute-done | bytes 1572896 | tf_op jit(solution)/shard_map/grad_ring/ppermute | solution.py:156
  304.4 22.0 %ffn_block.6 = (bf16[384,4224]{1,0:T(8,128)(2,1)}, bf16[384,2048]{1,0:T(8,128)(2,1)}, bf16[384,2048]{1,0:T(8,128)(2,1)}) custom-call(bf16[384,2048]{1,0:T(8,128)(2,1)} %collective-permute-done.21.refs_0_.refs_2_, bf16[384,2048]{1,0:T(8,128)(2,1)} %collective-permute-done.17.refs_1_.refs_5_, bf16[512,4224]{1,0:T(8,128)(2,1)} %constant_dynamic-update-slice_fusion.5.refs_2_, ...), custom_call_target="tpu_custom_call" | custom-call | flops 13287555072 | bytes 26738688 | tf_op jit(solution)/shard_map/ffn_block/pallas_call | solution.py:630
  326.4 11.7 %collective-permute-done.22.refs_0_ = bf16[384,2048]{1,0:T(8,128)(2,1)S(1)} collective-permute-done((bf16[384,2048]{1,0:T(8,128)(2,1)}, bf16[384,2048]{1,0:T(8,128)(2,1)S(1)}, u32[]{:S(2)}, u32[]{:S(2)}) %collective-permute-start.22) | collective-permute-done | bytes 1572896 | tf_op jit(solution)/shard_map/ffn_ring/ppermute | solution.py:156
  338.1 20.3 %ffn_weights.4.refs_3_ = bf16[1024,4224]{1,0:T(8,128)(2,1)} custom-call(bf16[384,2048]{1,0:T(8,128)(2,1)} %copy-done.21, bf16[384,2048]{1,0:T(8,128)(2,1)} %copy-done.40, bf16[384,2048]{1,0:T(8,128)(2,1)} %collective-permute-done.21.refs_0_.refs_2_, bf16[384,2048]{1,0:T(8,128)(2,1)} %take_columns.1.refs_1_.refs_3_.given_ref, ...), custom_call_target="tpu_custom_call" | custom-call | flops 9965666304 | bytes 18382848 | tf_op jit(solution)/shard_map/ffn_weights/pallas_call | solution.py:695
  358.5 12.1 %collective-permute-done.24 = bf16[384,2048]{1,0:T(8,128)(2,1)S(1)} collective-permute-done((bf16[384,2048]{1,0:T(8,128)(2,1)}, bf16[384,2048]{1,0:T(8,128)(2,1)S(1)}, u32[]{:S(2)}, u32[]{:S(2)}) %collective-permute-start.24) | collective-permute-done | bytes 1572896 | tf_op jit(solution)/shard_map/backs/ppermute | solution.py:156
  371.3 20.8 %ffn_weights.5 = (bf16[512,4224]{1,0:T(8,128)(2,1)}, bf16[512,4224]{1,0:T(8,128)(2,1)}) custom-call(bf16[384,2048]{1,0:T(8,128)(2,1)} %copy-done.21, bf16[384,2048]{1,0:T(8,128)(2,1)} %copy-done.40, bf16[384,2048]{1,0:T(8,128)(2,1)} %collective-permute-done.21.refs_0_.refs_2_, bf16[384,2048]{1,0:T(8,128)(2,1)} %take_columns.1.refs_1_.refs_3_.given_ref, ...), custom_call_target="tpu_custom_call" | custom-call | flops 9965666304 | bytes 28114944 | tf_op jit(solution)/shard_map/ffn_weights/pallas_call | solution.py:695
  392.1 21.7 %ffn_block.7 = (bf16[384,4224]{1,0:T(8,128)(2,1)}, bf16[384,2048]{1,0:T(8,128)(2,1)}, bf16[384,2048]{1,0:T(8,128)(2,1)}) custom-call(bf16[384,2048]{1,0:T(8,128)(2,1)} %copy-done.12, bf16[384,2048]{1,0:T(8,128)(2,1)} %copy-done.11, bf16[512,4224]{1,0:T(8,128)(2,1)} %constant_dynamic-update-slice_fusion.5.refs_2_, ...), custom_call_target="tpu_custom_call" | custom-call | flops 13287555072 | bytes 26738688 | tf_op jit(solution)/shard_map/ffn_block/pallas_call | solution.py:630
  413.8 11.4 %ffn_weights.6 = bf16[1024,4224]{1,0:T(8,128)(2,1)} custom-call(bf16[384,2048]{1,0:T(8,128)(2,1)} %copy-done.12, bf16[384,2048]{1,0:T(8,128)(2,1)} %copy-done.11, bf16[384,4224]{1,0:T(8,128)(2,1)} %get-tuple-element.230.refs_2_, bf16[1024,4224]{1,0:T(8,128)(2,1)} %ffn_weights.4.refs_3_), custom_call_target="tpu_custom_call" | custom-call | flops 3321888768 | bytes 11894784 | tf_op jit(solution)/shard_map/ffn_weights/pallas_call | solution.py:695
  425.9 13.1 %collective-permute-done.26.refs_5_.refs_6_ = bf16[1024,4224]{1,0:T(8,128)(2,1)} collective-permute-done((bf16[1024,4224]{1,0:T(8,128)(2,1)}, bf16[1024,4224]{1,0:T(8,128)(2,1)}, u32[]{:S(2)}, u32[]{:S(2)}) %collective-permute-start.26) | collective-permute-done | bytes 8650784 | tf_op jit(solution)/shard_map/ffn_g/ppermute | solution.py:59
  439.1 15.2 %ffn_weights.7 = (bf16[512,4224]{1,0:T(8,128)(2,1)}, bf16[512,4224]{1,0:T(8,128)(2,1)}) custom-call(bf16[384,2048]{1,0:T(8,128)(2,1)} %copy-done.12, bf16[384,2048]{1,0:T(8,128)(2,1)} %copy-done.11, bf16[384,4224]{1,0:T(8,128)(2,1)} %get-tuple-element.230.refs_2_, bf16[512,4224]{1,0:T(8,128)(2,1)} %get-tuple-element.231.refs_3_, ...), custom_call_target="tpu_custom_call" | custom-call | flops 3321888768 | bytes 15138816 | tf_op jit(solution)/shard_map/ffn_weights/pallas_call | solution.py:695
  454.2 10.5 %collective-permute-done.27.come_ref = bf16[384,2048]{1,0:T(8,128)(2,1)S(1)} collective-permute-done((bf16[384,2048]{1,0:T(8,128)(2,1)S(1)}, bf16[384,2048]{1,0:T(8,128)(2,1)S(1)}, u32[]{:S(2)}, u32[]{:S(2)}) %collective-permute-start.27) | collective-permute-done | bytes 1572896 | tf_op jit(solution)/shard_map/backs/ppermute | solution.py:156
  465.9 8.3 %turn.1 = (f32[384,2048]{1,0:T(8,128)}, bf16[384,2048]{1,0:T(8,128)(2,1)}, bf16[2048,384]{1,0:T(8,128)(2,1)}, f32[1,2048]{1,0:T(1,128)}) custom-call(bf16[384,2048]{1,0:T(8,128)(2,1)} %copy-done.24, bf16[384,2048]{1,0:T(8,128)(2,1)} %get-tuple-element.239.part_ref, bf16[384,2048]{1,0:T(8,128)(2,1)} %take_columns.1.refs_1_.refs_3_.given_ref, ...), custom_call_target="tpu_custom_call" | custom-call | bytes 15728640 | tf_op jit(solution)/shard_map/turn/pallas_call | solution.py:728
  474.2 15.3 %attend_back.4 = (bf16[384,512]{1,0:T(8,128)(2,1)}, f32[1536,256]{1,0:T(8,128)}, f32[384,2048]{1,0:T(8,128)}) custom-call(bf16[384,2048]{1,0:T(8,128)(2,1)} %get-tuple-element.278.refs_0_, f32[1536,384]{1,0:T(8,128)} %and_select_fusion.refs_1_, bf16[384,1536]{1,0:T(8,128)(2,1)} %get-tuple-element.243.refs_2_.refs_4_, ...), custom_call_target="tpu_custom_call" | custom-call | flops 4630511616 | bytes 16000000 | tf_op jit(solution)/shard_map/attend_back/pallas_call | solution.py:497
  494.4 9.4 %collective-permute-done.28 = bf16[384,2048]{1,0:T(8,128)(2,1)S(1)} collective-permute-done((bf16[384,2048]{1,0:T(8,128)(2,1)}, bf16[384,2048]{1,0:T(8,128)(2,1)S(1)}, u32[]{:S(2)}, u32[]{:S(2)}) %collective-permute-start.28) | collective-permute-done | bytes 1572896 | tf_op jit(solution)/shard_map/parts/ppermute | solution.py:156
  503.8 11.2 %collective-permute-done.29 = bf16[512,4224]{1,0:T(8,128)(2,1)} collective-permute-done((bf16[512,4224]{1,0:T(8,128)(2,1)}, bf16[512,4224]{1,0:T(8,128)(2,1)}, u32[]{:S(2)}, u32[]{:S(2)}) %collective-permute-start.29) | collective-permute-done | bytes 4325408 | tf_op jit(solution)/shard_map/ffn_g/ppermute | solution.py:55
  522.6 16.6 %attend_back.5 = (bf16[384,512]{1,0:T(8,128)(2,1)}, f32[1536,256]{1,0:T(8,128)}, f32[384,2048]{1,0:T(8,128)}) custom-call(bf16[384,2048]{1,0:T(8,128)(2,1)} %get-tuple-element.278.refs_0_, f32[1536,384]{1,0:T(8,128)} %and_select_fusion.refs_1_, f32[1536,256]{1,0:T(8,128)} %get-tuple-element.250.refs_2_, f32[384,2048]{1,0:T(8,128)} %get-tuple-element.251.refs_3_, ...), custom_call_target="tpu_custom_call" | custom-call | flops 4630511616 | bytes 16000000 | tf_op jit(solution)/shard_map/attend_back/pallas_call | solution.py:497
  539.2 6.9 collective-permute-done.31.come_ref
  546.1 7.7 %attend_weights.6 = (bf16[1024,1024]{1,0:T(8,128)(2,1)}, bf16[1024,1024]{1,0:T(8,128)(2,1)}) custom-call(bf16[2048,384]{1,0:T(8,128)(2,1)} %get-tuple-element.241.refs_0_.refs_4_, bf16[2048,384]{1,0:T(8,128)(2,1)} %get-tuple-element.242.refs_1_.refs_5_, bf16[384,512]{1,0:T(8,128)(2,1)} %get-tuple-element.256.refs_2_.refs_6_, ...), custom_call_target="tpu_custom_call" | custom-call | flops 1610612736 | bytes 6000000 | tf_op jit(solution)/shard_map/attend_weights/pallas_call | solution.py:564
  556.6 4.9 collective-permute-done.32
  563.7 16.6 %attend_back.6 = (bf16[384,512]{1,0:T(8,128)(2,1)}, f32[1536,256]{1,0:T(8,128)}, f32[384,2048]{1,0:T(8,128)}) custom-call(bf16[384,2048]{1,0:T(8,128)(2,1)} %get-tuple-element.278.refs_0_, f32[1536,384]{1,0:T(8,128)} %and_select_fusion.refs_1_, f32[1536,256]{1,0:T(8,128)} %get-tuple-element.263.refs_2_, f32[384,2048]{1,0:T(8,128)} %get-tuple-element.264.refs_3_, ...), custom_call_target="tpu_custom_call" | custom-call | flops 4630511616 | bytes 16000000 | tf_op jit(solution)/shard_map/attend_back/pallas_call | solution.py:497
  581.7 7.0 attend_weights.7
  591.4 10.9 %collective-permute-done.35.come_ref = bf16[384,2048]{1,0:T(8,128)(2,1)} collective-permute-done((bf16[384,2048]{1,0:T(8,128)(2,1)S(1)}, bf16[384,2048]{1,0:T(8,128)(2,1)}, u32[]{:S(2)}, u32[]{:S(2)}) %collective-permute-start.35) | collective-permute-done | bytes 1572896 | tf_op jit(solution)/shard_map/parts/ppermute | solution.py:156
  603.7 16.0 %attend_back.7 = (bf16[384,512]{1,0:T(8,128)(2,1)}, f32[1536,256]{1,0:T(8,128)}, f32[384,2048]{1,0:T(8,128)}) custom-call(bf16[384,2048]{1,0:T(8,128)(2,1)} %get-tuple-element.278.refs_0_, f32[1536,384]{1,0:T(8,128)} %and_select_fusion.refs_1_, f32[1536,256]{1,0:T(8,128)} %get-tuple-element.279.refs_2_, f32[384,2048]{1,0:T(8,128)} %get-tuple-element.280.refs_3_, ...), custom_call_target="tpu_custom_call" | custom-call | flops 4630511616 | bytes 16000000 | tf_op jit(solution)/shard_map/attend_back/pallas_call | solution.py:497
  628.0 7.2 attend_weights.8
  637.9 7.3 collective-permute-done.38.refs_1_
  645.2 7.5 collective-permute-done.39.refs_2_
  659.1 9.9 %leave.1 = (f32[384,2048]{1,0:T(8,128)}, bf16[1024,384]{1,0:T(8,128)(2,1)}, bf16[1024,384]{1,0:T(8,128)(2,1)}) custom-call(s32[8]{0:T(128)} %stack.36.table_ref, f32[1536,256]{1,0:T(8,128)} %get-tuple-element.284.refs_0_, bf16[384,256]{1,0:T(8,128)(2,1)} %copy-done.35, bf16[384,256]{1,0:T(8,128)(2,1)} %copy-done.36, ...), custom_call_target="tpu_custom_call" | custom-call | flops 805306368 | bytes 16000000 | tf_op jit(solution)/shard_map/leave/pallas_call | solution.py:811
  675.7 5.2 attend_weights.9
  687.7 11.6 %collective-permute-done.48 = bf16[256,1024]{1,0:T(8,128)(2,1)S(1)} collective-permute-done((bf16[256,1024]{1,0:T(8,128)(2,1)S(1)}, bf16[256,1024]{1,0:T(8,128)(2,1)S(1)}, u32[]{:S(2)}, u32[]{:S(2)}) %collective-permute-start.48) | collective-permute-done | bytes 524320 | tf_op jit(solution)/shard_map/attn_g_3/ppermute | solution.py:55
  707.7 7.5 %collective-permute-done.49 = bf16[512,384]{1,0:T(8,128)(2,1)S(1)} collective-permute-done((bf16[512,384]{1,0:T(8,128)(2,1)S(1)}, bf16[512,384]{1,0:T(8,128)(2,1)S(1)}, u32[]{:S(2)}, u32[]{:S(2)}) %collective-permute-start.49) | collective-permute-done | bytes 393248 | tf_op jit(solution)/shard_map/small_g/ppermute | solution.py:55
  730.2 4.9 unpack_ffn.1
  735.1 5.2 leave_out.1
  (236 shorter events, 137.7 us)
Async XLA Ops:
  5.2 18.4 %collective-permute-start = (bf16[256,1408]{1,0:T(8,128)(2,1)}, bf16[256,1408]{1,0:T(8,128)(2,1)S(1)}, u32[]{:S(2)}, u32[]{:S(2)}) collective-permute-start(bf16[256,1408]{1,0:T(8,128)(2,1)} %get-tuple-element.170), channel_id=1, source_target_pairs={{0,8},{4,20},{8,0},{12,28},{16,24},{20,4},{24,16},{28,12},{1,9},{5... | collective-permute-start | bytes 2162696 | tf_op jit(solution)/shard_map/attn_w_near/ppermute | solution.py:55
  8.2 15.5 %collective-permute-start.1 = (bf16[256,1024]{1,0:T(8,128)(2,1)}, bf16[256,1024]{1,0:T(8,128)(2,1)S(1)}, u32[]{:S(2)}, u32[]{:S(2)}) collective-permute-start(bf16[256,1024]{1,0:T(8,128)(2,1)} %get-tuple-element.171), channel_id=1, source_target_pairs={{0,1},{1,2},{2,3},{3,0},{4,5},{5,6},{6,7},{7,4},{8,9},{9,10},{10,1... | collective-permute-start | bytes 1572872 | tf_op jit(solution)/shard_map/attn_w_ring/ppermute | solution.py:156
  24.5 27.6 %collective-permute-start.2 = (bf16[512,1408]{1,0:T(8,128)(2,1)S(1)}, bf16[512,1408]{1,0:T(8,128)(2,1)S(1)}, u32[]{:S(2)}, u32[]{:S(2)}) collective-permute-start(bf16[512,1408]{1,0:T(8,128)(2,1)S(1)} %constant_dynamic-update-slice_fusion.refs_0_.refs_4_.refs_8_.refs_7_.refs_11_.refs_15_.refs_12_.refs_16_), channel_id=1, source_target_pairs={{0,16},{4,12},{8,24},{12,4},{16,0},{20,28},{24,8},{28,20},{1,17},{... | collective-permute-start | bytes 4325384 | tf_op jit(solution)/shard_map/attn_w_near/ppermute | solution.py:55
  35.7 16.3 %collective-permute-start.3 = (bf16[256,1024]{1,0:T(8,128)(2,1)S(1)}, bf16[256,1024]{1,0:T(8,128)(2,1)S(1)}, u32[]{:S(2)}, u32[]{:S(2)}) collective-permute-start(bf16[256,1024]{1,0:T(8,128)(2,1)S(1)} %copy-done.33), channel_id=1, source_target_pairs={{0,1},{1,2},{2,3},{3,0},{4,5},{5,6},{6,7},{7,4},{8,9},{9,10},{10,1... | collective-permute-start | bytes 1572872 | tf_op jit(solution)/shard_map/attn_w_ring/ppermute | solution.py:156
  37.8 16.4 %collective-permute-start.4 = (bf16[512,1408]{1,0:T(8,128)(2,1)S(1)}, bf16[512,1408]{1,0:T(8,128)(2,1)S(1)}, u32[]{:S(2)}, u32[]{:S(2)}) collective-permute-start(bf16[512,1408]{1,0:T(8,128)(2,1)S(1)} %constant_dynamic-update-slice_fusion.refs_0_.refs_4_.refs_8_.refs_7_.refs_11_.refs_15_.refs_12_.refs_16_), channel_id=1, source_target_pairs={{0,4},{4,0},{8,12},{12,8},{16,20},{20,16},{24,28},{28,24},{1,5},{5... | collective-permute-start | bytes 4325384 | tf_op jit(solution)/shard_map/attn_w_near/ppermute | solution.py:59
  52.0 16.1 %collective-permute-start.5 = (bf16[512,1408]{1,0:T(8,128)(2,1)S(1)}, bf16[512,1408]{1,0:T(8,128)(2,1)S(1)}, u32[]{:S(2)}, u32[]{:S(2)}) collective-permute-start(bf16[512,1408]{1,0:T(8,128)(2,1)S(1)} %collective-permute-done.2.refs_1_.refs_5_.refs_9_.refs_8_.refs_12_.refs_16_.refs_13_.refs_17_), channel_id=1, source_target_pairs={{0,4},{4,0},{8,12},{12,8},{16,20},{20,16},{24,28},{28,24},{1,5},{5... | collective-permute-start | bytes 4325384 | tf_op jit(solution)/shard_map/attn_w_near/ppermute | solution.py:59
  52.0 16.1 %collective-permute-start.6 = (bf16[256,1024]{1,0:T(8,128)(2,1)S(1)}, bf16[256,1024]{1,0:T(8,128)(2,1)S(1)}, u32[]{:S(2)}, u32[]{:S(2)}) collective-permute-start(bf16[256,1024]{1,0:T(8,128)(2,1)S(1)} %collective-permute-done.3), channel_id=1, source_target_pairs={{0,1},{1,2},{2,3},{3,0},{4,5},{5,6},{6,7},{7,4},{8,9},{9,10},{10,1... | collective-permute-start | bytes 1572872 | tf_op jit(solution)/shard_map/attn_w_ring/ppermute | solution.py:156
  52.1 40.0 %collective-permute-start.11 = (bf16[256,4224]{1,0:T(8,128)(2,1)}, bf16[256,4224]{1,0:T(8,128)(2,1)}, u32[]{:S(2)}, u32[]{:S(2)}) collective-permute-start(bf16[256,4224]{1,0:T(8,128)(2,1)} %pack_ffn.1), channel_id=1, source_target_pairs={{0,8},{4,20},{8,0},{12,28},{16,24},{20,4},{24,16},{28,12},{1,9},{5... | collective-permute-start | bytes 6488072 | tf_op jit(solution)/shard_map/ffn_w/ppermute | solution.py:55
  69.1 27.0 %collective-permute-start.10 = (bf16[256,3072]{1,0:T(8,128)(2,1)}, bf16[256,3072]{1,0:T(8,128)(2,1)}, u32[]{:S(2)}, u32[]{:S(2)}) collective-permute-start(bf16[256,3072]{1,0:T(8,128)(2,1)} %constant_dynamic-update-slice_fusion.2), channel_id=1, source_target_pairs={{0,8},{4,20},{8,0},{12,28},{16,24},{20,4},{24,16},{28,12},{1,9},{5... | collective-permute-start | bytes 4718600 | tf_op jit(solution)/shard_map/attn_w_far/ppermute | solution.py:55
  75.1 17.1 %collective-permute-start.8 = (bf16[384,256]{1,0:T(8,128)(2,1)}, bf16[384,256]{1,0:T(8,128)(2,1)S(1)}, u32[]{:S(2)}, u32[]{:S(2)}) collective-permute-start(bf16[384,256]{1,0:T(8,128)(2,1)} %get-tuple-element.192.refs_3_.refs_5_.refs_7_.refs_0_), channel_id=1, source_target_pairs={{0,2},{1,3},{2,0},{3,1},{4,6},{5,7},{6,4},{7,5},{8,10},{9,11},{10,... | collective-permute-start | bytes 589832 | tf_op jit(solution)/shard_map/kv/ppermute | solution.py:160
  75.2 17.0 %collective-permute-start.9 = (bf16[384,256]{1,0:T(8,128)(2,1)}, bf16[384,256]{1,0:T(8,128)(2,1)S(1)}, u32[]{:S(2)}, u32[]{:S(2)}) collective-permute-start(bf16[384,256]{1,0:T(8,128)(2,1)} %get-tuple-element.192.refs_3_.refs_5_.refs_7_.refs_0_), channel_id=1, source_target_pairs={{0,3},{1,0},{2,1},{3,2},{4,7},{5,4},{6,5},{7,6},{8,11},{9,8},{10,9... | collective-permute-start | bytes 589832 | tf_op jit(solution)/shard_map/kv/ppermute | solution.py:160
  98.3 37.9 %collective-permute-start.13 = (bf16[512,3072]{1,0:T(8,128)(2,1)S(1)}, bf16[512,3072]{1,0:T(8,128)(2,1)}, u32[]{:S(2)}, u32[]{:S(2)}) collective-permute-start(bf16[512,3072]{1,0:T(8,128)(2,1)S(1)} %pad_maximum_fusion.refs_7_.refs_11_.refs_9_.refs_13_.refs_15_), channel_id=1, source_target_pairs={{0,16},{4,12},{8,24},{12,4},{16,0},{20,28},{24,8},{28,20},{1,17},{... | collective-permute-start | bytes 9437192 | tf_op jit(solution)/shard_map/attn_w_far/ppermute | solution.py:55
  98.4 37.8 %collective-permute-start.12 = (bf16[384,2048]{1,0:T(8,128)(2,1)S(1)}, bf16[384,2048]{1,0:T(8,128)(2,1)}, u32[]{:S(2)}, u32[]{:S(2)}) collective-permute-start(bf16[384,2048]{1,0:T(8,128)(2,1)S(1)} %copy-done.13), channel_id=1, source_target_pairs={{0,1},{1,2},{2,3},{3,0},{4,5},{5,6},{6,7},{7,4},{8,9},{9,10},{10,1... | collective-permute-start | bytes 4718600 | tf_op jit(solution)/shard_map/grad_ring/ppermute | solution.py:156
  139.3 50.2 %collective-permute-start.16 = (bf16[512,4224]{1,0:T(8,128)(2,1)}, bf16[512,4224]{1,0:T(8,128)(2,1)}, u32[]{:S(2)}, u32[]{:S(2)}) collective-permute-start(bf16[512,4224]{1,0:T(8,128)(2,1)} %constant_dynamic-update-slice_fusion.5.refs_2_), channel_id=1, source_target_pairs={{0,16},{4,12},{8,24},{12,4},{16,0},{20,28},{24,8},{28,20},{1,17},{... | collective-permute-start | bytes 12976136 | tf_op jit(solution)/shard_map/ffn_w/ppermute | solution.py:55
  140.8 42.1 %collective-permute-start.17 = (bf16[384,2048]{1,0:T(8,128)(2,1)}, bf16[384,2048]{1,0:T(8,128)(2,1)}, u32[]{:S(2)}, u32[]{:S(2)}) collective-permute-start(bf16[384,2048]{1,0:T(8,128)(2,1)} %collective-permute-done.12.refs_1_.refs_4_), channel_id=1, source_target_pairs={{0,1},{1,2},{2,3},{3,0},{4,5},{5,6},{6,7},{7,4},{8,9},{9,10},{10,1... | collective-permute-start | bytes 4718600 | tf_op jit(solution)/shard_map/grad_ring/ppermute | solution.py:156
  140.9 52.1 %collective-permute-start.19 = (bf16[512,4224]{1,0:T(8,128)(2,1)}, bf16[512,4224]{1,0:T(8,128)(2,1)}, u32[]{:S(2)}, u32[]{:S(2)}) collective-permute-start(bf16[512,4224]{1,0:T(8,128)(2,1)} %constant_dynamic-update-slice_fusion.5.refs_2_), channel_id=1, source_target_pairs={{0,4},{4,0},{8,12},{12,8},{16,20},{20,16},{24,28},{28,24},{1,5},{5... | collective-permute-start | bytes 12976136 | tf_op jit(solution)/shard_map/ffn_w/ppermute | solution.py:59
  192.9 38.7 %collective-permute-start.18 = (bf16[384,2048]{1,0:T(8,128)(2,1)S(1)}, bf16[384,2048]{1,0:T(8,128)(2,1)S(1)}, u32[]{:S(2)}, u32[]{:S(2)}) collective-permute-start(bf16[384,2048]{1,0:T(8,128)(2,1)S(1)} %multiply_convert_fusion.refs_0_), channel_id=1, source_target_pairs={{0,1},{1,2},{2,3},{3,0},{4,5},{5,6},{6,7},{7,4},{8,9},{9,10},{10,1... | collective-permute-start | bytes 4718600 | tf_op jit(solution)/shard_map/ffn_ring/ppermute | solution.py:156
  231.6 39.2 %collective-permute-start.21 = (bf16[384,2048]{1,0:T(8,128)(2,1)S(1)}, bf16[384,2048]{1,0:T(8,128)(2,1)}, u32[]{:S(2)}, u32[]{:S(2)}) collective-permute-start(bf16[384,2048]{1,0:T(8,128)(2,1)S(1)} %collective-permute-done.18.refs_0_.refs_1_), channel_id=1, source_target_pairs={{0,1},{1,2},{2,3},{3,0},{4,5},{5,6},{6,7},{7,4},{8,9},{9,10},{10,1... | collective-permute-start | bytes 4718600 | tf_op jit(solution)/shard_map/ffn_ring/ppermute | solution.py:156
  231.6 72.8 %collective-permute-start.23 = (bf16[384,2048]{1,0:T(8,128)(2,1)}, bf16[384,2048]{1,0:T(8,128)(2,1)S(1)}, u32[]{:S(2)}, u32[]{:S(2)}) collective-permute-start(bf16[384,2048]{1,0:T(8,128)(2,1)} %collective-permute-done.17.refs_1_.refs_5_), channel_id=1, source_target_pairs={{0,1},{1,2},{2,3},{3,0},{4,5},{5,6},{6,7},{7,4},{8,9},{9,10},{10,1... | collective-permute-start | bytes 4718600 | tf_op jit(solution)/shard_map/grad_ring/ppermute | solution.py:156
  270.8 67.3 %collective-permute-start.22 = (bf16[384,2048]{1,0:T(8,128)(2,1)}, bf16[384,2048]{1,0:T(8,128)(2,1)S(1)}, u32[]{:S(2)}, u32[]{:S(2)}) collective-permute-start(bf16[384,2048]{1,0:T(8,128)(2,1)} %collective-permute-done.21.refs_0_.refs_2_), channel_id=1, source_target_pairs={{0,1},{1,2},{2,3},{3,0},{4,5},{5,6},{6,7},{7,4},{8,9},{9,10},{10,1... | collective-permute-start | bytes 4718600 | tf_op jit(solution)/shard_map/ffn_ring/ppermute | solution.py:156
  270.8 99.7 %collective-permute-start.24 = (bf16[384,2048]{1,0:T(8,128)(2,1)}, bf16[384,2048]{1,0:T(8,128)(2,1)S(1)}, u32[]{:S(2)}, u32[]{:S(2)}) collective-permute-start(bf16[384,2048]{1,0:T(8,128)(2,1)} %get-tuple-element.221), channel_id=1, source_target_pairs={{0,1},{1,2},{2,3},{3,0},{4,5},{5,6},{6,7},{7,4},{8,9},{9,10},{10,1... | collective-permute-start | bytes 4718600 | tf_op jit(solution)/shard_map/backs/ppermute | solution.py:156
  371.2 42.6 %collective-permute-start.25 = (bf16[384,2048]{1,0:T(8,128)(2,1)S(1)}, bf16[384,2048]{1,0:T(8,128)(2,1)S(1)}, u32[]{:S(2)}, u32[]{:S(2)}) collective-permute-start(bf16[384,2048]{1,0:T(8,128)(2,1)S(1)} %add_convert_fusion.5), channel_id=1, source_target_pairs={{0,1},{1,2},{2,3},{3,0},{4,5},{5,6},{6,7},{7,4},{8,9},{9,10},{10,1... | collective-permute-start | bytes 4718600 | tf_op jit(solution)/shard_map/backs/ppermute | solution.py:156
  425.9 38.9 %collective-permute-start.27 = (bf16[384,2048]{1,0:T(8,128)(2,1)S(1)}, bf16[384,2048]{1,0:T(8,128)(2,1)S(1)}, u32[]{:S(2)}, u32[]{:S(2)}) collective-permute-start(bf16[384,2048]{1,0:T(8,128)(2,1)S(1)} %add_convert_fusion.4), channel_id=1, source_target_pairs={{0,1},{1,2},{2,3},{3,0},{4,5},{5,6},{6,7},{7,4},{8,9},{9,10},{10,1... | collective-permute-start | bytes 4718600 | tf_op jit(solution)/shard_map/backs/ppermute | solution.py:156
  464.8 50.2 %collective-permute-start.29 = (bf16[512,4224]{1,0:T(8,128)(2,1)}, bf16[512,4224]{1,0:T(8,128)(2,1)}, u32[]{:S(2)}, u32[]{:S(2)}) collective-permute-start(bf16[512,4224]{1,0:T(8,128)(2,1)} %get-tuple-element.248), channel_id=1, source_target_pairs={{0,16},{4,12},{8,24},{12,4},{16,0},{20,28},{24,8},{28,20},{1,17},{... | collective-permute-start | bytes 12976136 | tf_op jit(solution)/shard_map/ffn_g/ppermute | solution.py:55
  464.8 39.0 %collective-permute-start.28 = (bf16[384,2048]{1,0:T(8,128)(2,1)}, bf16[384,2048]{1,0:T(8,128)(2,1)S(1)}, u32[]{:S(2)}, u32[]{:S(2)}) collective-permute-start(bf16[384,2048]{1,0:T(8,128)(2,1)} %get-tuple-element.247), channel_id=1, source_target_pairs={{0,1},{1,2},{2,3},{3,0},{4,5},{5,6},{6,7},{7,4},{8,9},{9,10},{10,1... | collective-permute-start | bytes 4718600 | tf_op jit(solution)/shard_map/parts/ppermute | solution.py:156
  519.1 26.9 %collective-permute-start.31 = (bf16[256,4224]{1,0:T(8,128)(2,1)}, bf16[256,4224]{1,0:T(8,128)(2,1)S(1)}, u32[]{:S(2)}, u32[]{:S(2)}) collective-permute-start(bf16[256,4224]{1,0:T(8,128)(2,1)} %get-tuple-element.330), channel_id=1, source_target_pairs={{0,8},{4,20},{8,0},{12,28},{16,24},{20,4},{24,16},{28,12},{1,9},{5... | collective-permute-start | bytes 6488072 | tf_op jit(solution)/shard_map/ffn_g/ppermute | solution.py:55
  520.8 18.4 %collective-permute-start.30 = (bf16[1024,1024]{1,0:T(8,128)(2,1)}, bf16[1024,1024]{1,0:T(8,128)(2,1)S(1)}, u32[]{:S(2)}, u32[]{:S(2)}) collective-permute-start(bf16[1024,1024]{1,0:T(8,128)(2,1)} %attend_weights.5), channel_id=1, source_target_pairs={{0,4},{4,0},{8,12},{12,8},{16,20},{20,16},{24,28},{28,24},{1,5},{5... | collective-permute-start | bytes 6291464 | tf_op jit(solution)/shard_map/attn_g_1/ppermute | solution.py:59
  522.6 38.9 %collective-permute-start.32 = (bf16[384,2048]{1,0:T(8,128)(2,1)}, bf16[384,2048]{1,0:T(8,128)(2,1)}, u32[]{:S(2)}, u32[]{:S(2)}) collective-permute-start(bf16[384,2048]{1,0:T(8,128)(2,1)} %add_convert_fusion.3), channel_id=1, source_target_pairs={{0,1},{1,2},{2,3},{3,0},{4,5},{5,6},{6,7},{7,4},{8,9},{9,10},{10,1... | collective-permute-start | bytes 4718600 | tf_op jit(solution)/shard_map/parts/ppermute | solution.py:156
  561.5 18.8 %collective-permute-start.33 = (bf16[1024,1024]{1,0:T(8,128)(2,1)}, bf16[1024,1024]{1,0:T(8,128)(2,1)S(1)}, u32[]{:S(2)}, u32[]{:S(2)}) collective-permute-start(bf16[1024,1024]{1,0:T(8,128)(2,1)} %get-tuple-element.266), channel_id=1, source_target_pairs={{0,4},{4,0},{8,12},{12,8},{16,20},{20,16},{24,28},{28,24},{1,5},{5... | collective-permute-start | bytes 6291464 | tf_op jit(solution)/shard_map/attn_g_2/ppermute | solution.py:59
  563.6 38.8 %collective-permute-start.35 = (bf16[384,2048]{1,0:T(8,128)(2,1)S(1)}, bf16[384,2048]{1,0:T(8,128)(2,1)}, u32[]{:S(2)}, u32[]{:S(2)}) collective-permute-start(bf16[384,2048]{1,0:T(8,128)(2,1)S(1)} %add_convert_fusion.2), channel_id=1, source_target_pairs={{0,1},{1,2},{2,3},{3,0},{4,5},{5,6},{6,7},{7,4},{8,9},{9,10},{10,1... | collective-permute-start | bytes 4718600 | tf_op jit(solution)/shard_map/parts/ppermute | solution.py:156
  563.6 16.7 %collective-permute-start.34 = (bf16[512,1024]{1,0:T(8,128)(2,1)}, bf16[512,1024]{1,0:T(8,128)(2,1)S(1)}, u32[]{:S(2)}, u32[]{:S(2)}) collective-permute-start(bf16[512,1024]{1,0:T(8,128)(2,1)} %get-tuple-element.267), channel_id=1, source_target_pairs={{0,16},{4,12},{8,24},{12,4},{16,0},{20,28},{24,8},{28,20},{1,17},{... | collective-permute-start | bytes 3145736 | tf_op jit(solution)/shard_map/attn_g_1/ppermute | solution.py:55
  602.3 19.0 %collective-permute-start.36 = (bf16[1024,1024]{1,0:T(8,128)(2,1)}, bf16[1024,1024]{1,0:T(8,128)(2,1)S(1)}, u32[]{:S(2)}, u32[]{:S(2)}) collective-permute-start(bf16[1024,1024]{1,0:T(8,128)(2,1)} %get-tuple-element.286), channel_id=1, source_target_pairs={{0,4},{4,0},{8,12},{12,8},{16,20},{20,16},{24,28},{28,24},{1,5},{5... | collective-permute-start | bytes 6291464 | tf_op jit(solution)/shard_map/attn_g_3/ppermute | solution.py:59
  603.3 18.0 %collective-permute-start.37 = (bf16[256,1024]{1,0:T(8,128)(2,1)}, bf16[256,1024]{1,0:T(8,128)(2,1)S(1)}, u32[]{:S(2)}, u32[]{:S(2)}) collective-permute-start(bf16[256,1024]{1,0:T(8,128)(2,1)} %add_convert_fusion.18), channel_id=1, source_target_pairs={{0,8},{4,20},{8,0},{12,28},{16,24},{20,4},{24,16},{28,12},{1,9},{5... | collective-permute-start | bytes 1572872 | tf_op jit(solution)/shard_map/attn_g_1/ppermute | solution.py:55
  603.7 49.0 %collective-permute-start.41 = (bf16[512,1024]{1,0:T(8,128)(2,1)}, bf16[512,1024]{1,0:T(8,128)(2,1)S(1)}, u32[]{:S(2)}, u32[]{:S(2)}) collective-permute-start(bf16[512,1024]{1,0:T(8,128)(2,1)} %get-tuple-element.293), channel_id=1, source_target_pairs={{0,16},{4,12},{8,24},{12,4},{16,0},{20,28},{24,8},{28,20},{1,17},{... | collective-permute-start | bytes 3145736 | tf_op jit(solution)/shard_map/attn_g_2/ppermute | solution.py:55
  622.7 29.9 %collective-permute-start.42 = (bf16[256,1024]{1,0:T(8,128)(2,1)}, bf16[256,1024]{1,0:T(8,128)(2,1)S(1)}, u32[]{:S(2)}, u32[]{:S(2)}) collective-permute-start(bf16[256,1024]{1,0:T(8,128)(2,1)} %add_convert_fusion.16), channel_id=1, source_target_pairs={{0,1},{1,2},{2,3},{3,0},{4,5},{5,6},{6,7},{7,4},{8,9},{9,10},{10,1... | collective-permute-start | bytes 1572872 | tf_op jit(solution)/shard_map/attn_g_ring/ppermute | solution.py:156
  623.6 21.6 %collective-permute-start.38 = (bf16[384,256]{1,0:T(8,128)(2,1)}, bf16[384,256]{1,0:T(8,128)(2,1)S(1)}, u32[]{:S(2)}, u32[]{:S(2)}) collective-permute-start(bf16[384,256]{1,0:T(8,128)(2,1)} %get-tuple-element.343), channel_id=1, source_target_pairs={{0,3},{1,0},{2,1},{3,2},{4,7},{5,4},{6,5},{7,6},{8,11},{9,8},{10,9... | collective-permute-start | bytes 589832 | tf_op jit(solution)/shard_map/kv_g/ppermute | solution.py:160
  627.4 25.3 %collective-permute-start.39 = (bf16[384,256]{1,0:T(8,128)(2,1)}, bf16[384,256]{1,0:T(8,128)(2,1)S(1)}, u32[]{:S(2)}, u32[]{:S(2)}) collective-permute-start(bf16[384,256]{1,0:T(8,128)(2,1)} %get-tuple-element.342), channel_id=1, source_target_pairs={{0,2},{1,3},{2,0},{3,1},{4,6},{5,7},{6,4},{7,5},{8,10},{9,11},{10,... | collective-permute-start | bytes 589832 | tf_op jit(solution)/shard_map/kv_g/ppermute | solution.py:160
  627.4 25.3 %collective-permute-start.40 = (bf16[384,256]{1,0:T(8,128)(2,1)}, bf16[384,256]{1,0:T(8,128)(2,1)}, u32[]{:S(2)}, u32[]{:S(2)}) collective-permute-start(bf16[384,256]{1,0:T(8,128)(2,1)} %get-tuple-element.341), channel_id=1, source_target_pairs={{0,1},{1,2},{2,3},{3,0},{4,5},{5,6},{6,7},{7,4},{8,9},{9,10},{10,1... | collective-permute-start | bytes 589832 | tf_op jit(solution)/shard_map/kv_g/ppermute | solution.py:160
  653.7 20.6 %collective-permute-start.43 = (bf16[1024,1024]{1,0:T(8,128)(2,1)}, bf16[1024,1024]{1,0:T(8,128)(2,1)S(1)}, u32[]{:S(2)}, u32[]{:S(2)}) collective-permute-start(bf16[1024,1024]{1,0:T(8,128)(2,1)} %get-tuple-element.304), channel_id=1, source_target_pairs={{0,4},{4,0},{8,12},{12,8},{16,20},{20,16},{24,28},{28,24},{1,5},{5... | collective-permute-start | bytes 6291464 | tf_op jit(solution)/shard_map/attn_g_0/ppermute | solution.py:59
  653.7 20.6 %collective-permute-start.45 = (bf16[512,1024]{1,0:T(8,128)(2,1)}, bf16[512,1024]{1,0:T(8,128)(2,1)S(1)}, u32[]{:S(2)}, u32[]{:S(2)}) collective-permute-start(bf16[512,1024]{1,0:T(8,128)(2,1)} %get-tuple-element.307), channel_id=1, source_target_pairs={{0,16},{4,12},{8,24},{12,4},{16,0},{20,28},{24,8},{28,20},{1,17},{... | collective-permute-start | bytes 3145736 | tf_op jit(solution)/shard_map/attn_g_3/ppermute | solution.py:55
  657.5 15.2 %collective-permute-start.44 = (bf16[256,1024]{1,0:T(8,128)(2,1)}, bf16[256,1024]{1,0:T(8,128)(2,1)}, u32[]{:S(2)}, u32[]{:S(2)}) collective-permute-start(bf16[256,1024]{1,0:T(8,128)(2,1)} %add_convert_fusion.15), channel_id=1, source_target_pairs={{0,8},{4,20},{8,0},{12,28},{16,24},{20,4},{24,16},{28,12},{1,9},{5... | collective-permute-start | bytes 1572872 | tf_op jit(solution)/shard_map/attn_g_2/ppermute | solution.py:55
  682.3 20.5 %collective-permute-start.47 = (bf16[512,1024]{1,0:T(8,128)(2,1)S(1)}, bf16[512,1024]{1,0:T(8,128)(2,1)S(1)}, u32[]{:S(2)}, u32[]{:S(2)}) collective-permute-start(bf16[512,1024]{1,0:T(8,128)(2,1)S(1)} %slice.178), channel_id=1, source_target_pairs={{0,16},{4,12},{8,24},{12,4},{16,0},{20,28},{24,8},{28,20},{1,17},{... | collective-permute-start | bytes 3145736 | tf_op jit(solution)/shard_map/attn_g_0/ppermute | solution.py:55
  684.2 15.1 %collective-permute-start.46 = (bf16[1024,384]{1,0:T(8,128)(2,1)S(1)}, bf16[1024,384]{1,0:T(8,128)(2,1)S(1)}, u32[]{:S(2)}, u32[]{:S(2)}) collective-permute-start(bf16[1024,384]{1,0:T(8,128)(2,1)S(1)} %copy-done.41), channel_id=1, source_target_pairs={{0,4},{4,0},{8,12},{12,8},{16,20},{20,16},{24,28},{28,24},{1,5},{5... | collective-permute-start | bytes 2359304 | tf_op jit(solution)/shard_map/small_g/ppermute | solution.py:59
  687.6 20.1 %collective-permute-start.55 = (bf16[256,1024]{1,0:T(8,128)(2,1)S(1)}, bf16[256,1024]{1,0:T(8,128)(2,1)S(1)}, u32[]{:S(2)}, u32[]{:S(2)}) collective-permute-start(bf16[256,1024]{1,0:T(8,128)(2,1)S(1)} %add_convert_fusion.10), channel_id=1, source_target_pairs={{0,1},{1,2},{2,3},{3,0},{4,5},{5,6},{6,7},{7,4},{8,9},{9,10},{10,1... | collective-permute-start | bytes 1572872 | tf_op jit(solution)/shard_map/attn_g_ring/ppermute | solution.py:156
  719.1 21.2 %collective-permute-start.56 = (bf16[256,1024]{1,0:T(8,128)(2,1)S(1)}, bf16[256,1024]{1,0:T(8,128)(2,1)S(1)}, u32[]{:S(2)}, u32[]{:S(2)}) collective-permute-start(bf16[256,1024]{1,0:T(8,128)(2,1)S(1)} %add_convert_fusion.7), channel_id=1, source_target_pairs={{0,1},{1,2},{2,3},{3,0},{4,5},{5,6},{6,7},{7,4},{8,9},{9,10},{10,1... | collective-permute-start | bytes 1572872 | tf_op jit(solution)/shard_map/attn_g_ring/ppermute | solution.py:156
  722.9 20.8 %collective-permute-start.52 = (bf16[256,384]{1,0:T(8,128)(2,1)S(1)}, bf16[256,384]{1,0:T(8,128)(2,1)S(1)}, u32[]{:S(2)}, u32[]{:S(2)}) collective-permute-start(bf16[256,384]{1,0:T(8,128)(2,1)S(1)} %add_convert_fusion.21), channel_id=1, source_target_pairs={{0,1},{1,2},{2,3},{3,0},{4,5},{5,6},{6,7},{7,4},{8,9},{9,10},{10,1... | collective-permute-start | bytes 589832 | tf_op jit(solution)/shard_map/small_g_ring/ppermute | solution.py:160
  722.9 21.4 %collective-permute-start.53 = (bf16[256,384]{1,0:T(8,128)(2,1)S(1)}, bf16[256,384]{1,0:T(8,128)(2,1)S(1)}, u32[]{:S(2)}, u32[]{:S(2)}) collective-permute-start(bf16[256,384]{1,0:T(8,128)(2,1)S(1)} %add_convert_fusion.21), channel_id=1, source_target_pairs={{0,2},{1,3},{2,0},{3,1},{4,6},{5,7},{6,4},{7,5},{8,10},{9,11},{10,... | collective-permute-start | bytes 589832 | tf_op jit(solution)/shard_map/small_g_ring/ppermute | solution.py:160
  723.7 20.6 %collective-permute-start.54 = (bf16[256,384]{1,0:T(8,128)(2,1)S(1)}, bf16[256,384]{1,0:T(8,128)(2,1)S(1)}, u32[]{:S(2)}, u32[]{:S(2)}) collective-permute-start(bf16[256,384]{1,0:T(8,128)(2,1)S(1)} %add_convert_fusion.21), channel_id=1, source_target_pairs={{0,3},{1,0},{2,1},{3,2},{4,7},{5,4},{6,5},{7,6},{8,11},{9,8},{10,9... | collective-permute-start | bytes 589832 | tf_op jit(solution)/shard_map/small_g_ring/ppermute | solution.py:160
  (53 other events, 642.8 us)

commit v3 on v2

--- a/solution.py
+++ b/solution.py
@@ -74,9 +74,11 @@
     return table
 
 
-def gather_steps(shard, ndp):
+def gather_steps(shard, ndp, settle=False):
     moved = yield [plane_swap(shard, ndp, 0)]
     pieces = [jnp.concatenate([shard, moved[0]], axis=0)]
+    if settle:
+        pieces = yield pieces
     for step in range(1, len(bit_orders(ndp)[0])):
         pieces = pieces + (yield [plane_swap(piece, ndp, step) for piece in pieces])
     pieces = pieces + (yield [core_swap(piece, ndp) for piece in pieces])
@@ -110,10 +112,13 @@
     yield (low, come)
 
 
-def ring_steps(parts, nt_):
+def ring_steps(parts, nt_, ahead=None):
     moving = yield [ring_next(parts[1], nt_)]
     for place in range(2, nt_):
-        moving = yield [ring_next(add_low(moving[0], parts[place]), nt_)]
+        total = add_low(moving[0], parts[place])
+        if ahead:
+            total, ahead[-1] = tie(total, ahead[-1])
+        moving = yield [ring_next(total, nt_)]
     yield (moving[0], parts[0])
 
 
@@ -1178,11 +1183,11 @@
     near_flow = Flow("attn_w_near", gather_steps(near_item, ndp))
     attn_flow = Flow("attn_w_ring", ring_gather_steps(ring_item, nz))
     grad_low = move_columns(d_out, table, rows)
-    (ring_item,) = meet([ring_item], [near_flow, attn_flow])
-    near_flow.go(len(bit_orders(ndp)[0]) - 2)
     ffn_pack = do_pack_ffn(w_gate, w_up, w_down)
     grad_low, bias, ffn_pack = meet([grad_low, bias, ffn_pack], [near_flow, attn_flow])
-    ffn_flow = Flow("ffn_w", gather_steps(ffn_pack, ndp))
+    near_flow.go(len(bit_orders(ndp)[0]) - 2)
+    grad_low, ffn_pack = meet([grad_low, ffn_pack], [near_flow, attn_flow])
+    ffn_flow = Flow("ffn_w", gather_steps(ffn_pack, ndp, True))
     near = list(near_flow.finish())
     near = meet(near, [attn_flow])
     tokens_low, normed, normed_turned, kv_own, gain_rows = do_enter(
@@ -1195,21 +1200,21 @@
     far_flow = Flow("attn_w_far", gather_steps(jnp.concatenate(attn_ring, axis=1), ndp))
     grad_flow = Flow("grad_ring", ring_gather_steps(grad_low, nz))
 
-    normed, *kv_ring = meet([normed] + kv_ring, [far_flow], [ffn_flow])
+    normed, *kv_ring = meet([normed] + kv_ring, [far_flow, ffn_flow])
+    normed, *ffn_flow.held = tie(normed, *ffn_flow.held)
     *kept_near, after_attn = do_attend(normed, bias, tokens_low, kv_ring, near, 1)
     grad_first = grad_flow.held[0]
     (after_attn,) = meet([after_attn], [grad_flow])
     (after_attn,) = meet([after_attn], [far_flow, ffn_flow])
     far = far_flow.finish()
     *kept_far, after_attn = do_attend(normed, bias, after_attn, kv_ring, far, nz - 1)
-    (after_attn,) = meet([after_attn], [ffn_flow, grad_flow])
-    ffn_w = ffn_flow.finish()
     grad_ring = [grad_low, grad_first]
     ffn_scale = lax.rsqrt(jnp.mean(after_attn * after_attn, axis=-1, keepdims=True) + norm_eps)
     ffn_own = (after_attn * ffn_scale * ffn_gain).astype(BF16)
 
     ring_flow = Flow("ffn_ring", ring_gather_steps(ffn_own, nz))
-    ffn_ring, acts, parts, backs = [ffn_own], [], [], []
+    ffn_ring, acts, parts, backs = meet([ffn_own], [ffn_flow, grad_flow]), [], [], []
+    ffn_w = ffn_flow.finish()
     early = nz // 2 + 1
     backs_flow = None
     for block in range(nz):
@@ -1218,30 +1223,31 @@
             ring_flow.held = [come]
             ring_flow.go()
             ffn_ring.append(come)
-            if block == 2:
-                (ffn_ring[-1],) = meet(ffn_ring[-1:], [], [grad_flow])
-                grad_ring = grad_flow.finish()
         if block == early:
             first = (ffn_ring[:early], grad_ring[:early], acts[:early])
             (send,) = do_ffn_weights(*first, 1, 1, width // 2)
             kept = do_ffn_weights(*first, 0, 2, width // 4)
-            (send,) = meet([send], [backs_flow] if block > 2 else [])
             ffn_ring[-1], send, *kept = tie(ffn_ring[-1], send, *kept)
-        elif block > 2:
+        elif block > early:
             (ffn_ring[-1],) = meet(ffn_ring[-1:], [backs_flow])
+        if block == 2:
+            grad_ring = grad_flow.finish()
         act, part, back = do_ffn(ffn_ring[block], grad_ring[block], ffn_w)
         acts.append(act)
         parts.append(part)
         backs.append(back)
         if block == 1:
-            backs_flow = Flow("backs", ring_steps(backs, nz))
-
-    (acts[-1],) = meet([acts[-1]], [backs_flow])
+            backs_flow = Flow("backs", ring_steps(backs, nz, acts))
+
+    acts[-1], *backs_flow.held = tie(acts[-1], *backs_flow.held)
+    backs_flow.go()
     rest = (ffn_ring[early:], grad_ring[early:], acts[early:])
     (send,) = do_ffn_weights(*rest, 1, 1, width // 2, ([send],))
+    parts[1], send = meet([parts[1], send], [backs_flow])
     come = scoped("ffn_g", core_swap, send, ndp)
     made = do_ffn_weights(*rest, 0, 2, width // 4, (kept, come))
-    parts[1], *made = meet([parts[1], *made], [backs_flow])
+    tied = list(tie(*made, *backs_flow.held))
+    made, backs_flow.held = tied[: len(made)], tied[len(made) :]
     after_grad, branch, branch_turned, ffn_term = do_turn(
         *backs_flow.finish(), grad_low, after_attn, gain_rows
     )
@@ -1250,11 +1256,19 @@
 
     order = list(range(1, nz)) + [0]
     flows = [None] * nz
+    done = [None] * nz
     sums = None
     for turn, block in enumerate(order):
         stored, pieces, at = (kept_far, far, block - 1) if block else (kept_near, near, 0)
         if turn > 0:
-            branch, *made = meet([branch, *made], [part_flow] + [ffn_flow] * (turn == 1))
+            due = [part_flow] + ([flows[nz - 3]] if turn == nz - 1 else [])
+            branch, *made = meet([branch, *made], due)
+            if turn == nz - 1:
+                for place in range(1, nz - 2):
+                    done[place] = add_low(*flows[place].finish())
+                ring_flow = Flow("attn_g_ring", ring_steps(done, nz))
+                for _ in range(nz - 4):
+                    ring_flow.go()
             sent = scoped(f"attn_g_{order[turn - 1]}", core_swap, made[0], ndp)
             if turn > 1:
                 flow = Flow(f"attn_g_{order[turn - 2]}", chip_steps(*made[1:], ndp))
@@ -1264,15 +1278,14 @@
         )
         sums = (kv_acc, normed_grad)
         due = [flow for flow in flows if flow is not None]
-        if turn == 1:
-            due.append(ffn_flow)
-        if turn == nz - 1:
-            due.remove(flow)
+        due += [ffn_flow] if turn else []
         this = (query_grad, stored[1], at)
         if turn == 0:
             made = do_attend_weights(normed_turned, branch_turned, this)
         else:
-            query_grad, sent = meet([query_grad, sent], due)
+            waiting = [flow, ring_flow] if turn == nz - 1 else []
+            due = [item for item in due if item not in waiting]
+            query_grad, sent = meet([query_grad, sent], due, waiting)
             this = (query_grad, stored[1], at)
             made, both = do_attend_weights(normed_turned, branch_turned, this, (*back, sent))
             made = [made, both[: width // 4], both[width // 4 :]]
@@ -1281,16 +1294,12 @@
     kv_come = [
         scoped("kv_g", shift, kv_low[by * own : (by + 1) * own], nz, -by) for by in range(1, nz)
     ]
-    done = [None] * nz
-    for place in range(1, nz - 2):
-        done[place] = add_low(*flows[place].finish())
-    ring_flow = Flow("attn_g_ring", ring_steps(done, nz))
-    for _ in range(nz - 4):
-        ring_flow.go()
-    tied = meet([*made, *kv_come], [flows[nz - 2], part_flow], [ring_flow])
-    (send, *made), kv_come = tied[:3], tied[3:]
-    sent = scoped("attn_g_0", core_swap, send, ndp)
-    flows[nz - 1] = Flow(f"attn_g_{nz - 1}", chip_steps(*made, ndp))
+    sent = scoped("attn_g_0", core_swap, made[0], ndp)
+    flows[nz - 1] = Flow(f"attn_g_{nz - 1}", chip_steps(*made[1:], ndp))
+    (both,) = do_attend_weights(normed_turned, branch_turned, None, (*back, sent))
+    low, high = both[: width // 4], both[width // 4 :]
+    low, high, *kv_come = meet([low, high, *kv_come], [flows[nz - 2], part_flow, ffn_flow])
+    flows[0] = Flow("attn_g_0", chip_steps(low, high, ndp))
     input_grad, keep, send = do_leave(
         table,
         kv_acc,
@@ -1306,12 +1315,10 @@
         near,
         2 * heads_w,
     )
-    keep, send, sent = meet([keep, send, sent], [flows[nz - 2], flows[nz - 1]])
+    small_flow = Flow("small_g", scatter_steps(keep, send, ndp))
+    meet([], [flows[nz - 2], flows[nz - 1], flows[0]])
     done[nz - 2] = add_low(*flows[nz - 2].finish())
-    small_flow = Flow("small_g", scatter_steps(keep, send, ndp))
     (done[nz - 2],) = meet([done[nz - 2]], [ring_flow])
-    (both,) = do_attend_weights(normed_turned, branch_turned, None, (*back, sent))
-    flows[0] = Flow("attn_g_0", chip_steps(both[: width // 4], both[width // 4 :], ndp))
 
     meet([], [small_flow, flows[0], flows[nz - 1]])
     done[nz - 1] = add_low(*flows[nz - 1].finish())

time: 757 us -> 692 us (0.914)
  waiting for transfers between devices: 300 us -> 230 us
  starting transfers between devices: 36.1 us -> 49.4 us
  local copies, waits for them, and re-layouts: 35.6 us -> 24.8 us
    ppermute x18, waiting for transfers between devices: 183 us -> 152 us  [ring_next(): lax.ppermute(array, 'tensor', [(i, (i + 1) % nt_) for i in range(nt_)])]
    ppermute x18, waiting for transfers between devices: 61.9 us -> 37 us  [plane_swap(): lax.ppermute(array, 'dp', [(d, d ^ orders[d & 1][step]) for d in range(nd...]
    ppermute x18, starting transfers between devices: 2.84 us -> 12.9 us  [ring_next(): lax.ppermute(array, 'tensor', [(i, (i + 1) % nt_) for i in range(nt_)])]
    ppermute x9, waiting for transfers between devices: 28.7 us -> 19.2 us  [shift(): lax.ppermute(array, 'tensor', [(i, (i + by) % nt_) for i in range(nt_)])]
    unnamed x92 -> x85, local copies, waits for them, and re-layouts: 16.1 us -> 8.62 us
  transfers between devices with their start and end apart: 57 -> 57, of which waited for: 32 -> 29; matrix products, arithmetic and copies ran while one was open for 5% -> 7% of each run, Pallas kernels for 44% -> 49%
where the time goes in v3:
time: 692 us; the launch traced here: 684 us
  Pallas kernels  344 us (50%)
  waiting for transfers between devices  230 us (33%)
  starting transfers between devices  49.4 us (7%)
  other arithmetic  34.5 us (5%)
  local copies, waits for them, and re-layouts  24.8 us (4%)
    ppermute x18, waiting for transfers between devices, ring_next(): lax.ppermute(array, 'tensor', [(i, (i + 1) % nt_) for i in range(nt_)])  152 us
    pallas_call x4, Pallas kernels, ffn_block(): pl.pallas_call(lambda *refs: ffn_kernel(count, steps, last, refs), out_sh...  85.8 us
    pallas_call x4, Pallas kernels, ffn_weights(): pl.pallas_call(lambda *refs: ffn_weights_kernel(blocks, count, steps, las...  67.4 us
    pallas_call x4, Pallas kernels, attend_back_block(): pl.pallas_call(lambda *refs: attend_back_kernel(count, blocks, first, ref...  64.1 us
    pallas_call x2, Pallas kernels, attend_block(): pl.pallas_call(lambda *refs: attend_kernel(count, blocks, refs), out_shap...  44.3 us
    ppermute x18, waiting for transfers between devices, plane_swap(): lax.ppermute(array, 'dp', [(d, d ^ orders[d & 1][step]) for d in range(nd...  37 us
    pallas_call x5, Pallas kernels, attend_weights(): pl.pallas_call(lambda *refs: attend_weights_kernel(int(send is not None),...  31.2 us
    ppermute x12, waiting for transfers between devices, core_swap(): return lax.ppermute(array, 'dp', [(d, d ^ 1) for d in range(ndp)])  22.1 us
  transfers between devices with their start and end apart: 57, of which 29 were waited for; matrix products, arithmetic and copies ran while one was open for 7% of the time, Pallas kernels for 49%

profile of v3, /device:TPU:0, one launch (start us, length us, event | category | flops | bytes accessed | tf_op | source)
XLA Modules:
  0.0 684.1 jit_solution(13746648960991088016)
XLA Ops:
  12.3 6.2 take_columns.1.refs_1_.refs_3_.given_ref
  27.2 13.4 %collective-permute-done.3 = bf16[256,1024]{1,0:T(8,128)(2,1)S(1)} collective-permute-done((bf16[256,1024]{1,0:T(8,128)(2,1)S(1)}, bf16[256,1024]{1,0:T(8,128)(2,1)S(1)}, u32[]{:S(2)}, u32[]{:S(2)}) %collective-permute-start.3) | collective-permute-done | bytes 524320 | tf_op jit(solution)/shard_map/attn_w_ring/ppermute | solution.py:161
  48.0 11.3 %collective-permute-done.6 = bf16[256,1024]{1,0:T(8,128)(2,1)S(1)} collective-permute-done((bf16[256,1024]{1,0:T(8,128)(2,1)S(1)}, bf16[256,1024]{1,0:T(8,128)(2,1)S(1)}, u32[]{:S(2)}, u32[]{:S(2)}) %collective-permute-start.6) | collective-permute-done | bytes 524320 | tf_op jit(solution)/shard_map/attn_w_ring/ppermute | solution.py:161
  61.4 5.5 enter.1
  70.8 6.1 collective-permute-done.7.refs_4_.refs_6_.refs_8_.refs_1_
  76.9 7.3 %collective-permute-done.8.refs_5_.refs_7_.refs_9_.refs_2_ = bf16[384,256]{1,0:T(8,128)(2,1)S(1)} collective-permute-done((bf16[384,256]{1,0:T(8,128)(2,1)}, bf16[384,256]{1,0:T(8,128)(2,1)S(1)}, u32[]{:S(2)}, u32[]{:S(2)}) %collective-permute-start.8) | collective-permute-done | bytes 196640 | tf_op jit(solution)/shard_map/kv/ppermute | solution.py:165
  84.2 4.5 collective-permute-done.10
  94.1 4.6 pad_maximum_fusion.refs_2_
  98.7 13.6 %attend.2 = (bf16[384,512]{1,0:T(8,128)(2,1)}, bf16[384,512]{1,0:T(8,128)(2,1)}, f32[2,1,768]{2,1,0:T(1,128)}, f32[384,2048]{1,0:T(8,128)}) custom-call(bf16[384,2048]{1,0:T(8,128)(2,1)} %get-tuple-element.194.refs_0_.refs_7_, f32[1536,384]{1,0:T(8,128)} %and_select_fusion.refs_1_, bf16[384,2048]{1,0:T(8,128)(2,1)} %get-tuple-element.196.refs_2_.refs_8_, ...), custom_call_target="tpu_custom_call" | custom-call | flops 2818572288 | bytes 14000000 | tf_op jit(solution)/shard_map/attend/pallas_call | solution.py:412
  112.3 16.5 %collective-permute-done.12.refs_1_.refs_4_ = bf16[384,2048]{1,0:T(8,128)(2,1)} collective-permute-done((bf16[384,2048]{1,0:T(8,128)(2,1)S(1)}, bf16[384,2048]{1,0:T(8,128)(2,1)}, u32[]{:S(2)}, u32[]{:S(2)}) %collective-permute-start.12) | collective-permute-done | bytes 1572896 | tf_op jit(solution)/shard_map/grad_ring/ppermute | solution.py:161
  134.8 30.7 %attend.3 = (bf16[384,1536]{1,0:T(8,128)(2,1)}, bf16[384,1536]{1,0:T(8,128)(2,1)}, f32[6,1,768]{2,1,0:T(1,128)}, f32[384,2048]{1,0:T(8,128)}) custom-call(bf16[384,2048]{1,0:T(8,128)(2,1)} %get-tuple-element.194.refs_0_.refs_7_, f32[1536,384]{1,0:T(8,128)} %and_select_fusion.refs_1_, f32[384,2048]{1,0:T(8,128)} %get-tuple-element.206.refs_2_, ...), custom_call_target="tpu_custom_call" | custom-call | flops 8455716864 | bytes 14000000 | tf_op jit(solution)/shard_map/attend/pallas_call | solution.py:412
  169.9 9.1 %collective-permute-done.17.refs_3_ = bf16[512,4224]{1,0:T(8,128)(2,1)} collective-permute-done((bf16[512,4224]{1,0:T(8,128)(2,1)}, bf16[512,4224]{1,0:T(8,128)(2,1)}, u32[]{:S(2)}, u32[]{:S(2)}) %collective-permute-start.17) | collective-permute-done | bytes 4325408 | tf_op jit(solution)/shard_map/ffn_w/ppermute | solution.py:55
  180.2 6.6 collective-permute-done.20.refs_5_
  186.7 21.4 %ffn_block.4 = (bf16[384,4224]{1,0:T(8,128)(2,1)}, bf16[384,2048]{1,0:T(8,128)(2,1)}, bf16[384,2048]{1,0:T(8,128)(2,1)}) custom-call(bf16[384,2048]{1,0:T(8,128)(2,1)} %copy-done.18, bf16[384,2048]{1,0:T(8,128)(2,1)} %take_columns.1.refs_1_.refs_3_.given_ref, bf16[512,4224]{1,0:T(8,128)(2,1)} %pad_maximum_fusion.refs_2_, ...), custom_call_target="tpu_custom_call" | custom-call | flops 13287555072 | bytes 26738688 | tf_op jit(solution)/shard_map/ffn_block/pallas_call | solution.py:635
  208.1 9.5 %collective-permute-done.16.refs_0_.refs_1_ = bf16[384,2048]{1,0:T(8,128)(2,1)S(1)} collective-permute-done((bf16[384,2048]{1,0:T(8,128)(2,1)S(1)}, bf16[384,2048]{1,0:T(8,128)(2,1)S(1)}, u32[]{:S(2)}, u32[]{:S(2)}) %collective-permute-start.16) | collective-permute-done | bytes 1572896 | tf_op jit(solution)/shard_map/ffn_ring/ppermute | solution.py:161
  218.8 21.4 %ffn_block.5 = (bf16[384,4224]{1,0:T(8,128)(2,1)}, bf16[384,2048]{1,0:T(8,128)(2,1)}, bf16[384,2048]{1,0:T(8,128)(2,1)}) custom-call(bf16[384,2048]{1,0:T(8,128)(2,1)} %copy-done.38, bf16[384,2048]{1,0:T(8,128)(2,1)} %collective-permute-done.12.refs_1_.refs_4_, bf16[512,4224]{1,0:T(8,128)(2,1)} %pad_maximum_fusion.refs_2_, ...), custom_call_target="tpu_custom_call" | custom-call | flops 13287555072 | bytes 26738688 | tf_op jit(solution)/shard_map/ffn_block/pallas_call | solution.py:635
  240.3 15.5 %collective-permute-done.21.refs_0_.refs_2_ = bf16[384,2048]{1,0:T(8,128)(2,1)} collective-permute-done((bf16[384,2048]{1,0:T(8,128)(2,1)S(1)}, bf16[384,2048]{1,0:T(8,128)(2,1)}, u32[]{:S(2)}, u32[]{:S(2)}) %collective-permute-start.21) | collective-permute-done | bytes 1572896 | tf_op jit(solution)/shard_map/ffn_ring/ppermute | solution.py:161
  256.6 21.4 %ffn_block.6 = (bf16[384,4224]{1,0:T(8,128)(2,1)}, bf16[384,2048]{1,0:T(8,128)(2,1)}, bf16[384,2048]{1,0:T(8,128)(2,1)}) custom-call(bf16[384,2048]{1,0:T(8,128)(2,1)} %collective-permute-done.21.refs_0_.refs_2_, bf16[384,2048]{1,0:T(8,128)(2,1)} %collective-permute-done.18.refs_1_.refs_5_, bf16[512,4224]{1,0:T(8,128)(2,1)} %pad_maximum_fusion.refs_2_, ...), custom_call_target="tpu_custom_call" | custom-call | flops 13287555072 | bytes 26738688 | tf_op jit(solution)/shard_map/ffn_block/pallas_call | solution.py:635
  278.0 17.1 %collective-permute-done.22.refs_0_ = bf16[384,2048]{1,0:T(8,128)(2,1)S(1)} collective-permute-done((bf16[384,2048]{1,0:T(8,128)(2,1)}, bf16[384,2048]{1,0:T(8,128)(2,1)S(1)}, u32[]{:S(2)}, u32[]{:S(2)}) %collective-permute-start.22) | collective-permute-done | bytes 1572896 | tf_op jit(solution)/shard_map/ffn_ring/ppermute | solution.py:161
  295.1 21.2 %ffn_weights.5 = (bf16[512,4224]{1,0:T(8,128)(2,1)}, bf16[512,4224]{1,0:T(8,128)(2,1)}) custom-call(bf16[384,2048]{1,0:T(8,128)(2,1)} %copy-done.18, bf16[384,2048]{1,0:T(8,128)(2,1)} %copy-done.38, bf16[384,2048]{1,0:T(8,128)(2,1)} %collective-permute-done.21.refs_0_.refs_2_, bf16[384,2048]{1,0:T(8,128)(2,1)} %take_columns.1.refs_1_.refs_3_.given_ref, ...), custom_call_target="tpu_custom_call" | custom-call | flops 9965666304 | bytes 28114944 | tf_op jit(solution)/shard_map/ffn_weights/pallas_call | solution.py:700
  316.3 19.5 %ffn_weights.4.refs_3_ = bf16[1024,4224]{1,0:T(8,128)(2,1)} custom-call(bf16[384,2048]{1,0:T(8,128)(2,1)} %copy-done.18, bf16[384,2048]{1,0:T(8,128)(2,1)} %copy-done.38, bf16[384,2048]{1,0:T(8,128)(2,1)} %collective-permute-done.21.refs_0_.refs_2_, bf16[384,2048]{1,0:T(8,128)(2,1)} %take_columns.1.refs_1_.refs_3_.given_ref, ...), custom_call_target="tpu_custom_call" | custom-call | flops 9965666304 | bytes 18382848 | tf_op jit(solution)/shard_map/ffn_weights/pallas_call | solution.py:700
  337.1 21.6 %ffn_block.7 = (bf16[384,4224]{1,0:T(8,128)(2,1)}, bf16[384,2048]{1,0:T(8,128)(2,1)}, bf16[384,2048]{1,0:T(8,128)(2,1)}) custom-call(bf16[384,2048]{1,0:T(8,128)(2,1)} %copy-done.9, bf16[384,2048]{1,0:T(8,128)(2,1)} %copy-done.10, bf16[512,4224]{1,0:T(8,128)(2,1)} %pad_maximum_fusion.refs_2_, bf16[512,4224]{1,0:T(8,128)(2,1)} %collective-permute-done.17.refs_3_, ...), custom_call_target="tpu_custom_call" | custom-call | flops 13287555072 | bytes 26738688 | tf_op jit(solution)/shard_map/ffn_block/pallas_call | solution.py:635
  362.2 11.4 %ffn_weights.6 = bf16[1024,4224]{1,0:T(8,128)(2,1)} custom-call(bf16[384,2048]{1,0:T(8,128)(2,1)} %copy-done.9, bf16[384,2048]{1,0:T(8,128)(2,1)} %copy-done.10, bf16[384,4224]{1,0:T(8,128)(2,1)} %get-tuple-element.232.refs_2_, bf16[1024,4224]{1,0:T(8,128)(2,1)} %ffn_weights.4.refs_3_), custom_call_target="tpu_custom_call" | custom-call | flops 3321888768 | bytes 11894784 | tf_op jit(solution)/shard_map/ffn_weights/pallas_call | solution.py:700
  373.5 24.9 %collective-permute-done.25 = bf16[384,2048]{1,0:T(8,128)(2,1)S(1)} collective-permute-done((bf16[384,2048]{1,0:T(8,128)(2,1)}, bf16[384,2048]{1,0:T(8,128)(2,1)S(1)}, u32[]{:S(2)}, u32[]{:S(2)}) %collective-permute-start.25) | collective-permute-done | bytes 1572896 | tf_op jit(solution)/shard_map/backs/ppermute | solution.py:161
  399.2 13.1 %collective-permute-done.26.refs_5_.refs_6_ = bf16[1024,4224]{1,0:T(8,128)(2,1)} collective-permute-done((bf16[1024,4224]{1,0:T(8,128)(2,1)}, bf16[1024,4224]{1,0:T(8,128)(2,1)}, u32[]{:S(2)}, u32[]{:S(2)}) %collective-permute-start.26) | collective-permute-done | bytes 8650784 | tf_op jit(solution)/shard_map/ffn_g/ppermute | solution.py:59
  412.3 15.4 %ffn_weights.7 = (bf16[512,4224]{1,0:T(8,128)(2,1)}, bf16[512,4224]{1,0:T(8,128)(2,1)}) custom-call(bf16[384,2048]{1,0:T(8,128)(2,1)} %copy-done.9, bf16[384,2048]{1,0:T(8,128)(2,1)} %copy-done.10, bf16[384,4224]{1,0:T(8,128)(2,1)} %get-tuple-element.232.refs_2_, bf16[512,4224]{1,0:T(8,128)(2,1)} %get-tuple-element.233.refs_3_, ...), custom_call_target="tpu_custom_call" | custom-call | flops 3321888768 | bytes 15138816 | tf_op jit(solution)/shard_map/ffn_weights/pallas_call | solution.py:700
  427.6 10.1 %collective-permute-done.27.come_ref = bf16[384,2048]{1,0:T(8,128)(2,1)S(1)} collective-permute-done((bf16[384,2048]{1,0:T(8,128)(2,1)S(1)}, bf16[384,2048]{1,0:T(8,128)(2,1)S(1)}, u32[]{:S(2)}, u32[]{:S(2)}) %collective-permute-start.27) | collective-permute-done | bytes 1572896 | tf_op jit(solution)/shard_map/backs/ppermute | solution.py:161
  439.3 8.1 %turn.1 = (f32[384,2048]{1,0:T(8,128)}, bf16[384,2048]{1,0:T(8,128)(2,1)}, bf16[2048,384]{1,0:T(8,128)(2,1)}, f32[1,2048]{1,0:T(1,128)}) custom-call(bf16[384,2048]{1,0:T(8,128)(2,1)} %copy-done.22, bf16[384,2048]{1,0:T(8,128)(2,1)} %get-tuple-element.245.part_ref, bf16[384,2048]{1,0:T(8,128)(2,1)} %take_columns.1.refs_1_.refs_3_.given_ref, ...), custom_call_target="tpu_custom_call" | custom-call | bytes 15728640 | tf_op jit(solution)/shard_map/turn/pallas_call | solution.py:733
  447.4 14.9 %attend_back.4 = (bf16[384,512]{1,0:T(8,128)(2,1)}, f32[1536,256]{1,0:T(8,128)}, f32[384,2048]{1,0:T(8,128)}) custom-call(bf16[384,2048]{1,0:T(8,128)(2,1)} %get-tuple-element.286.refs_0_, f32[1536,384]{1,0:T(8,128)} %and_select_fusion.refs_1_, bf16[384,1536]{1,0:T(8,128)(2,1)} %get-tuple-element.249.refs_2_.refs_4_, ...), custom_call_target="tpu_custom_call" | custom-call | flops 4630511616 | bytes 16000000 | tf_op jit(solution)/shard_map/attend_back/pallas_call | solution.py:502
  462.2 5.0 attend_weights.5
  467.2 9.6 %collective-permute-done.28 = bf16[384,2048]{1,0:T(8,128)(2,1)S(1)} collective-permute-done((bf16[384,2048]{1,0:T(8,128)(2,1)S(1)}, bf16[384,2048]{1,0:T(8,128)(2,1)S(1)}, u32[]{:S(2)}, u32[]{:S(2)}) %collective-permute-start.28) | collective-permute-done | bytes 1572896 | tf_op jit(solution)/shard_map/parts/ppermute | solution.py:161
  478.7 16.7 %attend_back.5 = (bf16[384,512]{1,0:T(8,128)(2,1)}, f32[1536,256]{1,0:T(8,128)}, f32[384,2048]{1,0:T(8,128)}) custom-call(bf16[384,2048]{1,0:T(8,128)(2,1)} %get-tuple-element.286.refs_0_, f32[1536,384]{1,0:T(8,128)} %and_select_fusion.refs_1_, f32[1536,256]{1,0:T(8,128)} %get-tuple-element.255.refs_2_, f32[384,2048]{1,0:T(8,128)} %get-tuple-element.256.refs_3_, ...), custom_call_target="tpu_custom_call" | custom-call | flops 4630511616 | bytes 16000000 | tf_op jit(solution)/shard_map/attend_back/pallas_call | solution.py:502
  495.4 4.1 add_convert_fusion
  500.1 7.0 %attend_weights.6 = (bf16[1024,1024]{1,0:T(8,128)(2,1)}, bf16[1024,1024]{1,0:T(8,128)(2,1)}) custom-call(bf16[2048,384]{1,0:T(8,128)(2,1)} %get-tuple-element.247.refs_0_.refs_4_, bf16[2048,384]{1,0:T(8,128)(2,1)} %get-tuple-element.248.refs_1_.refs_5_, bf16[384,512]{1,0:T(8,128)(2,1)} %get-tuple-element.260.refs_2_.refs_6_, ...), custom_call_target="tpu_custom_call" | custom-call | flops 1610612736 | bytes 6000000 | tf_op jit(solution)/shard_map/attend_weights/pallas_call | solution.py:569
  509.9 7.6 %collective-permute-done.31 = bf16[384,2048]{1,0:T(8,128)(2,1)S(1)} collective-permute-done((bf16[384,2048]{1,0:T(8,128)(2,1)}, bf16[384,2048]{1,0:T(8,128)(2,1)S(1)}, u32[]{:S(2)}, u32[]{:S(2)}) %collective-permute-start.31) | collective-permute-done | bytes 1572896 | tf_op jit(solution)/shard_map/parts/ppermute | solution.py:161
  520.8 16.6 %attend_back.6 = (bf16[384,512]{1,0:T(8,128)(2,1)}, f32[1536,256]{1,0:T(8,128)}, f32[384,2048]{1,0:T(8,128)}) custom-call(bf16[384,2048]{1,0:T(8,128)(2,1)} %get-tuple-element.286.refs_0_, f32[1536,384]{1,0:T(8,128)} %and_select_fusion.refs_1_, f32[1536,256]{1,0:T(8,128)} %get-tuple-element.267.refs_2_, f32[384,2048]{1,0:T(8,128)} %get-tuple-element.268.refs_3_, ...), custom_call_target="tpu_custom_call" | custom-call | flops 4630511616 | bytes 16000000 | tf_op jit(solution)/shard_map/attend_back/pallas_call | solution.py:502
  539.2 7.0 %attend_weights.7 = (bf16[1024,1024]{1,0:T(8,128)(2,1)}, bf16[1024,1024]{1,0:T(8,128)(2,1)}) custom-call(bf16[2048,384]{1,0:T(8,128)(2,1)} %get-tuple-element.247.refs_0_.refs_4_, bf16[2048,384]{1,0:T(8,128)(2,1)} %get-tuple-element.248.refs_1_.refs_5_, bf16[384,512]{1,0:T(8,128)(2,1)} %get-tuple-element.274.refs_2_.refs_6_, ...), custom_call_target="tpu_custom_call" | custom-call | flops 1610612736 | bytes 6000000 | tf_op jit(solution)/shard_map/attend_weights/pallas_call | solution.py:569
  548.9 9.4 %collective-permute-done.35.come_ref = bf16[384,2048]{1,0:T(8,128)(2,1)S(1)} collective-permute-done((bf16[384,2048]{1,0:T(8,128)(2,1)}, bf16[384,2048]{1,0:T(8,128)(2,1)S(1)}, u32[]{:S(2)}, u32[]{:S(2)}) %collective-permute-start.35) | collective-permute-done | bytes 1572896 | tf_op jit(solution)/shard_map/parts/ppermute | solution.py:161
  562.1 16.0 %attend_back.7 = (bf16[384,512]{1,0:T(8,128)(2,1)}, f32[1536,256]{1,0:T(8,128)}, f32[384,2048]{1,0:T(8,128)}) custom-call(bf16[384,2048]{1,0:T(8,128)(2,1)} %get-tuple-element.286.refs_0_, f32[1536,384]{1,0:T(8,128)} %and_select_fusion.refs_1_, f32[1536,256]{1,0:T(8,128)} %get-tuple-element.287.refs_2_, f32[384,2048]{1,0:T(8,128)} %get-tuple-element.288.refs_3_, ...), custom_call_target="tpu_custom_call" | custom-call | flops 4630511616 | bytes 16000000 | tf_op jit(solution)/shard_map/attend_back/pallas_call | solution.py:502
  579.6 7.0 %attend_weights.8 = (bf16[1024,1024]{1,0:T(8,128)(2,1)}, bf16[1024,1024]{1,0:T(8,128)(2,1)}) custom-call(bf16[2048,384]{1,0:T(8,128)(2,1)} %get-tuple-element.247.refs_0_.refs_4_, bf16[2048,384]{1,0:T(8,128)(2,1)} %get-tuple-element.248.refs_1_.refs_5_, bf16[384,512]{1,0:T(8,128)(2,1)} %get-tuple-element.297.refs_2_, ...), custom_call_target="tpu_custom_call" | custom-call | flops 1610612736 | bytes 6000000 | tf_op jit(solution)/shard_map/attend_weights/pallas_call | solution.py:569
  594.2 5.2 attend_weights.9
  602.1 5.9 collective-permute-done.42.refs_2_
  612.0 9.8 %leave.1 = (f32[384,2048]{1,0:T(8,128)}, bf16[1024,384]{1,0:T(8,128)(2,1)}, bf16[1024,384]{1,0:T(8,128)(2,1)}) custom-call(s32[8]{0:T(128)} %stack.36.table_ref, f32[1536,256]{1,0:T(8,128)} %get-tuple-element.292.refs_0_, bf16[384,256]{1,0:T(8,128)(2,1)} %copy-done.32, bf16[384,256]{1,0:T(8,128)(2,1)} %copy-done.33, bf16[384,256]{1,0:T(8,128)(2,1)} %copy-done.34, ...), custom_call_target="tpu_custom_call" | custom-call | flops 805306368 | bytes 16000000 | tf_op jit(solution)/shard_map/leave/pallas_call | solution.py:816
  625.5 3.9 collective-permute-done.47
  638.9 5.6 collective-permute-done.48.come_ref
  645.3 4.1 collective-permute-done.55
  668.6 4.9 unpack_ffn.1
  673.5 5.2 leave_out.1
  (229 shorter events, 130.2 us)
Async XLA Ops:
  5.2 18.8 %collective-permute-start = (bf16[256,1408]{1,0:T(8,128)(2,1)}, bf16[256,1408]{1,0:T(8,128)(2,1)S(1)}, u32[]{:S(2)}, u32[]{:S(2)}) collective-permute-start(bf16[256,1408]{1,0:T(8,128)(2,1)} %get-tuple-element.171), channel_id=1, source_target_pairs={{0,8},{4,20},{8,0},{12,28},{16,24},{20,4},{24,16},{28,12},{1,9},{5... | collective-permute-start | bytes 2162696 | tf_op jit(solution)/shard_map/attn_w_near/ppermute | solution.py:55
  8.1 15.8 %collective-permute-start.1 = (bf16[256,1024]{1,0:T(8,128)(2,1)}, bf16[256,1024]{1,0:T(8,128)(2,1)S(1)}, u32[]{:S(2)}, u32[]{:S(2)}) collective-permute-start(bf16[256,1024]{1,0:T(8,128)(2,1)} %get-tuple-element.172), channel_id=1, source_target_pairs={{0,1},{1,2},{2,3},{3,0},{4,5},{5,6},{6,7},{7,4},{8,9},{9,10},{10,1... | collective-permute-start | bytes 1572872 | tf_op jit(solution)/shard_map/attn_w_ring/ppermute | solution.py:161
  24.1 19.1 %collective-permute-start.2 = (bf16[512,1408]{1,0:T(8,128)(2,1)S(1)}, bf16[512,1408]{1,0:T(8,128)(2,1)S(1)}, u32[]{:S(2)}, u32[]{:S(2)}) collective-permute-start(bf16[512,1408]{1,0:T(8,128)(2,1)S(1)} %constant_dynamic-update-slice_fusion.refs_0_.refs_4_.refs_8_.refs_7_.refs_11_.refs_15_.refs_12_.refs_16_), channel_id=1, source_target_pairs={{0,16},{4,12},{8,24},{12,4},{16,0},{20,28},{24,8},{28,20},{1,17},{... | collective-permute-start | bytes 4325384 | tf_op jit(solution)/shard_map/attn_w_near/ppermute | solution.py:55
  25.7 14.9 %collective-permute-start.3 = (bf16[256,1024]{1,0:T(8,128)(2,1)S(1)}, bf16[256,1024]{1,0:T(8,128)(2,1)S(1)}, u32[]{:S(2)}, u32[]{:S(2)}) collective-permute-start(bf16[256,1024]{1,0:T(8,128)(2,1)S(1)} %collective-permute-done.1), channel_id=1, source_target_pairs={{0,1},{1,2},{2,3},{3,0},{4,5},{5,6},{6,7},{7,4},{8,9},{9,10},{10,1... | collective-permute-start | bytes 1572872 | tf_op jit(solution)/shard_map/attn_w_ring/ppermute | solution.py:161
  27.2 20.8 %collective-permute-start.4 = (bf16[512,1408]{1,0:T(8,128)(2,1)S(1)}, bf16[512,1408]{1,0:T(8,128)(2,1)S(1)}, u32[]{:S(2)}, u32[]{:S(2)}) collective-permute-start(bf16[512,1408]{1,0:T(8,128)(2,1)S(1)} %constant_dynamic-update-slice_fusion.refs_0_.refs_4_.refs_8_.refs_7_.refs_11_.refs_15_.refs_12_.refs_16_), channel_id=1, source_target_pairs={{0,4},{4,0},{8,12},{12,8},{16,20},{20,16},{24,28},{28,24},{1,5},{5... | collective-permute-start | bytes 4325384 | tf_op jit(solution)/shard_map/attn_w_near/ppermute | solution.py:59
  43.2 16.1 %collective-permute-start.5 = (bf16[512,1408]{1,0:T(8,128)(2,1)S(1)}, bf16[512,1408]{1,0:T(8,128)(2,1)S(1)}, u32[]{:S(2)}, u32[]{:S(2)}) collective-permute-start(bf16[512,1408]{1,0:T(8,128)(2,1)S(1)} %collective-permute-done.2.refs_1_.refs_5_.refs_9_.refs_8_.refs_12_.refs_16_.refs_13_.refs_17_), channel_id=1, source_target_pairs={{0,4},{4,0},{8,12},{12,8},{16,20},{20,16},{24,28},{28,24},{1,5},{5... | collective-permute-start | bytes 4325384 | tf_op jit(solution)/shard_map/attn_w_near/ppermute | solution.py:59
  43.2 16.1 %collective-permute-start.6 = (bf16[256,1024]{1,0:T(8,128)(2,1)S(1)}, bf16[256,1024]{1,0:T(8,128)(2,1)S(1)}, u32[]{:S(2)}, u32[]{:S(2)}) collective-permute-start(bf16[256,1024]{1,0:T(8,128)(2,1)S(1)} %collective-permute-done.3), channel_id=1, source_target_pairs={{0,1},{1,2},{2,3},{3,0},{4,5},{5,6},{6,7},{7,4},{8,9},{9,10},{10,1... | collective-permute-start | bytes 1572872 | tf_op jit(solution)/shard_map/attn_w_ring/ppermute | solution.py:161
  44.7 39.4 %collective-permute-start.11 = (bf16[256,4224]{1,0:T(8,128)(2,1)}, bf16[256,4224]{1,0:T(8,128)(2,1)}, u32[]{:S(2)}, u32[]{:S(2)}) collective-permute-start(bf16[256,4224]{1,0:T(8,128)(2,1)} %pack_ffn.1), channel_id=1, source_target_pairs={{0,8},{4,20},{8,0},{12,28},{16,24},{20,4},{24,16},{28,12},{1,9},{5... | collective-permute-start | bytes 6488072 | tf_op jit(solution)/shard_map/ffn_w/ppermute | solution.py:55
  60.3 28.4 %collective-permute-start.10 = (bf16[256,3072]{1,0:T(8,128)(2,1)}, bf16[256,3072]{1,0:T(8,128)(2,1)}, u32[]{:S(2)}, u32[]{:S(2)}) collective-permute-start(bf16[256,3072]{1,0:T(8,128)(2,1)} %constant_dynamic-update-slice_fusion.2), channel_id=1, source_target_pairs={{0,8},{4,20},{8,0},{12,28},{16,24},{20,4},{24,16},{28,12},{1,9},{5... | collective-permute-start | bytes 4718600 | tf_op jit(solution)/shard_map/attn_w_far/ppermute | solution.py:55
  66.9 17.2 %collective-permute-start.8 = (bf16[384,256]{1,0:T(8,128)(2,1)}, bf16[384,256]{1,0:T(8,128)(2,1)S(1)}, u32[]{:S(2)}, u32[]{:S(2)}) collective-permute-start(bf16[384,256]{1,0:T(8,128)(2,1)} %get-tuple-element.197.refs_3_.refs_5_.refs_7_.refs_0_), channel_id=1, source_target_pairs={{0,2},{1,3},{2,0},{3,1},{4,6},{5,7},{6,4},{7,5},{8,10},{9,11},{10,... | collective-permute-start | bytes 589832 | tf_op jit(solution)/shard_map/kv/ppermute | solution.py:165
  67.5 16.7 %collective-permute-start.9 = (bf16[384,256]{1,0:T(8,128)(2,1)}, bf16[384,256]{1,0:T(8,128)(2,1)S(1)}, u32[]{:S(2)}, u32[]{:S(2)}) collective-permute-start(bf16[384,256]{1,0:T(8,128)(2,1)} %get-tuple-element.197.refs_3_.refs_5_.refs_7_.refs_0_), channel_id=1, source_target_pairs={{0,3},{1,0},{2,1},{3,2},{4,7},{5,4},{6,5},{7,6},{8,11},{9,8},{10,9... | collective-permute-start | bytes 589832 | tf_op jit(solution)/shard_map/kv/ppermute | solution.py:165
  90.9 37.9 %collective-permute-start.13 = (bf16[512,3072]{1,0:T(8,128)(2,1)S(1)}, bf16[512,3072]{1,0:T(8,128)(2,1)}, u32[]{:S(2)}, u32[]{:S(2)}) collective-permute-start(bf16[512,3072]{1,0:T(8,128)(2,1)S(1)} %pad_maximum_fusion.1.refs_7_.refs_11_.refs_9_.refs_13_.refs_15_), channel_id=1, source_target_pairs={{0,16},{4,12},{8,24},{12,4},{16,0},{20,28},{24,8},{28,20},{1,17},{... | collective-permute-start | bytes 9437192 | tf_op jit(solution)/shard_map/attn_w_far/ppermute | solution.py:55
  92.5 36.3 %collective-permute-start.12 = (bf16[384,2048]{1,0:T(8,128)(2,1)S(1)}, bf16[384,2048]{1,0:T(8,128)(2,1)}, u32[]{:S(2)}, u32[]{:S(2)}) collective-permute-start(bf16[384,2048]{1,0:T(8,128)(2,1)S(1)} %copy-done.12), channel_id=1, source_target_pairs={{0,1},{1,2},{2,3},{3,0},{4,5},{5,6},{6,7},{7,4},{8,9},{9,10},{10,1... | collective-permute-start | bytes 4718600 | tf_op jit(solution)/shard_map/grad_ring/ppermute | solution.py:161
  94.1 38.4 %collective-permute-start.14 = (bf16[512,3072]{1,0:T(8,128)(2,1)S(1)}, bf16[512,3072]{1,0:T(8,128)(2,1)}, u32[]{:S(2)}, u32[]{:S(2)}) collective-permute-start(bf16[512,3072]{1,0:T(8,128)(2,1)S(1)} %pad_maximum_fusion.1.refs_7_.refs_11_.refs_9_.refs_13_.refs_15_), channel_id=1, source_target_pairs={{0,4},{4,0},{8,12},{12,8},{16,20},{20,16},{24,28},{28,24},{1,5},{5... | collective-permute-start | bytes 9437192 | tf_op jit(solution)/shard_map/attn_w_far/ppermute | solution.py:59
  128.8 50.2 %collective-permute-start.17 = (bf16[512,4224]{1,0:T(8,128)(2,1)}, bf16[512,4224]{1,0:T(8,128)(2,1)}, u32[]{:S(2)}, u32[]{:S(2)}) collective-permute-start(bf16[512,4224]{1,0:T(8,128)(2,1)} %pad_maximum_fusion.refs_2_), channel_id=1, source_target_pairs={{0,16},{4,12},{8,24},{12,4},{16,0},{20,28},{24,8},{28,20},{1,17},{... | collective-permute-start | bytes 12976136 | tf_op jit(solution)/shard_map/ffn_w/ppermute | solution.py:55
  131.2 38.8 %collective-permute-start.18 = (bf16[384,2048]{1,0:T(8,128)(2,1)}, bf16[384,2048]{1,0:T(8,128)(2,1)}, u32[]{:S(2)}, u32[]{:S(2)}) collective-permute-start(bf16[384,2048]{1,0:T(8,128)(2,1)} %collective-permute-done.12.refs_1_.refs_4_), channel_id=1, source_target_pairs={{0,1},{1,2},{2,3},{3,0},{4,5},{5,6},{6,7},{7,4},{8,9},{9,10},{10,1... | collective-permute-start | bytes 4718600 | tf_op jit(solution)/shard_map/grad_ring/ppermute | solution.py:161
  132.4 47.7 %collective-permute-start.19 = (bf16[512,4224]{1,0:T(8,128)(2,1)}, bf16[512,4224]{1,0:T(8,128)(2,1)}, u32[]{:S(2)}, u32[]{:S(2)}) collective-permute-start(bf16[512,4224]{1,0:T(8,128)(2,1)} %pad_maximum_fusion.refs_2_), channel_id=1, source_target_pairs={{0,4},{4,0},{8,12},{12,8},{16,20},{20,16},{24,28},{28,24},{1,5},{5... | collective-permute-start | bytes 12976136 | tf_op jit(solution)/shard_map/ffn_w/ppermute | solution.py:59
  179.0 38.6 %collective-permute-start.16 = (bf16[384,2048]{1,0:T(8,128)(2,1)S(1)}, bf16[384,2048]{1,0:T(8,128)(2,1)S(1)}, u32[]{:S(2)}, u32[]{:S(2)}) collective-permute-start(bf16[384,2048]{1,0:T(8,128)(2,1)S(1)} %multiply_convert_fusion.refs_0_), channel_id=1, source_target_pairs={{0,1},{1,2},{2,3},{3,0},{4,5},{5,6},{6,7},{7,4},{8,9},{9,10},{10,1... | collective-permute-start | bytes 4718600 | tf_op jit(solution)/shard_map/ffn_ring/ppermute | solution.py:161
  217.6 38.1 %collective-permute-start.21 = (bf16[384,2048]{1,0:T(8,128)(2,1)S(1)}, bf16[384,2048]{1,0:T(8,128)(2,1)}, u32[]{:S(2)}, u32[]{:S(2)}) collective-permute-start(bf16[384,2048]{1,0:T(8,128)(2,1)S(1)} %collective-permute-done.16.refs_0_.refs_1_), channel_id=1, source_target_pairs={{0,1},{1,2},{2,3},{3,0},{4,5},{5,6},{6,7},{7,4},{8,9},{9,10},{10,1... | collective-permute-start | bytes 4718600 | tf_op jit(solution)/shard_map/ffn_ring/ppermute | solution.py:161
  255.8 39.3 %collective-permute-start.22 = (bf16[384,2048]{1,0:T(8,128)(2,1)}, bf16[384,2048]{1,0:T(8,128)(2,1)S(1)}, u32[]{:S(2)}, u32[]{:S(2)}) collective-permute-start(bf16[384,2048]{1,0:T(8,128)(2,1)} %collective-permute-done.21.refs_0_.refs_2_), channel_id=1, source_target_pairs={{0,1},{1,2},{2,3},{3,0},{4,5},{5,6},{6,7},{7,4},{8,9},{9,10},{10,1... | collective-permute-start | bytes 4718600 | tf_op jit(solution)/shard_map/ffn_ring/ppermute | solution.py:161
  255.8 80.1 %collective-permute-start.23 = (bf16[384,2048]{1,0:T(8,128)(2,1)}, bf16[384,2048]{1,0:T(8,128)(2,1)S(1)}, u32[]{:S(2)}, u32[]{:S(2)}) collective-permute-start(bf16[384,2048]{1,0:T(8,128)(2,1)} %collective-permute-done.18.refs_1_.refs_5_), channel_id=1, source_target_pairs={{0,1},{1,2},{2,3},{3,0},{4,5},{5,6},{6,7},{7,4},{8,9},{9,10},{10,1... | collective-permute-start | bytes 4718600 | tf_op jit(solution)/shard_map/grad_ring/ppermute | solution.py:161
  255.8 104.6 %collective-permute-start.24 = (bf16[384,2048]{1,0:T(8,128)(2,1)}, bf16[384,2048]{1,0:T(8,128)(2,1)S(1)}, u32[]{:S(2)}, u32[]{:S(2)}) collective-permute-start(bf16[384,2048]{1,0:T(8,128)(2,1)} %get-tuple-element.228), channel_id=1, source_target_pairs={{0,1},{1,2},{2,3},{3,0},{4,5},{5,6},{6,7},{7,4},{8,9},{9,10},{10,1... | collective-permute-start | bytes 4718600 | tf_op jit(solution)/shard_map/backs/ppermute | solution.py:161
  362.2 36.2 %collective-permute-start.25 = (bf16[384,2048]{1,0:T(8,128)(2,1)}, bf16[384,2048]{1,0:T(8,128)(2,1)S(1)}, u32[]{:S(2)}, u32[]{:S(2)}) collective-permute-start(bf16[384,2048]{1,0:T(8,128)(2,1)} %add_convert_fusion.5), channel_id=1, source_target_pairs={{0,1},{1,2},{2,3},{3,0},{4,5},{5,6},{6,7},{7,4},{8,9},{9,10},{10,1... | collective-permute-start | bytes 4718600 | tf_op jit(solution)/shard_map/backs/ppermute | solution.py:161
  398.4 13.9 %collective-permute-start.26 = (bf16[1024,4224]{1,0:T(8,128)(2,1)}, bf16[1024,4224]{1,0:T(8,128)(2,1)}, u32[]{:S(2)}, u32[]{:S(2)}) collective-permute-start(bf16[1024,4224]{1,0:T(8,128)(2,1)} %ffn_weights.6), channel_id=1, source_target_pairs={{0,4},{4,0},{8,12},{12,8},{16,20},{20,16},{24,28},{28,24},{1,5},{5... | collective-permute-start | bytes 25952264 | tf_op jit(solution)/shard_map/ffn_g/ppermute | solution.py:59
  399.1 38.7 %collective-permute-start.27 = (bf16[384,2048]{1,0:T(8,128)(2,1)S(1)}, bf16[384,2048]{1,0:T(8,128)(2,1)S(1)}, u32[]{:S(2)}, u32[]{:S(2)}) collective-permute-start(bf16[384,2048]{1,0:T(8,128)(2,1)S(1)} %add_convert_fusion.4), channel_id=1, source_target_pairs={{0,1},{1,2},{2,3},{3,0},{4,5},{5,6},{6,7},{7,4},{8,9},{9,10},{10,1... | collective-permute-start | bytes 4718600 | tf_op jit(solution)/shard_map/backs/ppermute | solution.py:161
  437.7 57.6 %collective-permute-start.30 = (bf16[512,4224]{1,0:T(8,128)(2,1)}, bf16[512,4224]{1,0:T(8,128)(2,1)}, u32[]{:S(2)}, u32[]{:S(2)}) collective-permute-start(bf16[512,4224]{1,0:T(8,128)(2,1)} %get-tuple-element.259), channel_id=1, source_target_pairs={{0,16},{4,12},{8,24},{12,4},{16,0},{20,28},{24,8},{28,20},{1,17},{... | collective-permute-start | bytes 12976136 | tf_op jit(solution)/shard_map/ffn_g/ppermute | solution.py:55
  439.3 37.5 %collective-permute-start.28 = (bf16[384,2048]{1,0:T(8,128)(2,1)S(1)}, bf16[384,2048]{1,0:T(8,128)(2,1)S(1)}, u32[]{:S(2)}, u32[]{:S(2)}) collective-permute-start(bf16[384,2048]{1,0:T(8,128)(2,1)S(1)} %copy-done.37), channel_id=1, source_target_pairs={{0,1},{1,2},{2,3},{3,0},{4,5},{5,6},{6,7},{7,4},{8,9},{9,10},{10,1... | collective-permute-start | bytes 4718600 | tf_op jit(solution)/shard_map/parts/ppermute | solution.py:161
  476.8 18.6 %collective-permute-start.29 = (bf16[1024,1024]{1,0:T(8,128)(2,1)}, bf16[1024,1024]{1,0:T(8,128)(2,1)}, u32[]{:S(2)}, u32[]{:S(2)}) collective-permute-start(bf16[1024,1024]{1,0:T(8,128)(2,1)} %attend_weights.5), channel_id=1, source_target_pairs={{0,4},{4,0},{8,12},{12,8},{16,20},{20,16},{24,28},{28,24},{1,5},{5... | collective-permute-start | bytes 6291464 | tf_op jit(solution)/shard_map/attn_g_1/ppermute | solution.py:59
  478.7 38.8 %collective-permute-start.31 = (bf16[384,2048]{1,0:T(8,128)(2,1)}, bf16[384,2048]{1,0:T(8,128)(2,1)S(1)}, u32[]{:S(2)}, u32[]{:S(2)}) collective-permute-start(bf16[384,2048]{1,0:T(8,128)(2,1)} %add_convert_fusion.3), channel_id=1, source_target_pairs={{0,1},{1,2},{2,3},{3,0},{4,5},{5,6},{6,7},{7,4},{8,9},{9,10},{10,1... | collective-permute-start | bytes 4718600 | tf_op jit(solution)/shard_map/parts/ppermute | solution.py:161
  499.5 37.9 %collective-permute-start.34 = (bf16[256,4224]{1,0:T(8,128)(2,1)}, bf16[256,4224]{1,0:T(8,128)(2,1)S(1)}, u32[]{:S(2)}, u32[]{:S(2)}) collective-permute-start(bf16[256,4224]{1,0:T(8,128)(2,1)} %get-tuple-element.332), channel_id=1, source_target_pairs={{0,8},{4,20},{8,0},{12,28},{16,24},{20,4},{24,16},{28,12},{1,9},{5... | collective-permute-start | bytes 6488072 | tf_op jit(solution)/shard_map/ffn_g/ppermute | solution.py:55
  517.5 20.0 %collective-permute-start.32 = (bf16[1024,1024]{1,0:T(8,128)(2,1)}, bf16[1024,1024]{1,0:T(8,128)(2,1)}, u32[]{:S(2)}, u32[]{:S(2)}) collective-permute-start(bf16[1024,1024]{1,0:T(8,128)(2,1)} %get-tuple-element.270), channel_id=1, source_target_pairs={{0,4},{4,0},{8,12},{12,8},{16,20},{20,16},{24,28},{28,24},{1,5},{5... | collective-permute-start | bytes 6291464 | tf_op jit(solution)/shard_map/attn_g_2/ppermute | solution.py:59
  517.5 20.0 %collective-permute-start.33 = (bf16[512,1024]{1,0:T(8,128)(2,1)}, bf16[512,1024]{1,0:T(8,128)(2,1)S(1)}, u32[]{:S(2)}, u32[]{:S(2)}) collective-permute-start(bf16[512,1024]{1,0:T(8,128)(2,1)} %get-tuple-element.271), channel_id=1, source_target_pairs={{0,16},{4,12},{8,24},{12,4},{16,0},{20,28},{24,8},{28,20},{1,17},{... | collective-permute-start | bytes 3145736 | tf_op jit(solution)/shard_map/attn_g_1/ppermute | solution.py:55
  520.8 37.5 %collective-permute-start.35 = (bf16[384,2048]{1,0:T(8,128)(2,1)}, bf16[384,2048]{1,0:T(8,128)(2,1)S(1)}, u32[]{:S(2)}, u32[]{:S(2)}) collective-permute-start(bf16[384,2048]{1,0:T(8,128)(2,1)} %add_convert_fusion.2), channel_id=1, source_target_pairs={{0,1},{1,2},{2,3},{3,0},{4,5},{5,6},{6,7},{7,4},{8,9},{9,10},{10,1... | collective-permute-start | bytes 4718600 | tf_op jit(solution)/shard_map/parts/ppermute | solution.py:161
  538.6 19.7 %collective-permute-start.36 = (bf16[256,1024]{1,0:T(8,128)(2,1)}, bf16[256,1024]{1,0:T(8,128)(2,1)}, u32[]{:S(2)}, u32[]{:S(2)}) collective-permute-start(bf16[256,1024]{1,0:T(8,128)(2,1)} %add_convert_fusion.18), channel_id=1, source_target_pairs={{0,8},{4,20},{8,0},{12,28},{16,24},{20,4},{24,16},{28,12},{1,9},{5... | collective-permute-start | bytes 1572872 | tf_op jit(solution)/shard_map/attn_g_1/ppermute | solution.py:55
  558.4 19.8 %collective-permute-start.37 = (bf16[1024,1024]{1,0:T(8,128)(2,1)}, bf16[1024,1024]{1,0:T(8,128)(2,1)S(1)}, u32[]{:S(2)}, u32[]{:S(2)}) collective-permute-start(bf16[1024,1024]{1,0:T(8,128)(2,1)} %get-tuple-element.294), channel_id=1, source_target_pairs={{0,4},{4,0},{8,12},{12,8},{16,20},{20,16},{24,28},{28,24},{1,5},{5... | collective-permute-start | bytes 6291464 | tf_op jit(solution)/shard_map/attn_g_3/ppermute | solution.py:59
  558.4 19.7 %collective-permute-start.38 = (bf16[512,1024]{1,0:T(8,128)(2,1)}, bf16[512,1024]{1,0:T(8,128)(2,1)}, u32[]{:S(2)}, u32[]{:S(2)}) collective-permute-start(bf16[512,1024]{1,0:T(8,128)(2,1)} %get-tuple-element.295), channel_id=1, source_target_pairs={{0,16},{4,12},{8,24},{12,4},{16,0},{20,28},{24,8},{28,20},{1,17},{... | collective-permute-start | bytes 3145736 | tf_op jit(solution)/shard_map/attn_g_2/ppermute | solution.py:55
  562.1 16.0 %collective-permute-start.39 = (bf16[256,1024]{1,0:T(8,128)(2,1)}, bf16[256,1024]{1,0:T(8,128)(2,1)S(1)}, u32[]{:S(2)}, u32[]{:S(2)}) collective-permute-start(bf16[256,1024]{1,0:T(8,128)(2,1)} %add_convert_fusion.16), channel_id=1, source_target_pairs={{0,1},{1,2},{2,3},{3,0},{4,5},{5,6},{6,7},{7,4},{8,9},{9,10},{10,1... | collective-permute-start | bytes 1572872 | tf_op jit(solution)/shard_map/attn_g_ring/ppermute | solution.py:161
  587.7 14.4 %collective-permute-start.41 = (bf16[384,256]{1,0:T(8,128)(2,1)}, bf16[384,256]{1,0:T(8,128)(2,1)S(1)}, u32[]{:S(2)}, u32[]{:S(2)}) collective-permute-start(bf16[384,256]{1,0:T(8,128)(2,1)} %get-tuple-element.345), channel_id=1, source_target_pairs={{0,3},{1,0},{2,1},{3,2},{4,7},{5,4},{6,5},{7,6},{8,11},{9,8},{10,9... | collective-permute-start | bytes 589832 | tf_op jit(solution)/shard_map/kv_g/ppermute | solution.py:165
  591.4 16.5 %collective-permute-start.42 = (bf16[384,256]{1,0:T(8,128)(2,1)}, bf16[384,256]{1,0:T(8,128)(2,1)S(1)}, u32[]{:S(2)}, u32[]{:S(2)}) collective-permute-start(bf16[384,256]{1,0:T(8,128)(2,1)} %get-tuple-element.344), channel_id=1, source_target_pairs={{0,2},{1,3},{2,0},{3,1},{4,6},{5,7},{6,4},{7,5},{8,10},{9,11},{10,... | collective-permute-start | bytes 589832 | tf_op jit(solution)/shard_map/kv_g/ppermute | solution.py:165
  591.4 16.5 %collective-permute-start.43 = (bf16[384,256]{1,0:T(8,128)(2,1)S(1)}, bf16[384,256]{1,0:T(8,128)(2,1)S(1)}, u32[]{:S(2)}, u32[]{:S(2)}) collective-permute-start(bf16[384,256]{1,0:T(8,128)(2,1)S(1)} %get-tuple-element.343), channel_id=1, source_target_pairs={{0,1},{1,2},{2,3},{3,0},{4,5},{5,6},{6,7},{7,4},{8,9},{9,10},{10,1... | collective-permute-start | bytes 589832 | tf_op jit(solution)/shard_map/kv_g/ppermute | solution.py:165
  593.3 28.6 %collective-permute-start.46 = (bf16[512,1024]{1,0:T(8,128)(2,1)}, bf16[512,1024]{1,0:T(8,128)(2,1)S(1)}, u32[]{:S(2)}, u32[]{:S(2)}) collective-permute-start(bf16[512,1024]{1,0:T(8,128)(2,1)} %slice.152), channel_id=1, source_target_pairs={{0,16},{4,12},{8,24},{12,4},{16,0},{20,28},{24,8},{28,20},{1,17},{... | collective-permute-start | bytes 3145736 | tf_op jit(solution)/shard_map/attn_g_3/ppermute | solution.py:55
  608.7 20.7 %collective-permute-start.47 = (bf16[512,1024]{1,0:T(8,128)(2,1)}, bf16[512,1024]{1,0:T(8,128)(2,1)}, u32[]{:S(2)}, u32[]{:S(2)}) collective-permute-start(bf16[512,1024]{1,0:T(8,128)(2,1)} %get-tuple-element.314), channel_id=1, source_target_pairs={{0,16},{4,12},{8,24},{12,4},{16,0},{20,28},{24,8},{28,20},{1,17},{... | collective-permute-start | bytes 3145736 | tf_op jit(solution)/shard_map/attn_g_0/ppermute | solution.py:55
  610.5 15.0 %collective-permute-start.45 = (bf16[256,1024]{1,0:T(8,128)(2,1)S(1)}, bf16[256,1024]{1,0:T(8,128)(2,1)}, u32[]{:S(2)}, u32[]{:S(2)}) collective-permute-start(bf16[256,1024]{1,0:T(8,128)(2,1)S(1)} %add_convert_fusion.15), channel_id=1, source_target_pairs={{0,8},{4,20},{8,0},{12,28},{16,24},{20,4},{24,16},{28,12},{1,9},{5... | collective-permute-start | bytes 1572872 | tf_op jit(solution)/shard_map/attn_g_2/ppermute | solution.py:55
  621.9 15.7 %collective-permute-start.44 = (bf16[1024,384]{1,0:T(8,128)(2,1)}, bf16[1024,384]{1,0:T(8,128)(2,1)S(1)}, u32[]{:S(2)}, u32[]{:S(2)}) collective-permute-start(bf16[1024,384]{1,0:T(8,128)(2,1)} %get-tuple-element.309), channel_id=1, source_target_pairs={{0,4},{4,0},{8,12},{12,8},{16,20},{20,16},{24,28},{28,24},{1,5},{5... | collective-permute-start | bytes 2359304 | tf_op jit(solution)/shard_map/small_g/ppermute | solution.py:59
  654.5 24.2 %collective-permute-start.56 = (bf16[256,1024]{1,0:T(8,128)(2,1)S(1)}, bf16[256,1024]{1,0:T(8,128)(2,1)S(1)}, u32[]{:S(2)}, u32[]{:S(2)}) collective-permute-start(bf16[256,1024]{1,0:T(8,128)(2,1)S(1)} %add_convert_fusion.7), channel_id=1, source_target_pairs={{0,1},{1,2},{2,3},{3,0},{4,5},{5,6},{6,7},{7,4},{8,9},{9,10},{10,1... | collective-permute-start | bytes 1572872 | tf_op jit(solution)/shard_map/attn_g_ring/ppermute | solution.py:161
  658.8 23.2 %collective-permute-start.52 = (bf16[256,384]{1,0:T(8,128)(2,1)S(1)}, bf16[256,384]{1,0:T(8,128)(2,1)S(1)}, u32[]{:S(2)}, u32[]{:S(2)}) collective-permute-start(bf16[256,384]{1,0:T(8,128)(2,1)S(1)} %add_convert_fusion.21), channel_id=1, source_target_pairs={{0,1},{1,2},{2,3},{3,0},{4,5},{5,6},{6,7},{7,4},{8,9},{9,10},{10,1... | collective-permute-start | bytes 589832 | tf_op jit(solution)/shard_map/small_g_ring/ppermute | solution.py:165
  660.3 21.8 %collective-permute-start.53 = (bf16[256,384]{1,0:T(8,128)(2,1)S(1)}, bf16[256,384]{1,0:T(8,128)(2,1)S(1)}, u32[]{:S(2)}, u32[]{:S(2)}) collective-permute-start(bf16[256,384]{1,0:T(8,128)(2,1)S(1)} %add_convert_fusion.21), channel_id=1, source_target_pairs={{0,2},{1,3},{2,0},{3,1},{4,6},{5,7},{6,4},{7,5},{8,10},{9,11},{10,... | collective-permute-start | bytes 589832 | tf_op jit(solution)/shard_map/small_g_ring/ppermute | solution.py:165
  662.3 19.8 %collective-permute-start.54 = (bf16[256,384]{1,0:T(8,128)(2,1)S(1)}, bf16[256,384]{1,0:T(8,128)(2,1)S(1)}, u32[]{:S(2)}, u32[]{:S(2)}) collective-permute-start(bf16[256,384]{1,0:T(8,128)(2,1)S(1)} %add_convert_fusion.21), channel_id=1, source_target_pairs={{0,3},{1,0},{2,1},{3,2},{4,7},{5,4},{6,5},{7,6},{8,11},{9,8},{10,9... | collective-permute-start | bytes 589832 | tf_op jit(solution)/shard_map/small_g_ring/ppermute | solution.py:165
  (50 other events, 532.3 us)

commit v4 on v3

--- a/solution.py
+++ b/solution.py
@@ -550,7 +550,7 @@
 
 def attend_weights(normed, branch, send=None, keep=None):
     width, tokens = normed.shape
-    steps = 4
+    steps = 2
     rows = width // 2 // steps
     specs, arrays, out_shape = [], [], []
     for item, first in ((send, steps), (keep, 0)):

time: 692 us -> 691 us (level)
  transfers between devices with their start and end apart: 57 -> 57, of which waited for: 29 -> 30; matrix products, arithmetic and copies ran while one was open for 7% -> 7% of each run, Pallas kernels for 49% -> 48%
where the time goes in v4:
time: 691 us; the launch traced here: 683 us
  Pallas kernels  339 us (49%)
  waiting for transfers between devices  234 us (34%)
  starting transfers between devices  49.5 us (7%)
  other arithmetic  34.5 us (5%)
  local copies, waits for them, and re-layouts  24.6 us (4%)
    ppermute x18, waiting for transfers between devices, ring_next(): lax.ppermute(array, 'tensor', [(i, (i + 1) % nt_) for i in range(nt_)])  155 us
    pallas_call x4, Pallas kernels, ffn_block(): pl.pallas_call(lambda *refs: ffn_kernel(count, steps, last, refs), out_sh...  86.1 us
    pallas_call x4, Pallas kernels, ffn_weights(): pl.pallas_call(lambda *refs: ffn_weights_kernel(blocks, count, steps, las...  67.3 us
    pallas_call x4, Pallas kernels, attend_back_block(): pl.pallas_call(lambda *refs: attend_back_kernel(count, blocks, first, ref...  64.4 us
    pallas_call x2, Pallas kernels, attend_block(): pl.pallas_call(lambda *refs: attend_kernel(count, blocks, refs), out_shap...  44.3 us
    ppermute x18, waiting for transfers between devices, plane_swap(): lax.ppermute(array, 'dp', [(d, d ^ orders[d & 1][step]) for d in range(nd...  36.9 us
    pallas_call x5, Pallas kernels, attend_weights(): pl.pallas_call(lambda *refs: attend_weights_kernel(int(send is not None),...  26.2 us
    ppermute x12, waiting for transfers between devices, core_swap(): return lax.ppermute(array, 'dp', [(d, d ^ 1) for d in range(ndp)])  22 us
  transfers between devices with their start and end apart: 57, of which 30 were waited for; matrix products, arithmetic and copies ran while one was open for 7% of the time, Pallas kernels for 48%

profile of v4, /device:TPU:0, one launch (start us, length us, event | category | flops | bytes accessed | tf_op | source)
XLA Modules:
  0.0 683.3 jit_solution(11449892828258544313)
XLA Ops:
  12.3 6.2 take_columns.1.refs_1_.refs_3_.given_ref
  27.2 13.4 %collective-permute-done.3 = bf16[256,1024]{1,0:T(8,128)(2,1)S(1)} collective-permute-done((bf16[256,1024]{1,0:T(8,128)(2,1)S(1)}, bf16[256,1024]{1,0:T(8,128)(2,1)S(1)}, u32[]{:S(2)}, u32[]{:S(2)}) %collective-permute-start.3) | collective-permute-done | bytes 524320 | tf_op jit(solution)/shard_map/attn_w_ring/ppermute | solution.py:161
  48.0 11.3 %collective-permute-done.6 = bf16[256,1024]{1,0:T(8,128)(2,1)S(1)} collective-permute-done((bf16[256,1024]{1,0:T(8,128)(2,1)S(1)}, bf16[256,1024]{1,0:T(8,128)(2,1)S(1)}, u32[]{:S(2)}, u32[]{:S(2)}) %collective-permute-start.6) | collective-permute-done | bytes 524320 | tf_op jit(solution)/shard_map/attn_w_ring/ppermute | solution.py:161
  61.4 5.5 enter.1
  70.8 6.1 collective-permute-done.7.refs_4_.refs_6_.refs_8_.refs_1_
  76.9 7.3 %collective-permute-done.8.refs_5_.refs_7_.refs_9_.refs_2_ = bf16[384,256]{1,0:T(8,128)(2,1)S(1)} collective-permute-done((bf16[384,256]{1,0:T(8,128)(2,1)}, bf16[384,256]{1,0:T(8,128)(2,1)S(1)}, u32[]{:S(2)}, u32[]{:S(2)}) %collective-permute-start.8) | collective-permute-done | bytes 196640 | tf_op jit(solution)/shard_map/kv/ppermute | solution.py:165
  84.2 4.5 collective-permute-done.10
  94.1 4.6 pad_maximum_fusion.refs_2_
  98.7 13.6 %attend.2 = (bf16[384,512]{1,0:T(8,128)(2,1)}, bf16[384,512]{1,0:T(8,128)(2,1)}, f32[2,1,768]{2,1,0:T(1,128)}, f32[384,2048]{1,0:T(8,128)}) custom-call(bf16[384,2048]{1,0:T(8,128)(2,1)} %get-tuple-element.194.refs_0_.refs_7_, f32[1536,384]{1,0:T(8,128)} %and_select_fusion.refs_1_, bf16[384,2048]{1,0:T(8,128)(2,1)} %get-tuple-element.196.refs_2_.refs_8_, ...), custom_call_target="tpu_custom_call" | custom-call | flops 2818572288 | bytes 14000000 | tf_op jit(solution)/shard_map/attend/pallas_call | solution.py:412
  112.3 16.5 %collective-permute-done.12.refs_1_.refs_4_ = bf16[384,2048]{1,0:T(8,128)(2,1)} collective-permute-done((bf16[384,2048]{1,0:T(8,128)(2,1)S(1)}, bf16[384,2048]{1,0:T(8,128)(2,1)}, u32[]{:S(2)}, u32[]{:S(2)}) %collective-permute-start.12) | collective-permute-done | bytes 1572896 | tf_op jit(solution)/shard_map/grad_ring/ppermute | solution.py:161
  134.8 30.7 %attend.3 = (bf16[384,1536]{1,0:T(8,128)(2,1)}, bf16[384,1536]{1,0:T(8,128)(2,1)}, f32[6,1,768]{2,1,0:T(1,128)}, f32[384,2048]{1,0:T(8,128)}) custom-call(bf16[384,2048]{1,0:T(8,128)(2,1)} %get-tuple-element.194.refs_0_.refs_7_, f32[1536,384]{1,0:T(8,128)} %and_select_fusion.refs_1_, f32[384,2048]{1,0:T(8,128)} %get-tuple-element.206.refs_2_, ...), custom_call_target="tpu_custom_call" | custom-call | flops 8455716864 | bytes 14000000 | tf_op jit(solution)/shard_map/attend/pallas_call | solution.py:412
  170.0 9.1 %collective-permute-done.17.refs_3_ = bf16[512,4224]{1,0:T(8,128)(2,1)} collective-permute-done((bf16[512,4224]{1,0:T(8,128)(2,1)}, bf16[512,4224]{1,0:T(8,128)(2,1)}, u32[]{:S(2)}, u32[]{:S(2)}) %collective-permute-start.17) | collective-permute-done | bytes 4325408 | tf_op jit(solution)/shard_map/ffn_w/ppermute | solution.py:55
  180.2 6.6 collective-permute-done.20.refs_5_
  186.7 21.4 %ffn_block.4 = (bf16[384,4224]{1,0:T(8,128)(2,1)}, bf16[384,2048]{1,0:T(8,128)(2,1)}, bf16[384,2048]{1,0:T(8,128)(2,1)}) custom-call(bf16[384,2048]{1,0:T(8,128)(2,1)} %copy-done.18, bf16[384,2048]{1,0:T(8,128)(2,1)} %take_columns.1.refs_1_.refs_3_.given_ref, bf16[512,4224]{1,0:T(8,128)(2,1)} %pad_maximum_fusion.refs_2_, ...), custom_call_target="tpu_custom_call" | custom-call | flops 13287555072 | bytes 26738688 | tf_op jit(solution)/shard_map/ffn_block/pallas_call | solution.py:635
  208.1 9.5 %collective-permute-done.16.refs_0_.refs_1_ = bf16[384,2048]{1,0:T(8,128)(2,1)S(1)} collective-permute-done((bf16[384,2048]{1,0:T(8,128)(2,1)S(1)}, bf16[384,2048]{1,0:T(8,128)(2,1)S(1)}, u32[]{:S(2)}, u32[]{:S(2)}) %collective-permute-start.16) | collective-permute-done | bytes 1572896 | tf_op jit(solution)/shard_map/ffn_ring/ppermute | solution.py:161
  218.8 21.4 %ffn_block.5 = (bf16[384,4224]{1,0:T(8,128)(2,1)}, bf16[384,2048]{1,0:T(8,128)(2,1)}, bf16[384,2048]{1,0:T(8,128)(2,1)}) custom-call(bf16[384,2048]{1,0:T(8,128)(2,1)} %copy-done.38, bf16[384,2048]{1,0:T(8,128)(2,1)} %collective-permute-done.12.refs_1_.refs_4_, bf16[512,4224]{1,0:T(8,128)(2,1)} %pad_maximum_fusion.refs_2_, ...), custom_call_target="tpu_custom_call" | custom-call | flops 13287555072 | bytes 26738688 | tf_op jit(solution)/shard_map/ffn_block/pallas_call | solution.py:635
  240.3 15.7 %collective-permute-done.21.refs_0_.refs_2_ = bf16[384,2048]{1,0:T(8,128)(2,1)} collective-permute-done((bf16[384,2048]{1,0:T(8,128)(2,1)S(1)}, bf16[384,2048]{1,0:T(8,128)(2,1)}, u32[]{:S(2)}, u32[]{:S(2)}) %collective-permute-start.21) | collective-permute-done | bytes 1572896 | tf_op jit(solution)/shard_map/ffn_ring/ppermute | solution.py:161
  256.7 21.4 %ffn_block.6 = (bf16[384,4224]{1,0:T(8,128)(2,1)}, bf16[384,2048]{1,0:T(8,128)(2,1)}, bf16[384,2048]{1,0:T(8,128)(2,1)}) custom-call(bf16[384,2048]{1,0:T(8,128)(2,1)} %collective-permute-done.21.refs_0_.refs_2_, bf16[384,2048]{1,0:T(8,128)(2,1)} %collective-permute-done.18.refs_1_.refs_5_, bf16[512,4224]{1,0:T(8,128)(2,1)} %pad_maximum_fusion.refs_2_, ...), custom_call_target="tpu_custom_call" | custom-call | flops 13287555072 | bytes 26738688 | tf_op jit(solution)/shard_map/ffn_block/pallas_call | solution.py:635
  278.1 17.2 %collective-permute-done.22.refs_0_ = bf16[384,2048]{1,0:T(8,128)(2,1)S(1)} collective-permute-done((bf16[384,2048]{1,0:T(8,128)(2,1)}, bf16[384,2048]{1,0:T(8,128)(2,1)S(1)}, u32[]{:S(2)}, u32[]{:S(2)}) %collective-permute-start.22) | collective-permute-done | bytes 1572896 | tf_op jit(solution)/shard_map/ffn_ring/ppermute | solution.py:161
  295.3 21.2 %ffn_weights.5 = (bf16[512,4224]{1,0:T(8,128)(2,1)}, bf16[512,4224]{1,0:T(8,128)(2,1)}) custom-call(bf16[384,2048]{1,0:T(8,128)(2,1)} %copy-done.18, bf16[384,2048]{1,0:T(8,128)(2,1)} %copy-done.38, bf16[384,2048]{1,0:T(8,128)(2,1)} %collective-permute-done.21.refs_0_.refs_2_, bf16[384,2048]{1,0:T(8,128)(2,1)} %take_columns.1.refs_1_.refs_3_.given_ref, ...), custom_call_target="tpu_custom_call" | custom-call | flops 9965666304 | bytes 28114944 | tf_op jit(solution)/shard_map/ffn_weights/pallas_call | solution.py:700
  316.5 19.6 %ffn_weights.4.refs_3_ = bf16[1024,4224]{1,0:T(8,128)(2,1)} custom-call(bf16[384,2048]{1,0:T(8,128)(2,1)} %copy-done.18, bf16[384,2048]{1,0:T(8,128)(2,1)} %copy-done.38, bf16[384,2048]{1,0:T(8,128)(2,1)} %collective-permute-done.21.refs_0_.refs_2_, bf16[384,2048]{1,0:T(8,128)(2,1)} %take_columns.1.refs_1_.refs_3_.given_ref, ...), custom_call_target="tpu_custom_call" | custom-call | flops 9965666304 | bytes 18382848 | tf_op jit(solution)/shard_map/ffn_weights/pallas_call | solution.py:700
  337.4 21.8 %ffn_block.7 = (bf16[384,4224]{1,0:T(8,128)(2,1)}, bf16[384,2048]{1,0:T(8,128)(2,1)}, bf16[384,2048]{1,0:T(8,128)(2,1)}) custom-call(bf16[384,2048]{1,0:T(8,128)(2,1)} %copy-done.9, bf16[384,2048]{1,0:T(8,128)(2,1)} %copy-done.10, bf16[512,4224]{1,0:T(8,128)(2,1)} %pad_maximum_fusion.refs_2_, bf16[512,4224]{1,0:T(8,128)(2,1)} %collective-permute-done.17.refs_3_, ...), custom_call_target="tpu_custom_call" | custom-call | flops 13287555072 | bytes 26738688 | tf_op jit(solution)/shard_map/ffn_block/pallas_call | solution.py:635
  362.4 11.4 %ffn_weights.6 = bf16[1024,4224]{1,0:T(8,128)(2,1)} custom-call(bf16[384,2048]{1,0:T(8,128)(2,1)} %copy-done.9, bf16[384,2048]{1,0:T(8,128)(2,1)} %copy-done.10, bf16[384,4224]{1,0:T(8,128)(2,1)} %get-tuple-element.232.refs_2_, bf16[1024,4224]{1,0:T(8,128)(2,1)} %ffn_weights.4.refs_3_), custom_call_target="tpu_custom_call" | custom-call | flops 3321888768 | bytes 11894784 | tf_op jit(solution)/shard_map/ffn_weights/pallas_call | solution.py:700
  373.7 24.9 %collective-permute-done.25 = bf16[384,2048]{1,0:T(8,128)(2,1)S(1)} collective-permute-done((bf16[384,2048]{1,0:T(8,128)(2,1)}, bf16[384,2048]{1,0:T(8,128)(2,1)S(1)}, u32[]{:S(2)}, u32[]{:S(2)}) %collective-permute-start.25) | collective-permute-done | bytes 1572896 | tf_op jit(solution)/shard_map/backs/ppermute | solution.py:161
  399.3 13.1 %collective-permute-done.26.refs_5_.refs_6_ = bf16[1024,4224]{1,0:T(8,128)(2,1)} collective-permute-done((bf16[1024,4224]{1,0:T(8,128)(2,1)}, bf16[1024,4224]{1,0:T(8,128)(2,1)}, u32[]{:S(2)}, u32[]{:S(2)}) %collective-permute-start.26) | collective-permute-done | bytes 8650784 | tf_op jit(solution)/shard_map/ffn_g/ppermute | solution.py:59
  412.5 15.1 %ffn_weights.7 = (bf16[512,4224]{1,0:T(8,128)(2,1)}, bf16[512,4224]{1,0:T(8,128)(2,1)}) custom-call(bf16[384,2048]{1,0:T(8,128)(2,1)} %copy-done.9, bf16[384,2048]{1,0:T(8,128)(2,1)} %copy-done.10, bf16[384,4224]{1,0:T(8,128)(2,1)} %get-tuple-element.232.refs_2_, bf16[512,4224]{1,0:T(8,128)(2,1)} %get-tuple-element.233.refs_3_, ...), custom_call_target="tpu_custom_call" | custom-call | flops 3321888768 | bytes 15138816 | tf_op jit(solution)/shard_map/ffn_weights/pallas_call | solution.py:700
  427.6 10.3 %collective-permute-done.27.come_ref = bf16[384,2048]{1,0:T(8,128)(2,1)S(1)} collective-permute-done((bf16[384,2048]{1,0:T(8,128)(2,1)S(1)}, bf16[384,2048]{1,0:T(8,128)(2,1)S(1)}, u32[]{:S(2)}, u32[]{:S(2)}) %collective-permute-start.27) | collective-permute-done | bytes 1572896 | tf_op jit(solution)/shard_map/backs/ppermute | solution.py:161
  439.5 8.1 %turn.1 = (f32[384,2048]{1,0:T(8,128)}, bf16[384,2048]{1,0:T(8,128)(2,1)}, bf16[2048,384]{1,0:T(8,128)(2,1)}, f32[1,2048]{1,0:T(1,128)}) custom-call(bf16[384,2048]{1,0:T(8,128)(2,1)} %copy-done.22, bf16[384,2048]{1,0:T(8,128)(2,1)} %get-tuple-element.245.part_ref, bf16[384,2048]{1,0:T(8,128)(2,1)} %take_columns.1.refs_1_.refs_3_.given_ref, ...), custom_call_target="tpu_custom_call" | custom-call | bytes 15728640 | tf_op jit(solution)/shard_map/turn/pallas_call | solution.py:733
  447.5 14.9 %attend_back.4 = (bf16[384,512]{1,0:T(8,128)(2,1)}, f32[1536,256]{1,0:T(8,128)}, f32[384,2048]{1,0:T(8,128)}) custom-call(bf16[384,2048]{1,0:T(8,128)(2,1)} %get-tuple-element.286.refs_0_, f32[1536,384]{1,0:T(8,128)} %and_select_fusion.refs_1_, bf16[384,1536]{1,0:T(8,128)(2,1)} %get-tuple-element.249.refs_2_.refs_4_, ...), custom_call_target="tpu_custom_call" | custom-call | flops 4630511616 | bytes 16000000 | tf_op jit(solution)/shard_map/attend_back/pallas_call | solution.py:502
  462.4 4.0 attend_weights.5
  466.4 10.6 %collective-permute-done.28 = bf16[384,2048]{1,0:T(8,128)(2,1)S(1)} collective-permute-done((bf16[384,2048]{1,0:T(8,128)(2,1)S(1)}, bf16[384,2048]{1,0:T(8,128)(2,1)S(1)}, u32[]{:S(2)}, u32[]{:S(2)}) %collective-permute-start.28) | collective-permute-done | bytes 1572896 | tf_op jit(solution)/shard_map/parts/ppermute | solution.py:161
  478.9 17.0 %attend_back.5 = (bf16[384,512]{1,0:T(8,128)(2,1)}, f32[1536,256]{1,0:T(8,128)}, f32[384,2048]{1,0:T(8,128)}) custom-call(bf16[384,2048]{1,0:T(8,128)(2,1)} %get-tuple-element.286.refs_0_, f32[1536,384]{1,0:T(8,128)} %and_select_fusion.refs_1_, f32[1536,256]{1,0:T(8,128)} %get-tuple-element.255.refs_2_, f32[384,2048]{1,0:T(8,128)} %get-tuple-element.256.refs_3_, ...), custom_call_target="tpu_custom_call" | custom-call | flops 4630511616 | bytes 16000000 | tf_op jit(solution)/shard_map/attend_back/pallas_call | solution.py:502
  495.9 4.1 add_convert_fusion
  500.6 5.9 attend_weights.6
  509.4 8.3 %collective-permute-done.31 = bf16[384,2048]{1,0:T(8,128)(2,1)S(1)} collective-permute-done((bf16[384,2048]{1,0:T(8,128)(2,1)}, bf16[384,2048]{1,0:T(8,128)(2,1)S(1)}, u32[]{:S(2)}, u32[]{:S(2)}) %collective-permute-start.31) | collective-permute-done | bytes 1572896 | tf_op jit(solution)/shard_map/parts/ppermute | solution.py:161
  521.0 16.4 %attend_back.6 = (bf16[384,512]{1,0:T(8,128)(2,1)}, f32[1536,256]{1,0:T(8,128)}, f32[384,2048]{1,0:T(8,128)}) custom-call(bf16[384,2048]{1,0:T(8,128)(2,1)} %get-tuple-element.286.refs_0_, f32[1536,384]{1,0:T(8,128)} %and_select_fusion.refs_1_, f32[1536,256]{1,0:T(8,128)} %get-tuple-element.267.refs_2_, f32[384,2048]{1,0:T(8,128)} %get-tuple-element.268.refs_3_, ...), custom_call_target="tpu_custom_call" | custom-call | flops 4630511616 | bytes 16000000 | tf_op jit(solution)/shard_map/attend_back/pallas_call | solution.py:502
  539.5 6.0 attend_weights.7
  548.2 10.3 %collective-permute-done.35.come_ref = bf16[384,2048]{1,0:T(8,128)(2,1)S(1)} collective-permute-done((bf16[384,2048]{1,0:T(8,128)(2,1)}, bf16[384,2048]{1,0:T(8,128)(2,1)S(1)}, u32[]{:S(2)}, u32[]{:S(2)}) %collective-permute-start.35) | collective-permute-done | bytes 1572896 | tf_op jit(solution)/shard_map/parts/ppermute | solution.py:161
  562.3 16.2 %attend_back.7 = (bf16[384,512]{1,0:T(8,128)(2,1)}, f32[1536,256]{1,0:T(8,128)}, f32[384,2048]{1,0:T(8,128)}) custom-call(bf16[384,2048]{1,0:T(8,128)(2,1)} %get-tuple-element.286.refs_0_, f32[1536,384]{1,0:T(8,128)} %and_select_fusion.refs_1_, f32[1536,256]{1,0:T(8,128)} %get-tuple-element.287.refs_2_, f32[384,2048]{1,0:T(8,128)} %get-tuple-element.288.refs_3_, ...), custom_call_target="tpu_custom_call" | custom-call | flops 4630511616 | bytes 16000000 | tf_op jit(solution)/shard_map/attend_back/pallas_call | solution.py:502
  580.0 6.1 attend_weights.8
  593.3 4.2 attend_weights.9
  600.2 7.1 %collective-permute-done.42.refs_2_ = bf16[384,256]{1,0:T(8,128)(2,1)S(1)} collective-permute-done((bf16[384,256]{1,0:T(8,128)(2,1)}, bf16[384,256]{1,0:T(8,128)(2,1)S(1)}, u32[]{:S(2)}, u32[]{:S(2)}) %collective-permute-start.42) | collective-permute-done | bytes 196640 | tf_op jit(solution)/shard_map/kv_g/ppermute | solution.py:165
  611.4 9.9 %leave.1 = (f32[384,2048]{1,0:T(8,128)}, bf16[1024,384]{1,0:T(8,128)(2,1)}, bf16[1024,384]{1,0:T(8,128)(2,1)}) custom-call(s32[8]{0:T(128)} %stack.36.table_ref, f32[1536,256]{1,0:T(8,128)} %get-tuple-element.292.refs_0_, bf16[384,256]{1,0:T(8,128)(2,1)} %copy-done.32, bf16[384,256]{1,0:T(8,128)(2,1)} %copy-done.33, bf16[384,256]{1,0:T(8,128)(2,1)} %copy-done.34, ...), custom_call_target="tpu_custom_call" | custom-call | flops 805306368 | bytes 16000000 | tf_op jit(solution)/shard_map/leave/pallas_call | solution.py:816
  624.9 4.0 collective-permute-done.47
  638.3 5.6 collective-permute-done.48.come_ref
  644.7 4.4 collective-permute-done.55
  668.0 4.9 unpack_ffn.1
  672.8 5.2 leave_out.1
  (229 shorter events, 129.6 us)
Async XLA Ops:
  5.2 18.8 %collective-permute-start = (bf16[256,1408]{1,0:T(8,128)(2,1)}, bf16[256,1408]{1,0:T(8,128)(2,1)S(1)}, u32[]{:S(2)}, u32[]{:S(2)}) collective-permute-start(bf16[256,1408]{1,0:T(8,128)(2,1)} %get-tuple-element.171), channel_id=1, source_target_pairs={{0,8},{4,20},{8,0},{12,28},{16,24},{20,4},{24,16},{28,12},{1,9},{5... | collective-permute-start | bytes 2162696 | tf_op jit(solution)/shard_map/attn_w_near/ppermute | solution.py:55
  8.1 15.8 %collective-permute-start.1 = (bf16[256,1024]{1,0:T(8,128)(2,1)}, bf16[256,1024]{1,0:T(8,128)(2,1)S(1)}, u32[]{:S(2)}, u32[]{:S(2)}) collective-permute-start(bf16[256,1024]{1,0:T(8,128)(2,1)} %get-tuple-element.172), channel_id=1, source_target_pairs={{0,1},{1,2},{2,3},{3,0},{4,5},{5,6},{6,7},{7,4},{8,9},{9,10},{10,1... | collective-permute-start | bytes 1572872 | tf_op jit(solution)/shard_map/attn_w_ring/ppermute | solution.py:161
  24.1 19.1 %collective-permute-start.2 = (bf16[512,1408]{1,0:T(8,128)(2,1)S(1)}, bf16[512,1408]{1,0:T(8,128)(2,1)S(1)}, u32[]{:S(2)}, u32[]{:S(2)}) collective-permute-start(bf16[512,1408]{1,0:T(8,128)(2,1)S(1)} %constant_dynamic-update-slice_fusion.refs_0_.refs_4_.refs_8_.refs_7_.refs_11_.refs_15_.refs_12_.refs_16_), channel_id=1, source_target_pairs={{0,16},{4,12},{8,24},{12,4},{16,0},{20,28},{24,8},{28,20},{1,17},{... | collective-permute-start | bytes 4325384 | tf_op jit(solution)/shard_map/attn_w_near/ppermute | solution.py:55
  25.7 14.9 %collective-permute-start.3 = (bf16[256,1024]{1,0:T(8,128)(2,1)S(1)}, bf16[256,1024]{1,0:T(8,128)(2,1)S(1)}, u32[]{:S(2)}, u32[]{:S(2)}) collective-permute-start(bf16[256,1024]{1,0:T(8,128)(2,1)S(1)} %collective-permute-done.1), channel_id=1, source_target_pairs={{0,1},{1,2},{2,3},{3,0},{4,5},{5,6},{6,7},{7,4},{8,9},{9,10},{10,1... | collective-permute-start | bytes 1572872 | tf_op jit(solution)/shard_map/attn_w_ring/ppermute | solution.py:161
  27.2 20.8 %collective-permute-start.4 = (bf16[512,1408]{1,0:T(8,128)(2,1)S(1)}, bf16[512,1408]{1,0:T(8,128)(2,1)S(1)}, u32[]{:S(2)}, u32[]{:S(2)}) collective-permute-start(bf16[512,1408]{1,0:T(8,128)(2,1)S(1)} %constant_dynamic-update-slice_fusion.refs_0_.refs_4_.refs_8_.refs_7_.refs_11_.refs_15_.refs_12_.refs_16_), channel_id=1, source_target_pairs={{0,4},{4,0},{8,12},{12,8},{16,20},{20,16},{24,28},{28,24},{1,5},{5... | collective-permute-start | bytes 4325384 | tf_op jit(solution)/shard_map/attn_w_near/ppermute | solution.py:59
  43.2 16.1 %collective-permute-start.5 = (bf16[512,1408]{1,0:T(8,128)(2,1)S(1)}, bf16[512,1408]{1,0:T(8,128)(2,1)S(1)}, u32[]{:S(2)}, u32[]{:S(2)}) collective-permute-start(bf16[512,1408]{1,0:T(8,128)(2,1)S(1)} %collective-permute-done.2.refs_1_.refs_5_.refs_9_.refs_8_.refs_12_.refs_16_.refs_13_.refs_17_), channel_id=1, source_target_pairs={{0,4},{4,0},{8,12},{12,8},{16,20},{20,16},{24,28},{28,24},{1,5},{5... | collective-permute-start | bytes 4325384 | tf_op jit(solution)/shard_map/attn_w_near/ppermute | solution.py:59
  43.2 16.1 %collective-permute-start.6 = (bf16[256,1024]{1,0:T(8,128)(2,1)S(1)}, bf16[256,1024]{1,0:T(8,128)(2,1)S(1)}, u32[]{:S(2)}, u32[]{:S(2)}) collective-permute-start(bf16[256,1024]{1,0:T(8,128)(2,1)S(1)} %collective-permute-done.3), channel_id=1, source_target_pairs={{0,1},{1,2},{2,3},{3,0},{4,5},{5,6},{6,7},{7,4},{8,9},{9,10},{10,1... | collective-permute-start | bytes 1572872 | tf_op jit(solution)/shard_map/attn_w_ring/ppermute | solution.py:161
  44.7 39.4 %collective-permute-start.11 = (bf16[256,4224]{1,0:T(8,128)(2,1)}, bf16[256,4224]{1,0:T(8,128)(2,1)}, u32[]{:S(2)}, u32[]{:S(2)}) collective-permute-start(bf16[256,4224]{1,0:T(8,128)(2,1)} %pack_ffn.1), channel_id=1, source_target_pairs={{0,8},{4,20},{8,0},{12,28},{16,24},{20,4},{24,16},{28,12},{1,9},{5... | collective-permute-start | bytes 6488072 | tf_op jit(solution)/shard_map/ffn_w/ppermute | solution.py:55
  60.3 28.4 %collective-permute-start.10 = (bf16[256,3072]{1,0:T(8,128)(2,1)}, bf16[256,3072]{1,0:T(8,128)(2,1)}, u32[]{:S(2)}, u32[]{:S(2)}) collective-permute-start(bf16[256,3072]{1,0:T(8,128)(2,1)} %constant_dynamic-update-slice_fusion.2), channel_id=1, source_target_pairs={{0,8},{4,20},{8,0},{12,28},{16,24},{20,4},{24,16},{28,12},{1,9},{5... | collective-permute-start | bytes 4718600 | tf_op jit(solution)/shard_map/attn_w_far/ppermute | solution.py:55
  66.9 17.2 %collective-permute-start.8 = (bf16[384,256]{1,0:T(8,128)(2,1)}, bf16[384,256]{1,0:T(8,128)(2,1)S(1)}, u32[]{:S(2)}, u32[]{:S(2)}) collective-permute-start(bf16[384,256]{1,0:T(8,128)(2,1)} %get-tuple-element.197.refs_3_.refs_5_.refs_7_.refs_0_), channel_id=1, source_target_pairs={{0,2},{1,3},{2,0},{3,1},{4,6},{5,7},{6,4},{7,5},{8,10},{9,11},{10,... | collective-permute-start | bytes 589832 | tf_op jit(solution)/shard_map/kv/ppermute | solution.py:165
  67.5 16.7 %collective-permute-start.9 = (bf16[384,256]{1,0:T(8,128)(2,1)}, bf16[384,256]{1,0:T(8,128)(2,1)S(1)}, u32[]{:S(2)}, u32[]{:S(2)}) collective-permute-start(bf16[384,256]{1,0:T(8,128)(2,1)} %get-tuple-element.197.refs_3_.refs_5_.refs_7_.refs_0_), channel_id=1, source_target_pairs={{0,3},{1,0},{2,1},{3,2},{4,7},{5,4},{6,5},{7,6},{8,11},{9,8},{10,9... | collective-permute-start | bytes 589832 | tf_op jit(solution)/shard_map/kv/ppermute | solution.py:165
  90.9 37.9 %collective-permute-start.13 = (bf16[512,3072]{1,0:T(8,128)(2,1)S(1)}, bf16[512,3072]{1,0:T(8,128)(2,1)}, u32[]{:S(2)}, u32[]{:S(2)}) collective-permute-start(bf16[512,3072]{1,0:T(8,128)(2,1)S(1)} %pad_maximum_fusion.1.refs_7_.refs_11_.refs_9_.refs_13_.refs_15_), channel_id=1, source_target_pairs={{0,16},{4,12},{8,24},{12,4},{16,0},{20,28},{24,8},{28,20},{1,17},{... | collective-permute-start | bytes 9437192 | tf_op jit(solution)/shard_map/attn_w_far/ppermute | solution.py:55
  92.5 36.3 %collective-permute-start.12 = (bf16[384,2048]{1,0:T(8,128)(2,1)S(1)}, bf16[384,2048]{1,0:T(8,128)(2,1)}, u32[]{:S(2)}, u32[]{:S(2)}) collective-permute-start(bf16[384,2048]{1,0:T(8,128)(2,1)S(1)} %copy-done.12), channel_id=1, source_target_pairs={{0,1},{1,2},{2,3},{3,0},{4,5},{5,6},{6,7},{7,4},{8,9},{9,10},{10,1... | collective-permute-start | bytes 4718600 | tf_op jit(solution)/shard_map/grad_ring/ppermute | solution.py:161
  94.1 38.4 %collective-permute-start.14 = (bf16[512,3072]{1,0:T(8,128)(2,1)S(1)}, bf16[512,3072]{1,0:T(8,128)(2,1)}, u32[]{:S(2)}, u32[]{:S(2)}) collective-permute-start(bf16[512,3072]{1,0:T(8,128)(2,1)S(1)} %pad_maximum_fusion.1.refs_7_.refs_11_.refs_9_.refs_13_.refs_15_), channel_id=1, source_target_pairs={{0,4},{4,0},{8,12},{12,8},{16,20},{20,16},{24,28},{28,24},{1,5},{5... | collective-permute-start | bytes 9437192 | tf_op jit(solution)/shard_map/attn_w_far/ppermute | solution.py:59
  128.8 50.2 %collective-permute-start.17 = (bf16[512,4224]{1,0:T(8,128)(2,1)}, bf16[512,4224]{1,0:T(8,128)(2,1)}, u32[]{:S(2)}, u32[]{:S(2)}) collective-permute-start(bf16[512,4224]{1,0:T(8,128)(2,1)} %pad_maximum_fusion.refs_2_), channel_id=1, source_target_pairs={{0,16},{4,12},{8,24},{12,4},{16,0},{20,28},{24,8},{28,20},{1,17},{... | collective-permute-start | bytes 12976136 | tf_op jit(solution)/shard_map/ffn_w/ppermute | solution.py:55
  131.2 38.8 %collective-permute-start.18 = (bf16[384,2048]{1,0:T(8,128)(2,1)}, bf16[384,2048]{1,0:T(8,128)(2,1)}, u32[]{:S(2)}, u32[]{:S(2)}) collective-permute-start(bf16[384,2048]{1,0:T(8,128)(2,1)} %collective-permute-done.12.refs_1_.refs_4_), channel_id=1, source_target_pairs={{0,1},{1,2},{2,3},{3,0},{4,5},{5,6},{6,7},{7,4},{8,9},{9,10},{10,1... | collective-permute-start | bytes 4718600 | tf_op jit(solution)/shard_map/grad_ring/ppermute | solution.py:161
  132.5 47.7 %collective-permute-start.19 = (bf16[512,4224]{1,0:T(8,128)(2,1)}, bf16[512,4224]{1,0:T(8,128)(2,1)}, u32[]{:S(2)}, u32[]{:S(2)}) collective-permute-start(bf16[512,4224]{1,0:T(8,128)(2,1)} %pad_maximum_fusion.refs_2_), channel_id=1, source_target_pairs={{0,4},{4,0},{8,12},{12,8},{16,20},{20,16},{24,28},{28,24},{1,5},{5... | collective-permute-start | bytes 12976136 | tf_op jit(solution)/shard_map/ffn_w/ppermute | solution.py:59
  179.0 38.6 %collective-permute-start.16 = (bf16[384,2048]{1,0:T(8,128)(2,1)S(1)}, bf16[384,2048]{1,0:T(8,128)(2,1)S(1)}, u32[]{:S(2)}, u32[]{:S(2)}) collective-permute-start(bf16[384,2048]{1,0:T(8,128)(2,1)S(1)} %multiply_convert_fusion.refs_0_), channel_id=1, source_target_pairs={{0,1},{1,2},{2,3},{3,0},{4,5},{5,6},{6,7},{7,4},{8,9},{9,10},{10,1... | collective-permute-start | bytes 4718600 | tf_op jit(solution)/shard_map/ffn_ring/ppermute | solution.py:161
  217.6 38.3 %collective-permute-start.21 = (bf16[384,2048]{1,0:T(8,128)(2,1)S(1)}, bf16[384,2048]{1,0:T(8,128)(2,1)}, u32[]{:S(2)}, u32[]{:S(2)}) collective-permute-start(bf16[384,2048]{1,0:T(8,128)(2,1)S(1)} %collective-permute-done.16.refs_0_.refs_1_), channel_id=1, source_target_pairs={{0,1},{1,2},{2,3},{3,0},{4,5},{5,6},{6,7},{7,4},{8,9},{9,10},{10,1... | collective-permute-start | bytes 4718600 | tf_op jit(solution)/shard_map/ffn_ring/ppermute | solution.py:161
  256.0 39.3 %collective-permute-start.22 = (bf16[384,2048]{1,0:T(8,128)(2,1)}, bf16[384,2048]{1,0:T(8,128)(2,1)S(1)}, u32[]{:S(2)}, u32[]{:S(2)}) collective-permute-start(bf16[384,2048]{1,0:T(8,128)(2,1)} %collective-permute-done.21.refs_0_.refs_2_), channel_id=1, source_target_pairs={{0,1},{1,2},{2,3},{3,0},{4,5},{5,6},{6,7},{7,4},{8,9},{9,10},{10,1... | collective-permute-start | bytes 4718600 | tf_op jit(solution)/shard_map/ffn_ring/ppermute | solution.py:161
  256.0 80.2 %collective-permute-start.23 = (bf16[384,2048]{1,0:T(8,128)(2,1)}, bf16[384,2048]{1,0:T(8,128)(2,1)S(1)}, u32[]{:S(2)}, u32[]{:S(2)}) collective-permute-start(bf16[384,2048]{1,0:T(8,128)(2,1)} %collective-permute-done.18.refs_1_.refs_5_), channel_id=1, source_target_pairs={{0,1},{1,2},{2,3},{3,0},{4,5},{5,6},{6,7},{7,4},{8,9},{9,10},{10,1... | collective-permute-start | bytes 4718600 | tf_op jit(solution)/shard_map/grad_ring/ppermute | solution.py:161
  256.0 104.6 %collective-permute-start.24 = (bf16[384,2048]{1,0:T(8,128)(2,1)}, bf16[384,2048]{1,0:T(8,128)(2,1)S(1)}, u32[]{:S(2)}, u32[]{:S(2)}) collective-permute-start(bf16[384,2048]{1,0:T(8,128)(2,1)} %get-tuple-element.228), channel_id=1, source_target_pairs={{0,1},{1,2},{2,3},{3,0},{4,5},{5,6},{6,7},{7,4},{8,9},{9,10},{10,1... | collective-permute-start | bytes 4718600 | tf_op jit(solution)/shard_map/backs/ppermute | solution.py:161
  362.4 36.2 %collective-permute-start.25 = (bf16[384,2048]{1,0:T(8,128)(2,1)}, bf16[384,2048]{1,0:T(8,128)(2,1)S(1)}, u32[]{:S(2)}, u32[]{:S(2)}) collective-permute-start(bf16[384,2048]{1,0:T(8,128)(2,1)} %add_convert_fusion.5), channel_id=1, source_target_pairs={{0,1},{1,2},{2,3},{3,0},{4,5},{5,6},{6,7},{7,4},{8,9},{9,10},{10,1... | collective-permute-start | bytes 4718600 | tf_op jit(solution)/shard_map/backs/ppermute | solution.py:161
  398.6 13.9 %collective-permute-start.26 = (bf16[1024,4224]{1,0:T(8,128)(2,1)}, bf16[1024,4224]{1,0:T(8,128)(2,1)}, u32[]{:S(2)}, u32[]{:S(2)}) collective-permute-start(bf16[1024,4224]{1,0:T(8,128)(2,1)} %ffn_weights.6), channel_id=1, source_target_pairs={{0,4},{4,0},{8,12},{12,8},{16,20},{20,16},{24,28},{28,24},{1,5},{5... | collective-permute-start | bytes 25952264 | tf_op jit(solution)/shard_map/ffn_g/ppermute | solution.py:59
  399.3 38.7 %collective-permute-start.27 = (bf16[384,2048]{1,0:T(8,128)(2,1)S(1)}, bf16[384,2048]{1,0:T(8,128)(2,1)S(1)}, u32[]{:S(2)}, u32[]{:S(2)}) collective-permute-start(bf16[384,2048]{1,0:T(8,128)(2,1)S(1)} %add_convert_fusion.4), channel_id=1, source_target_pairs={{0,1},{1,2},{2,3},{3,0},{4,5},{5,6},{6,7},{7,4},{8,9},{9,10},{10,1... | collective-permute-start | bytes 4718600 | tf_op jit(solution)/shard_map/backs/ppermute | solution.py:161
  437.9 57.9 %collective-permute-start.30 = (bf16[512,4224]{1,0:T(8,128)(2,1)}, bf16[512,4224]{1,0:T(8,128)(2,1)}, u32[]{:S(2)}, u32[]{:S(2)}) collective-permute-start(bf16[512,4224]{1,0:T(8,128)(2,1)} %get-tuple-element.259), channel_id=1, source_target_pairs={{0,16},{4,12},{8,24},{12,4},{16,0},{20,28},{24,8},{28,20},{1,17},{... | collective-permute-start | bytes 12976136 | tf_op jit(solution)/shard_map/ffn_g/ppermute | solution.py:55
  439.5 37.5 %collective-permute-start.28 = (bf16[384,2048]{1,0:T(8,128)(2,1)S(1)}, bf16[384,2048]{1,0:T(8,128)(2,1)S(1)}, u32[]{:S(2)}, u32[]{:S(2)}) collective-permute-start(bf16[384,2048]{1,0:T(8,128)(2,1)S(1)} %copy-done.37), channel_id=1, source_target_pairs={{0,1},{1,2},{2,3},{3,0},{4,5},{5,6},{6,7},{7,4},{8,9},{9,10},{10,1... | collective-permute-start | bytes 4718600 | tf_op jit(solution)/shard_map/parts/ppermute | solution.py:161
  477.0 18.9 %collective-permute-start.29 = (bf16[1024,1024]{1,0:T(8,128)(2,1)}, bf16[1024,1024]{1,0:T(8,128)(2,1)}, u32[]{:S(2)}, u32[]{:S(2)}) collective-permute-start(bf16[1024,1024]{1,0:T(8,128)(2,1)} %attend_weights.5), channel_id=1, source_target_pairs={{0,4},{4,0},{8,12},{12,8},{16,20},{20,16},{24,28},{28,24},{1,5},{5... | collective-permute-start | bytes 6291464 | tf_op jit(solution)/shard_map/attn_g_1/ppermute | solution.py:59
  478.9 38.8 %collective-permute-start.31 = (bf16[384,2048]{1,0:T(8,128)(2,1)}, bf16[384,2048]{1,0:T(8,128)(2,1)S(1)}, u32[]{:S(2)}, u32[]{:S(2)}) collective-permute-start(bf16[384,2048]{1,0:T(8,128)(2,1)} %add_convert_fusion.3), channel_id=1, source_target_pairs={{0,1},{1,2},{2,3},{3,0},{4,5},{5,6},{6,7},{7,4},{8,9},{9,10},{10,1... | collective-permute-start | bytes 4718600 | tf_op jit(solution)/shard_map/parts/ppermute | solution.py:161
  500.0 37.7 %collective-permute-start.34 = (bf16[256,4224]{1,0:T(8,128)(2,1)}, bf16[256,4224]{1,0:T(8,128)(2,1)S(1)}, u32[]{:S(2)}, u32[]{:S(2)}) collective-permute-start(bf16[256,4224]{1,0:T(8,128)(2,1)} %get-tuple-element.332), channel_id=1, source_target_pairs={{0,8},{4,20},{8,0},{12,28},{16,24},{20,4},{24,16},{28,12},{1,9},{5... | collective-permute-start | bytes 6488072 | tf_op jit(solution)/shard_map/ffn_g/ppermute | solution.py:55
  517.7 20.1 %collective-permute-start.32 = (bf16[1024,1024]{1,0:T(8,128)(2,1)}, bf16[1024,1024]{1,0:T(8,128)(2,1)}, u32[]{:S(2)}, u32[]{:S(2)}) collective-permute-start(bf16[1024,1024]{1,0:T(8,128)(2,1)} %get-tuple-element.270), channel_id=1, source_target_pairs={{0,4},{4,0},{8,12},{12,8},{16,20},{20,16},{24,28},{28,24},{1,5},{5... | collective-permute-start | bytes 6291464 | tf_op jit(solution)/shard_map/attn_g_2/ppermute | solution.py:59
  517.7 20.1 %collective-permute-start.33 = (bf16[512,1024]{1,0:T(8,128)(2,1)}, bf16[512,1024]{1,0:T(8,128)(2,1)S(1)}, u32[]{:S(2)}, u32[]{:S(2)}) collective-permute-start(bf16[512,1024]{1,0:T(8,128)(2,1)} %get-tuple-element.271), channel_id=1, source_target_pairs={{0,16},{4,12},{8,24},{12,4},{16,0},{20,28},{24,8},{28,20},{1,17},{... | collective-permute-start | bytes 3145736 | tf_op jit(solution)/shard_map/attn_g_1/ppermute | solution.py:55
  521.0 37.5 %collective-permute-start.35 = (bf16[384,2048]{1,0:T(8,128)(2,1)}, bf16[384,2048]{1,0:T(8,128)(2,1)S(1)}, u32[]{:S(2)}, u32[]{:S(2)}) collective-permute-start(bf16[384,2048]{1,0:T(8,128)(2,1)} %add_convert_fusion.2), channel_id=1, source_target_pairs={{0,1},{1,2},{2,3},{3,0},{4,5},{5,6},{6,7},{7,4},{8,9},{9,10},{10,1... | collective-permute-start | bytes 4718600 | tf_op jit(solution)/shard_map/parts/ppermute | solution.py:161
  538.9 19.6 %collective-permute-start.36 = (bf16[256,1024]{1,0:T(8,128)(2,1)}, bf16[256,1024]{1,0:T(8,128)(2,1)}, u32[]{:S(2)}, u32[]{:S(2)}) collective-permute-start(bf16[256,1024]{1,0:T(8,128)(2,1)} %add_convert_fusion.18), channel_id=1, source_target_pairs={{0,8},{4,20},{8,0},{12,28},{16,24},{20,4},{24,16},{28,12},{1,9},{5... | collective-permute-start | bytes 1572872 | tf_op jit(solution)/shard_map/attn_g_1/ppermute | solution.py:55
  558.6 19.9 %collective-permute-start.37 = (bf16[1024,1024]{1,0:T(8,128)(2,1)}, bf16[1024,1024]{1,0:T(8,128)(2,1)S(1)}, u32[]{:S(2)}, u32[]{:S(2)}) collective-permute-start(bf16[1024,1024]{1,0:T(8,128)(2,1)} %get-tuple-element.294), channel_id=1, source_target_pairs={{0,4},{4,0},{8,12},{12,8},{16,20},{20,16},{24,28},{28,24},{1,5},{5... | collective-permute-start | bytes 6291464 | tf_op jit(solution)/shard_map/attn_g_3/ppermute | solution.py:59
  558.6 19.9 %collective-permute-start.38 = (bf16[512,1024]{1,0:T(8,128)(2,1)}, bf16[512,1024]{1,0:T(8,128)(2,1)}, u32[]{:S(2)}, u32[]{:S(2)}) collective-permute-start(bf16[512,1024]{1,0:T(8,128)(2,1)} %get-tuple-element.295), channel_id=1, source_target_pairs={{0,16},{4,12},{8,24},{12,4},{16,0},{20,28},{24,8},{28,20},{1,17},{... | collective-permute-start | bytes 3145736 | tf_op jit(solution)/shard_map/attn_g_2/ppermute | solution.py:55
  562.3 16.2 %collective-permute-start.39 = (bf16[256,1024]{1,0:T(8,128)(2,1)}, bf16[256,1024]{1,0:T(8,128)(2,1)S(1)}, u32[]{:S(2)}, u32[]{:S(2)}) collective-permute-start(bf16[256,1024]{1,0:T(8,128)(2,1)} %add_convert_fusion.16), channel_id=1, source_target_pairs={{0,1},{1,2},{2,3},{3,0},{4,5},{5,6},{6,7},{7,4},{8,9},{9,10},{10,1... | collective-permute-start | bytes 1572872 | tf_op jit(solution)/shard_map/attn_g_ring/ppermute | solution.py:161
  590.8 16.5 %collective-permute-start.42 = (bf16[384,256]{1,0:T(8,128)(2,1)}, bf16[384,256]{1,0:T(8,128)(2,1)S(1)}, u32[]{:S(2)}, u32[]{:S(2)}) collective-permute-start(bf16[384,256]{1,0:T(8,128)(2,1)} %get-tuple-element.344), channel_id=1, source_target_pairs={{0,2},{1,3},{2,0},{3,1},{4,6},{5,7},{6,4},{7,5},{8,10},{9,11},{10,... | collective-permute-start | bytes 589832 | tf_op jit(solution)/shard_map/kv_g/ppermute | solution.py:165
  590.8 16.5 %collective-permute-start.43 = (bf16[384,256]{1,0:T(8,128)(2,1)S(1)}, bf16[384,256]{1,0:T(8,128)(2,1)S(1)}, u32[]{:S(2)}, u32[]{:S(2)}) collective-permute-start(bf16[384,256]{1,0:T(8,128)(2,1)S(1)} %get-tuple-element.343), channel_id=1, source_target_pairs={{0,1},{1,2},{2,3},{3,0},{4,5},{5,6},{6,7},{7,4},{8,9},{9,10},{10,1... | collective-permute-start | bytes 589832 | tf_op jit(solution)/shard_map/kv_g/ppermute | solution.py:165
  592.5 28.8 %collective-permute-start.46 = (bf16[512,1024]{1,0:T(8,128)(2,1)}, bf16[512,1024]{1,0:T(8,128)(2,1)S(1)}, u32[]{:S(2)}, u32[]{:S(2)}) collective-permute-start(bf16[512,1024]{1,0:T(8,128)(2,1)} %slice.152), channel_id=1, source_target_pairs={{0,16},{4,12},{8,24},{12,4},{16,0},{20,28},{24,8},{28,20},{1,17},{... | collective-permute-start | bytes 3145736 | tf_op jit(solution)/shard_map/attn_g_3/ppermute | solution.py:55
  608.1 20.7 %collective-permute-start.47 = (bf16[512,1024]{1,0:T(8,128)(2,1)}, bf16[512,1024]{1,0:T(8,128)(2,1)}, u32[]{:S(2)}, u32[]{:S(2)}) collective-permute-start(bf16[512,1024]{1,0:T(8,128)(2,1)} %get-tuple-element.314), channel_id=1, source_target_pairs={{0,16},{4,12},{8,24},{12,4},{16,0},{20,28},{24,8},{28,20},{1,17},{... | collective-permute-start | bytes 3145736 | tf_op jit(solution)/shard_map/attn_g_0/ppermute | solution.py:55
  609.8 15.0 %collective-permute-start.45 = (bf16[256,1024]{1,0:T(8,128)(2,1)S(1)}, bf16[256,1024]{1,0:T(8,128)(2,1)}, u32[]{:S(2)}, u32[]{:S(2)}) collective-permute-start(bf16[256,1024]{1,0:T(8,128)(2,1)S(1)} %add_convert_fusion.15), channel_id=1, source_target_pairs={{0,8},{4,20},{8,0},{12,28},{16,24},{20,4},{24,16},{28,12},{1,9},{5... | collective-permute-start | bytes 1572872 | tf_op jit(solution)/shard_map/attn_g_2/ppermute | solution.py:55
  621.2 15.9 %collective-permute-start.44 = (bf16[1024,384]{1,0:T(8,128)(2,1)}, bf16[1024,384]{1,0:T(8,128)(2,1)S(1)}, u32[]{:S(2)}, u32[]{:S(2)}) collective-permute-start(bf16[1024,384]{1,0:T(8,128)(2,1)} %get-tuple-element.309), channel_id=1, source_target_pairs={{0,4},{4,0},{8,12},{12,8},{16,20},{20,16},{24,28},{28,24},{1,5},{5... | collective-permute-start | bytes 2359304 | tf_op jit(solution)/shard_map/small_g/ppermute | solution.py:59
  635.2 13.9 %collective-permute-start.55 = (bf16[256,1024]{1,0:T(8,128)(2,1)S(1)}, bf16[256,1024]{1,0:T(8,128)(2,1)S(1)}, u32[]{:S(2)}, u32[]{:S(2)}) collective-permute-start(bf16[256,1024]{1,0:T(8,128)(2,1)S(1)} %add_convert_fusion.10), channel_id=1, source_target_pairs={{0,1},{1,2},{2,3},{3,0},{4,5},{5,6},{6,7},{7,4},{8,9},{9,10},{10,1... | collective-permute-start | bytes 1572872 | tf_op jit(solution)/shard_map/attn_g_ring/ppermute | solution.py:161
  653.9 24.2 %collective-permute-start.56 = (bf16[256,1024]{1,0:T(8,128)(2,1)S(1)}, bf16[256,1024]{1,0:T(8,128)(2,1)S(1)}, u32[]{:S(2)}, u32[]{:S(2)}) collective-permute-start(bf16[256,1024]{1,0:T(8,128)(2,1)S(1)} %add_convert_fusion.7), channel_id=1, source_target_pairs={{0,1},{1,2},{2,3},{3,0},{4,5},{5,6},{6,7},{7,4},{8,9},{9,10},{10,1... | collective-permute-start | bytes 1572872 | tf_op jit(solution)/shard_map/attn_g_ring/ppermute | solution.py:161
  658.2 23.2 %collective-permute-start.52 = (bf16[256,384]{1,0:T(8,128)(2,1)S(1)}, bf16[256,384]{1,0:T(8,128)(2,1)S(1)}, u32[]{:S(2)}, u32[]{:S(2)}) collective-permute-start(bf16[256,384]{1,0:T(8,128)(2,1)S(1)} %add_convert_fusion.21), channel_id=1, source_target_pairs={{0,1},{1,2},{2,3},{3,0},{4,5},{5,6},{6,7},{7,4},{8,9},{9,10},{10,1... | collective-permute-start | bytes 589832 | tf_op jit(solution)/shard_map/small_g_ring/ppermute | solution.py:165
  659.6 21.8 %collective-permute-start.53 = (bf16[256,384]{1,0:T(8,128)(2,1)S(1)}, bf16[256,384]{1,0:T(8,128)(2,1)S(1)}, u32[]{:S(2)}, u32[]{:S(2)}) collective-permute-start(bf16[256,384]{1,0:T(8,128)(2,1)S(1)} %add_convert_fusion.21), channel_id=1, source_target_pairs={{0,2},{1,3},{2,0},{3,1},{4,6},{5,7},{6,4},{7,5},{8,10},{9,11},{10,... | collective-permute-start | bytes 589832 | tf_op jit(solution)/shard_map/small_g_ring/ppermute | solution.py:165
  661.6 19.8 %collective-permute-start.54 = (bf16[256,384]{1,0:T(8,128)(2,1)S(1)}, bf16[256,384]{1,0:T(8,128)(2,1)S(1)}, u32[]{:S(2)}, u32[]{:S(2)}) collective-permute-start(bf16[256,384]{1,0:T(8,128)(2,1)S(1)} %add_convert_fusion.21), channel_id=1, source_target_pairs={{0,3},{1,0},{2,1},{3,2},{4,7},{5,4},{6,5},{7,6},{8,11},{9,8},{10,9... | collective-permute-start | bytes 589832 | tf_op jit(solution)/shard_map/small_g_ring/ppermute | solution.py:165
  (50 other events, 531.9 us)
